TPU v7x, 32 devices: a whole 2x2x4 slice. The times are simulated.
32 devices in a mesh: wide: 8 (over z, y), narrow: 4 (over x, core).
Axes of the slice: x: 2, y: 2, z: 4, core: 2. Of those that a mesh axis runs over, the one named last changes fastest.
Arguments:
- face_blocks: float32 [1280, 320, 320], P(('wide', 'narrow')), may hold values from -0.3125 to 0.3125
- face_elems: int32 [1280, 2], P(('wide', 'narrow')), may hold values from 0 to 255, as said below
- coarse_slot: int32 [256], replicated, may hold values from 0 to 255, as said below
- prolong: float32 [320, 135], replicated, may hold values from -0.3125 to 0.3125
- fine_residual: float32 [256, 320], P(('wide', 'narrow')), may hold values from -6 to 6
- block_inverse: float32 [256, 135, 135], P(('wide', 'narrow'))
Outputs:
- fine_correction: float32 [256, 320], P(('wide', 'narrow'))
- owned_blocks: float32 [2560, 135, 135], P(('wide', 'narrow'))
Inputs may be any that keep to these rules, and one draw needn't show every extreme that they name: `coarse_slot`: A permutation: every element has its own coarse row. `face_elems`: the row and column elements of a face differ. With the owner of an element being coarse_slot // 32, among the 40 faces of each device (aligned blocks of 40 rows, devices in the order wide then narrow) at most 10 have row elements of any one owner, and for each narrow index one owner takes exactly 10 faces from every device with that narrow index.
All inputs are finite; a program needn't handle non-finite values.
Results may differ from a plain program's by a relative error of at most 0.000075.
Values sent between devices are 32-bit elements; how exact they have to be, the bound alone decides.
No kernel may reach another device: no remote copies, remote signals or barrier semaphores. Data moves between devices by JAX's collectives and lax.ppermute only.
A program may use at most 192 MiB of HBM per device.

v0:
```python
import jax
import jax.numpy as jnp
from jax import lax
from jax.sharding import PartitionSpec as P

DAMPING = 0.7
PRECISE = lax.Precision.HIGHEST


def galerkin(blocks, prolong):
    applied = jnp.einsum("fij,jc->fic", blocks, prolong, precision=PRECISE)
    return jnp.einsum("ia,fic->fac", prolong, applied, precision=PRECISE)


def sum_into_rows(values, targets, rows_total):
    selector = (
        lax.broadcasted_iota(jnp.int32, (rows_total, targets.shape[0]), 0) == targets[None, :]
    ).astype(jnp.float32)
    return jnp.dot(selector, values, precision=PRECISE)


def local(face_blocks, face_elems, coarse_slot, prolong, fine_residual, block_inverse):
    wide_size = lax.axis_size("wide")
    narrow_size = lax.axis_size("narrow")
    dev_rows = fine_residual.shape[0]
    owner_total = dev_rows * narrow_size
    face_total = face_blocks.shape[0]
    coarse_width = prolong.shape[1]
    capacity = max(2, (2 * face_total + wide_size - 1) // wide_size)
    buffer_rows = wide_size * capacity
    coarse_rhs = jnp.dot(fine_residual, prolong, precision=PRECISE)
    sweep_one = DAMPING * jnp.einsum("snm,sm->sn", block_inverse, coarse_rhs, precision=PRECISE)
    iterate_all = lax.all_gather(sweep_one, ("wide", "narrow"), axis=0, tiled=True)
    slot_pairs = jnp.take(coarse_slot, face_elems, axis=0)
    row_slot = slot_pairs[:, 0]
    col_slot = slot_pairs[:, 1]
    target = row_slot // owner_total
    local_row = row_slot % owner_total
    selector = (target[:, None] == jnp.arange(wide_size, dtype=jnp.int32)[None, :]).astype(
        jnp.int32
    )
    ranking = jnp.sum(selector * (jnp.cumsum(selector, axis=0) - 1), axis=1)
    position = target * capacity + ranking
    coarse_blocks = galerkin(face_blocks, prolong)
    send_blocks = (
        jnp.zeros((buffer_rows, coarse_width, coarse_width), jnp.float32)
        .at[position]
        .set(coarse_blocks)
    )
    send_blocks = send_blocks.reshape(wide_size, capacity, coarse_width, coarse_width)
    labels = (
        jnp.zeros((buffer_rows, 2), jnp.int32)
        .at[position]
        .set(jnp.stack([local_row, col_slot], axis=1))
    )
    labels = labels.reshape(wide_size, capacity, 2)
    blocks = lax.all_to_all(send_blocks, "wide", split_axis=0, concat_axis=0, tiled=True)
    labels_in = lax.all_to_all(labels, "wide", split_axis=0, concat_axis=0, tiled=True)
    vectors = jnp.take(iterate_all, labels_in[..., 1], axis=0)
    results = jnp.einsum("wkac,wkc->wka", blocks, vectors, precision=PRECISE)
    targets_in = labels_in[..., 0]
    partial_sums = sum_into_rows(
        results.reshape(-1, coarse_width), targets_in.reshape(-1), owner_total
    )
    coupling = lax.psum_scatter(partial_sums, "narrow", scatter_dimension=0, tiled=True)
    update = (1.0 - DAMPING) * coarse_rhs - coupling
    sweep_two = sweep_one + DAMPING * jnp.einsum(
        "snm,sm->sn", block_inverse, update, precision=PRECISE
    )
    correction = jnp.dot(sweep_two, prolong.T, precision=PRECISE)
    return (correction, blocks.reshape(buffer_rows, coarse_width, coarse_width))


def solution(mesh):
    placed = (
        P(("wide", "narrow"), None, None),
        P(("wide", "narrow"), None),
        P(),
        P(),
        P(("wide", "narrow"), None),
        P(("wide", "narrow"), None, None),
    )
    return jax.shard_map(
        local,
        mesh=mesh,
        in_specs=placed,
        out_specs=(P(("wide", "narrow"), None), P(("wide", "narrow"), None, None)),
        check_vma=False,
    )
```

profile of v0, /device:TPU:0, one launch (start us, length us, event | category | flops | bytes accessed | tf_op | source)
XLA Modules:
  0.0 394.1 jit_solution(11476387449523077553)
XLA Ops:
  7.2 0.0 copy-start
  7.2 0.0 copy-start.1
  7.2 0.7 compare_select_fusion.1
  7.9 0.1 copy.59
  8.0 0.1 reshape.33
  8.1 0.0 copy-done.1
  8.1 0.0 copy-start.4
  8.2 1.3 gather_fusion
  9.4 0.1 reshape.32
  9.5 0.1 copy.60
  9.6 0.0 copy-done.4
  9.7 0.1 fusion.5
  9.7 0.1 reduce_window_sum.11
  9.8 0.2 select_reduce_fusion
  10.0 0.1 copy.61
  10.1 0.7 scatter_custom_fusion
  10.8 0.1 copy.62
  10.9 0.1 reshape.27
  10.9 0.6 copy.63
  11.6 7.3 %all-to-all-start = ((s32[8,10,2]{1,2,0:T(2,128)}), s32[8,10,2]{1,2,0:T(2,128)S(1)}, u32[]{:S(2)}, u32[]{:S(2)}) async-start(s32[8,10,2]{1,2,0:T(2,128)} %copy.63), calls=%async_computation | async-start | bytes 16384 | tf_op jit(solution)/shard_map/all_to_all | solution.py:58
  18.9 0.0 copy-done
  18.9 25.5 %fusion.1 = f32[40,320,135]{1,2,0:T(8,128)S(1)} fusion(f32[40,320,320]{2,1,0:T(8,128)} %param.6, f32[320,135]{0,1:T(8,128)S(1)} %copy-done), kind=kOutput, calls=%fused_computation.6 | convolution fusion | flops 6635520000 | bytes 23468800 | tf_op jit(solution)/shard_map/fij,jc->fic/dot_general | solution.py:11
  44.4 10.7 %convolution_bitcast_fusion = f32[40,135,135]{1,2,0:T(8,128)} fusion(f32[40,320,135]{1,2,0:T(8,128)S(1)} %fusion.1, f32[320,135]{0,1:T(8,128)S(1)} %copy-done), kind=kOutput, calls=%fused_computation.4 | convolution fusion | flops 2799360000 | bytes 10000800 | tf_op jit(solution)/shard_map/ia,fic->fac/dot_general | solution.py:12
  55.1 6.9 %copy.64 = f32[40,135,135]{2,1,0:T(8,128)} copy(f32[40,135,135]{1,2,0:T(8,128)} %convolution_bitcast_fusion) | data formatting | bytes 5832000 | tf_op jit(solution)/shard_map/ia,fic->fac/transpose | solution.py:12
  62.0 4.8 %broadcast_in_dim.31 = f32[80,135,135]{2,1,0:T(8,128)} broadcast(f32[]{:T(128)} %constant.73.clone.1), dimensions={} | broadcast | bytes 5832004 | tf_op jit(solution)/shard_map/broadcast_in_dim | solution.py:46
  66.8 12.1 %scatter_fusion = f32[80,135,135]{2,1,0:T(8,128)} fusion(f32[80,135,135]{2,1,0:T(8,128)} %broadcast_in_dim.31, s32[40]{0:T(128)S(1)} %fusion.19, f32[40,135,135]{2,1,0:T(8,128)} %copy.64), kind=kCustom, calls=%fused_computation.3 | custom fusion | bytes 8748160 | tf_op jit(solution)/shard_map/scatter | solution.py:48
  78.9 0.0 all-to-all-done
  78.9 0.0 copy-start.2
  78.9 0.0 copy-start.3
  78.9 6.2 %all-to-all-start.1 = ((f32[8,10,135,135]{3,2,1,0:T(8,128)}), f32[8,10,135,135]{3,2,1,0:T(8,128)}, u32[]{:S(2)}, u32[]{:S(2)}) async-start(f32[8,10,135,135]{3,2,1,0:T(8,128)} %bitcast.50), calls=%async_computation.1 | async-start | bytes 22282240 | tf_op jit(solution)/shard_map/all_to_all | solution.py:57
  85.1 0.2 reduce-scatter.2.cloned.1.call-start
  85.3 0.0 copy-done.2
  85.3 0.7 copy.68
  86.0 0.0 copy-done.3
  86.0 0.3 fusion.21
  86.3 0.7 fusion.15
  87.0 214.9 %all_gather.3 = f32[256,135]{1,0:T(8,128)S(1)} all-gather(f32[8,135]{1,0:T(8,128)S(1)} %bitcast_multiply_fusion.1), channel_id=1, replica_groups=mesh['wide'=8,'narrow'=4] {'wide','narrow'}, dimensions={0}, use_global_device_ids=true | all-gather | bytes 142560 | tf_op jit(solution)/shard_map/all_gather | solution.py:33
  302.0 0.1 reshape.41
  302.0 0.7 gather_fusion.1
  302.7 0.1 eq.31
  302.8 0.1 select_bitcast_fusion
  302.9 25.0 %all-to-all-done.1 = f32[8,10,135,135]{3,2,1,0:T(8,128)} async-done(((f32[8,10,135,135]{3,2,1,0:T(8,128)}), f32[8,10,135,135]{3,2,1,0:T(8,128)}, u32[]{:S(2)}, u32[]{:S(2)}) %all-to-all-start.1) | async-done | bytes 5832032 | tf_op jit(solution)/shard_map/all_to_all | solution.py:57
  327.9 12.3 %fusion.3 = f32[8,10,1,135]{3,2,1,0:T(1,128)S(1)} fusion(f32[8,10,135,135]{3,2,1,0:T(8,128)} %all-to-all-done.1, f32[8,10,135,1]{2,1,0,3:T(8,128)S(1)} %select_bitcast_fusion), kind=kOutput, calls=%fused_computation.10 | convolution fusion | flops 17496000 | bytes 5918400 | tf_op jit(solution)/shard_map/wkac,wkc->wka/dot_general | solution.py:60
  340.3 0.8 fusion.8
  341.0 0.0 reduce-scatter.2.cloned.1.call-update
  341.1 12.9 %copy.66 = f32[80,135,135]{0,2,1:T(8,128)} copy(f32[80,135,135]{2,1,0:T(8,128)} %bitcast.13) | data formatting | bytes 11664000
  353.9 31.1 %reduce-scatter.2.cloned.1.call-done = f32[8,135]{1,0:T(8,128)} async-done(((f32[32,135]{1,0:T(8,128)}), f32[8,135]{1,0:T(8,128)}) %reduce-scatter.2.cloned.1.call-update) | async-done | bytes 4336 | tf_op jit(solution)/shard_map/reduce_scatter | solution.py:65
  385.0 0.7 subtract_bitcast_fusion
  385.7 0.7 fusion.13
  386.4 0.8 fusion.10
  (14 shorter events, 0.1 us)
Async XLA Ops:
  7.2 11.7 %copy-start = (f32[320,135]{0,1:T(8,128)S(1)}, f32[320,135]{0,1:T(8,128)}, u32[]{:S(2)}) copy-start(f32[320,135]{0,1:T(8,128)} %param.9) | copy-start | bytes 518404
  7.2 1.0 copy-start.1
  8.1 1.5 copy-start.4
  11.6 67.3 %all-to-all-start = ((s32[8,10,2]{1,2,0:T(2,128)}), s32[8,10,2]{1,2,0:T(2,128)S(1)}, u32[]{:S(2)}, u32[]{:S(2)}) async-start(s32[8,10,2]{1,2,0:T(2,128)} %copy.63), calls=%async_computation | async-start | bytes 16384 | tf_op jit(solution)/shard_map/all_to_all | solution.py:58
  78.9 6.4 %copy-start.2 = (f32[8,135,135]{2,0,1:T(8,128)S(1)}, f32[8,135,135]{2,0,1:T(8,128)}, u32[]{:S(2)}) copy-start(f32[8,135,135]{2,0,1:T(8,128)} %param.11) | copy-start | bytes 1749604
  78.9 7.1 %copy-start.3 = (f32[8,320]{1,0:T(8,128)S(1)}, f32[8,320]{1,0:T(8,128)}, u32[]{:S(2)}) copy-start(f32[8,320]{1,0:T(8,128)} %param.10) | copy-start | bytes 30724
  78.9 249.0 %all-to-all-start.1 = ((f32[8,10,135,135]{3,2,1,0:T(8,128)}), f32[8,10,135,135]{3,2,1,0:T(8,128)}, u32[]{:S(2)}, u32[]{:S(2)}) async-start(f32[8,10,135,135]{3,2,1,0:T(8,128)} %bitcast.50), calls=%async_computation.1 | async-start | bytes 22282240 | tf_op jit(solution)/shard_map/all_to_all | solution.py:57
  85.1 300.0 %reduce-scatter.2.cloned.1.call-start = ((), (), s32[]{:S(2)}) async-start(), calls=%async_computation.3 | async-start | bytes 40960 | tf_op jit(solution)/shard_map/reduce_scatter | solution.py:65
Sparse Core Ops, SparseCore 0:
  341.2 43.8 reduce-scatter.1
where the time goes:
time: 395 us; the launch traced here: 394 us
  blocking collectives  215 us (54%)
  waiting for transfers between devices  56.1 us (14%)
  matrix products  51.7 us (13%)
  local copies, waits for them, and re-layouts  41.5 us (11%)
  between operations  14.2 us (4%)
  starting transfers between devices  13.7 us (3%)
    all_gather x1, blocking collectives, local(): lax.all_gather(sweep_one, ('wide', 'narrow'), axis=0, tiled=True)  215 us
    reduce_scatter x1, waiting for transfers between devices, local(): lax.psum_scatter(partial_sums, 'narrow', scatter_dimension=0, tiled=True)  31.1 us
    dot_general x1, matrix products, galerkin(): applied = jnp.einsum('fij,jc->fic', blocks, prolong, precision=PRECISE)  25.5 us
    all_to_all x1, waiting for transfers between devices, local(): lax.all_to_all(send_blocks, 'wide', split_axis=0, concat_axis=0, tiled=True)  25 us
    unnamed x12, local copies, waits for them, and re-layouts  13.6 us
    dot_general x1, matrix products, local(): results = jnp.einsum('wkac,wkc->wka', blocks, vectors, precision=PRECISE)  12.3 us
    scatter x1, local copies, waits for them, and re-layouts, local(): send_blocks = jnp.zeros((buffer_rows, coarse_width, coarse_width), jnp.fl...  12.1 us
    dot_general x1, matrix products, galerkin(): return jnp.einsum('ia,fic->fac', prolong, applied, precision=PRECISE)  10.7 us
  transfers between devices with their start and end apart: 3, of which 2 were waited for; matrix products, arithmetic and copies ran while one was open for 19% of the time, Pallas kernels for 0%

commit v1 on v0

v1 whole, which is shorter than its diff:
```python
import functools

import jax
import jax.numpy as jnp
from jax import lax
from jax.experimental import pallas as pl
from jax.experimental.pallas import tpu as pltpu
from jax.sharding import PartitionSpec as P

DAMPING = 0.7
PRECISE = lax.Precision.HIGHEST
BOTH = ("wide", "narrow")
LANES = 128
F32 = jnp.float32
BF16 = jnp.bfloat16


def round_up(value, unit):
    return (value + unit - 1) // unit * unit


def place_kernel(owner_rows, cap, wide, chunks, elems, slots, fetch, valid, row, col, count, table):
    faces = elems.shape[1]
    total = wide * cap

    def clear(i, c):
        count[i] = 0
        return c

    def empty(i, c):
        table[i] = -1
        return c

    def put(f, c):
        r = slots[elems[0, f]]
        row[f] = r
        col[f] = slots[elems[1, f]]
        owner = lax.div(r, owner_rows)
        rank = count[owner]
        count[owner] = rank + 1
        table[owner * cap + rank] = f
        return c

    lax.fori_loop(0, wide, clear, 0)
    lax.fori_loop(0, total, empty, 0)
    lax.fori_loop(0, faces, put, 0)
    at, first = 0, 0
    for ranks in chunks:

        def take(i, last, at=at, first=first, ranks=ranks):
            f = table[lax.div(i, ranks) * cap + first + lax.rem(i, ranks)]
            here = f >= 0
            last = jnp.where(here, f, last)
            valid[at + i] = here.astype(jnp.int32)
            fetch[at + i] = last
            return last

        lax.fori_loop(0, wide * ranks, take, jnp.int32(0))
        at += wide * ranks
        first += ranks


def place_faces(face_elems, coarse_slot, owner_rows, cap, wide, chunks):
    faces = face_elems.shape[0]
    total = wide * cap
    smem = pl.BlockSpec(memory_space=pltpu.SMEM)
    shape = lambda n: jax.ShapeDtypeStruct((n,), jnp.int32)
    return pl.pallas_call(
        functools.partial(place_kernel, owner_rows, cap, wide, chunks),
        out_shape=(shape(total), shape(total), shape(faces), shape(faces)),
        in_specs=[smem, smem],
        out_specs=(smem, smem, smem, smem),
        scratch_shapes=[pltpu.SMEM((wide,), jnp.int32), pltpu.SMEM((total,), jnp.int32)],
        name="place_faces",
    )(face_elems.T, coarse_slot)


def split(x):
    high = x.astype(BF16)
    return high, (x - high.astype(F32)).astype(BF16)


def dot3(a, b):
    (ah, al), (bh, bl) = a, b
    dot = functools.partial(jnp.dot, preferred_element_type=F32)
    return dot(ah, bh) + (dot(al, bh) + dot(ah, bl))


def galerkin_kernel(rows_main, fetch, valid, a_ref, p_ref, pt_ref, o_ref, ph, pl_, th, tl):
    step = pl.program_id(0)

    @pl.when(step == 0)
    def _():
        ph[...], pl_[...] = split(p_ref[...])
        th[...], tl[...] = split(pt_ref[...])

    @pl.when(valid[step] == 0)
    def _():
        o_ref[...] = jnp.zeros_like(o_ref)

    @pl.when(valid[step] != 0)
    def _():
        applied = dot3(split(a_ref[0]), (ph[...], pl_[...]))
        block = dot3((th[...], tl[...]), split(applied))
        o_ref[0, :rows_main, :] = block[:, :LANES]
        right = block[:, LANES:]
        turned = right[:LANES].T[:8]
        corner = pltpu.roll(right[LANES:rows_main], 0, 1, stride=8, stride_axis=0)
        corner = jnp.sum(corner, axis=0, keepdims=True)
        last = lax.broadcasted_iota(jnp.int32, (8, LANES), 0) == 7
        o_ref[0, rows_main:, :] = jnp.where(last, corner, turned)


def galerkin(face_blocks, p_pad, pt_pad, fetch, valid, wide, ranks):
    fine = face_blocks.shape[1]
    rows_main, width = pt_pad.shape[0], p_pad.shape[1]
    rows = rows_main + 8
    steps = wide * ranks
    out = pl.pallas_call(
        functools.partial(galerkin_kernel, rows_main),
        out_shape=jax.ShapeDtypeStruct((steps, rows, LANES), F32),
        grid_spec=pltpu.PrefetchScalarGridSpec(
            num_scalar_prefetch=2,
            grid=(steps,),
            in_specs=[
                pl.BlockSpec((1, fine, fine), lambda s, fetch, valid: (fetch[s], 0, 0)),
                pl.BlockSpec((fine, width), lambda s, fetch, valid: (0, 0)),
                pl.BlockSpec((rows_main, fine), lambda s, fetch, valid: (0, 0)),
            ],
            out_specs=pl.BlockSpec((1, rows, LANES), lambda s, fetch, valid: (s, 0, 0)),
            scratch_shapes=[
                pltpu.VMEM((fine, width), BF16),
                pltpu.VMEM((fine, width), BF16),
                pltpu.VMEM((rows_main, fine), BF16),
                pltpu.VMEM((rows_main, fine), BF16),
            ],
        ),
        cost_estimate=pl.CostEstimate(
            flops=steps * 4 * 6 * fine * fine * width // 10,
            bytes_accessed=steps * 4 * (fine * fine // 2 + rows * LANES),
            transcendentals=0,
        ),
        name="galerkin",
    )(fetch, valid, face_blocks, p_pad, pt_pad)
    return out.reshape(wide, ranks, rows, LANES)


def unpack_kernel(chunks, cap, coarse, *refs):
    count = len(chunks)
    parts, out = refs[:count], refs[count]
    tiles, turned, tile_sem, turned_sem = refs[count + 1 :]
    step, steps = pl.program_id(0), pl.num_programs(0)
    wide = parts[0].shape[0]
    total = wide * cap

    def copies(source_row, target, sem):
        first = 0
        for part, ranks in zip(parts, chunks):
            yield pltpu.make_async_copy(
                part.at[:, :, pl.ds(source_row, 8), :],
                target.at[:, pl.ds(first, ranks)],
                sem,
            )
            first += ranks

    def fetch(tile, buffer):
        return copies(pl.multiple_of(tile * 8, 8), tiles.at[buffer], tile_sem.at[buffer])

    def rows_of(block, k):
        rows = block.reshape(total * 8, LANES)[pl.ds(k, total, stride=8), :]
        if total < LANES:
            rows = jnp.concatenate([rows, jnp.zeros((LANES - total, LANES), F32)], axis=0)
        return rows.T

    buffer = lax.rem(step, 2)

    @pl.when(step == 0)
    def _():
        last = tiles.at[1]
        for copy in copies(steps * 8, last, tile_sem.at[1]):
            copy.start()
        for copy in fetch(0, 0):
            copy.start()
        for copy in copies(steps * 8, last, tile_sem.at[1]):
            copy.wait()
        for k in range(8):
            turns = rows_of(last, k)
            if k < 7:
                turned[pl.ds(k, LANES, stride=8), :] = turns
            else:
                turned[pl.ds(8 * LANES, 64), :] = turns[:64]

    @pl.when(step + 1 < steps)
    def _():
        for copy in fetch(step + 1, 1 - buffer):
            copy.start()

    for copy in fetch(step, buffer):
        copy.wait()
    block = tiles.at[buffer]
    for k in range(8):
        out[k, :LANES, :] = rows_of(block, k)[:, :total]
        out[k, LANES:coarse, :] = turned[pl.ds(pl.multiple_of((step * 8 + k) * 8, 8), 8), :][
            : coarse - LANES, :total
        ]


def unpack(parts, chunks, cap, coarse):
    wide, _, rows, _ = parts[0].shape
    total = wide * cap
    steps = rows // 8 - 1
    out = pl.pallas_call(
        functools.partial(unpack_kernel, chunks, cap, coarse),
        out_shape=jax.ShapeDtypeStruct((coarse, coarse, total), F32),
        grid=(steps,),
        in_specs=[pl.BlockSpec(memory_space=pl.ANY)] * len(parts),
        out_specs=pl.BlockSpec((8, coarse, total), lambda s: (s, 0, 0)),
        scratch_shapes=[
            pltpu.VMEM((2, wide, cap, 8, LANES), F32),
            pltpu.VMEM((8 * LANES + 64, LANES), F32),
            pltpu.SemaphoreType.DMA((2,)),
            pltpu.SemaphoreType.DMA,
        ],
        cost_estimate=pl.CostEstimate(
            flops=0, bytes_accessed=total * 8 * rows * LANES, transcendentals=0
        ),
        name="unpack",
    )(*parts)
    return jnp.transpose(out, (2, 0, 1))


def local(face_blocks, face_elems, coarse_slot, prolong, fine_residual, block_inverse):
    wide = lax.axis_size("wide")
    narrow = lax.axis_size("narrow")
    devices = wide * narrow
    dev_rows = fine_residual.shape[0]
    owner_rows = dev_rows * narrow
    faces = face_blocks.shape[0]
    coarse = prolong.shape[1]
    cap = max(2, (2 * faces + wide - 1) // wide)
    first = max(1, cap // 5)
    chunks = (first, cap - first)
    rows_total = dev_rows * devices

    coarse_rhs = jnp.dot(fine_residual, prolong, precision=PRECISE)
    sweep_one = DAMPING * jnp.einsum("snm,sm->sn", block_inverse, coarse_rhs, precision=PRECISE)
    flat = dev_rows * coarse
    flat_pad = round_up(flat, 8 * LANES)
    packed = jnp.pad(sweep_one.reshape(-1), (0, flat_pad - flat)).reshape(1, flat_pad // LANES, LANES)
    spread = jnp.broadcast_to(packed, (devices,) + packed.shape[1:])
    gathered = lax.all_to_all(spread, BOTH, split_axis=0, concat_axis=0, tiled=True)

    fetch, valid, row_slot, col_slot = place_faces(
        face_elems, coarse_slot, owner_rows, cap, wide, chunks
    )
    rows_main = round_up(coarse, 8)
    p_pad = jnp.pad(prolong, ((0, 0), (0, 2 * LANES - coarse)))
    pt_pad = jnp.pad(prolong.T, ((0, rows_main - coarse), (0, 0)))
    parts, at = [], 0
    for ranks in chunks:
        n = wide * ranks
        packed_blocks = galerkin(
            face_blocks, p_pad, pt_pad, fetch[at : at + n], valid[at : at + n], wide, ranks
        )
        at += n
        parts.append(
            lax.all_to_all(packed_blocks, "wide", split_axis=0, concat_axis=0, tiled=True)
        )

    iterate = gathered.reshape(devices, flat_pad)[:, :flat].reshape(rows_total, coarse)
    vectors = jnp.take(iterate, col_slot, axis=0)
    fine_vectors = jnp.dot(vectors, prolong.T, precision=PRECISE)
    applied = jnp.einsum("fij,fj->fi", face_blocks, fine_vectors, precision=PRECISE)
    results = jnp.dot(applied, prolong, precision=PRECISE)
    selector = (
        lax.broadcasted_iota(jnp.int32, (rows_total, faces), 0) == row_slot[None, :]
    ).astype(F32)
    sums = jnp.dot(selector, results, precision=PRECISE).reshape(devices, flat)
    sums = jnp.pad(sums, ((0, 0), (0, flat_pad - flat))).reshape(devices, flat_pad // LANES, LANES)
    sums = lax.all_to_all(sums, BOTH, split_axis=0, concat_axis=0, tiled=True)
    coupling = jnp.sum(sums, axis=0).reshape(-1)[:flat].reshape(dev_rows, coarse)
    update = (1.0 - DAMPING) * coarse_rhs - coupling
    sweep_two = sweep_one + DAMPING * jnp.einsum(
        "snm,sm->sn", block_inverse, update, precision=PRECISE
    )
    correction = jnp.dot(sweep_two, prolong.T, precision=PRECISE)
    return (correction, unpack(parts, chunks, cap, coarse))


def solution(mesh):
    placed = (
        P(BOTH, None, None),
        P(BOTH, None),
        P(),
        P(),
        P(BOTH, None),
        P(BOTH, None, None),
    )
    return jax.shard_map(
        local,
        mesh=mesh,
        in_specs=placed,
        out_specs=(P(BOTH, None), P(BOTH, None, None)),
        check_vma=False,
    )
```

time: 395 us -> 245 us (0.62)
  blocking collectives: 215 us -> 0 us
  Pallas kernels: 0 us -> 80.1 us
  waiting for transfers between devices: 56.1 us -> 107 us
  local copies, waits for them, and re-layouts: 41.5 us -> 8.44 us
  matrix products: 51.7 us -> 23.3 us
  between operations: 14.2 us -> 0.82 us
  starting transfers between devices: 13.7 us -> 22.7 us
    all_gather x1 -> x0, blocking collectives: 215 us -> none  [local(): lax.all_gather(sweep_one, ('wide', 'narrow'), axis=0, tiled=True)]
    all_to_all x2 -> x4, waiting for transfers between devices: 25 us -> 107 us  [the longest x2 101 us: local(): lax.all_to_all(packed_blocks, 'wide', split_axis=0, concat_axis=0, tiled=...]
    pallas_call x0 -> x4, Pallas kernels: none -> 80.1 us  [the longest x2 62.7 us: galerkin(): pl.pallas_call(functools.partial(galerkin_kernel, rows_main), out_shape=j...]
    reduce_scatter x1 -> x0, waiting for transfers between devices: 31.1 us -> none  [local(): lax.psum_scatter(partial_sums, 'narrow', scatter_dimension=0, tiled=True)]
    dot_general x4, matrix products: 49.2 us -> 20.8 us  [the longest x1 19.8 us: local(): jnp.einsum('fij,fj->fi', face_blocks, fine_vectors, precision=PRECISE)]
    scatter x3 -> x0, local copies, waits for them, and re-layouts: 12.8 us -> none  [the longest x1 12.1 us: local(): send_blocks = jnp.zeros((buffer_rows, coarse_width, coarse_width), jnp.fl...]
    unnamed x12 -> x17, local copies, waits for them, and re-layouts: 13.6 us -> 3.96 us
    all_to_all x2 -> x4, starting transfers between devices: 13.5 us -> 22.7 us  [the longest x2 12.8 us: local(): lax.all_to_all(packed_blocks, 'wide', split_axis=0, concat_axis=0, tiled=...]
  transfers between devices with their start and end apart: 3 -> 4, of which waited for: 2 -> 2; matrix products, arithmetic and copies ran while one was open for 19% -> 2% of each run, Pallas kernels for 0% -> 27%
where the time goes in v1:
time: 245 us; the launch traced here: 244 us
  waiting for transfers between devices  107 us (44%)
  Pallas kernels  80.1 us (33%)
  matrix products  23.3 us (10%)
  starting transfers between devices  22.7 us (9%)
  local copies, waits for them, and re-layouts  8.44 us (3%)
    all_to_all x2, waiting for transfers between devices, local(): lax.all_to_all(packed_blocks, 'wide', split_axis=0, concat_axis=0, tiled=...  101 us
    pallas_call x2, Pallas kernels, galerkin(): pl.pallas_call(functools.partial(galerkin_kernel, rows_main), out_shape=j...  62.7 us
    dot_general x1, matrix products, local(): jnp.einsum('fij,fj->fi', face_blocks, fine_vectors, precision=PRECISE)  19.8 us
    pallas_call x1, Pallas kernels, unpack(): pl.pallas_call(functools.partial(unpack_kernel, chunks, cap, coarse), out...  13.9 us
    all_to_all x2, starting transfers between devices, local(): lax.all_to_all(packed_blocks, 'wide', split_axis=0, concat_axis=0, tiled=...  12.8 us
    all_to_all x1, starting transfers between devices, local(): lax.all_to_all(spread, BOTH, split_axis=0, concat_axis=0, tiled=True)  7.33 us
    all_to_all x1, waiting for transfers between devices, local(): lax.all_to_all(spread, BOTH, split_axis=0, concat_axis=0, tiled=True)  5.86 us
  transfers between devices with their start and end apart: 4, of which 2 were waited for; matrix products, arithmetic and copies ran while one was open for 2% of the time, Pallas kernels for 27%

profile of v1, /device:TPU:0, one launch (start us, length us, event | category | flops | bytes accessed | tf_op | source)
XLA Modules:
  0.0 243.7 jit_solution(3008670950099756936)
XLA Ops:
  0.6 0.0 copy-start
  0.6 0.0 copy-start.1
  0.7 1.9 copy.12
  2.5 0.0 copy-done
  2.5 0.0 copy-done.1
  2.6 0.3 fusion.21
  2.8 0.7 fusion.16
  3.6 0.1 reshape.39
  3.7 0.7 broadcast_in_dim.22
  4.4 7.3 %all-to-all-start = ((f32[32,16,128]{2,1,0:T(8,128)}), f32[32,16,128]{2,1,0:T(8,128)S(1)}, u32[]{:S(2)}, u32[]{:S(2)}) async-start(f32[32,16,128]{2,1,0:T(8,128)} %broadcast_in_dim.22), calls=%async_computation | async-start | bytes 524288 | tf_op jit(solution)/shard_map/all_to_all | solution.py:251
  11.7 3.5 %place_faces.1 = (s32[80]{0:T(128)}, s32[80]{0:T(128)}, s32[40]{0:T(128)}, s32[40]{0:T(128)}) custom-call(s32[2,40]{1,0:T(2,128)} %bitcast.53, s32[256]{0:T(256)} %slots.1), custom_call_target="tpu_custom_call" | custom-call | tf_op jit(solution)/shard_map/place_faces/pallas_call | solution.py:68
  15.2 0.6 compare_select_fusion
  15.8 0.6 compare_and_fusion
  16.4 5.9 %all-to-all-done = f32[32,16,128]{2,1,0:T(8,128)S(1)} async-done(((f32[32,16,128]{2,1,0:T(8,128)}), f32[32,16,128]{2,1,0:T(8,128)S(1)}, u32[]{:S(2)}, u32[]{:S(2)}) %all-to-all-start) | async-done | bytes 262176 | tf_op jit(solution)/shard_map/all_to_all | solution.py:251
  22.3 0.1 copy.40
  22.4 0.2 reshape.41
  22.6 0.6 gather_fusion
  23.2 0.3 convolution_bitcast_fusion
  23.5 0.0 copy-start.5
  23.5 19.8 %fusion.5 = f32[40,1,320]{2,1,0:T(1,128)S(1)} fusion(f32[40,320,320]{2,1,0:T(8,128)} %a_ref.3, f32[40,320,1]{1,0,2:T(8,128)S(1)} %convolution_bitcast_fusion), kind=kOutput, calls=%fused_computation.10 | convolution fusion | flops 49152000 | bytes 16486400 | tf_op jit(solution)/shard_map/fij,fj->fi/dot_general | solution.py:273
  43.3 0.4 fusion.2
  43.7 0.0 copy-done.5
  43.8 0.2 fusion
  44.0 0.1 reshape.42
  44.2 0.8 copy.20
  44.9 2.6 %all-to-all-start.1 = ((f32[32,16,128]{2,1,0:T(8,128)}), f32[32,16,128]{2,1,0:T(8,128)S(1)}, u32[]{:S(2)}, u32[]{:S(2)}) async-start(f32[32,16,128]{2,1,0:T(8,128)} %bitcast.16), calls=%async_computation.1 | async-start | bytes 524288 | tf_op jit(solution)/shard_map/all_to_all | solution.py:280
  47.5 0.1 copy.10
  47.7 0.8 pad.18.p_ref
  48.4 0.7 pad.19.pt_ref
  49.1 18.4 %galerkin.2 = f32[16,144,128]{2,1,0:T(8,128)} custom-call(s32[16]{0:T(128)} %bitcast.55, s32[16]{0:T(128)} %bitcast.54, f32[40,320,320]{2,1,0:T(8,128)} %a_ref.3, f32[320,256]{1,0:T(8,128)} %pad.18.p_ref, f32[136,320]{1,0:T(8,128)} %pad.19.pt_ref), custom_call_target="tpu_custom_call" | custom-call | flops 1006632960 | bytes 4456448 | tf_op jit(solution)/shard_map/galerkin/pallas_call | solution.py:119
  67.6 0.0 all-to-all-done.1
  67.6 0.0 copy-start.4
  67.6 0.0 copy-start.3
  67.6 6.0 %all-to-all-start.2 = ((f32[8,2,144,128]{3,2,1,0:T(8,128)}), f32[8,2,144,128]{3,2,1,0:T(8,128)S(1)}, u32[]{:S(2)}, u32[]{:S(2)}) async-start(f32[8,2,144,128]{3,2,1,0:T(8,128)} %bitcast.48), calls=%async_computation.2 | async-start | bytes 2359296 | tf_op jit(solution)/shard_map/all_to_all | solution.py:267
  73.6 0.0 copy-done.4
  73.6 0.6 slice.22.fetch
  74.2 0.0 copy-done.3
  74.2 0.6 slice.23.valid
  74.8 44.2 %galerkin.3 = f32[64,144,128]{2,1,0:T(8,128)} custom-call(s32[64]{0:T(128)} %slice.22.fetch, s32[64]{0:T(128)} %slice.23.valid, f32[40,320,320]{2,1,0:T(8,128)} %a_ref.3, f32[320,256]{1,0:T(8,128)} %pad.18.p_ref, f32[136,320]{1,0:T(8,128)} %pad.19.pt_ref), custom_call_target="tpu_custom_call" | custom-call | flops 4026531840 | bytes 17825792 | tf_op jit(solution)/shard_map/galerkin/pallas_call | solution.py:119
  119.0 0.0 all-to-all-done.2.refs_0_
  119.0 0.0 copy-start.2
  119.0 1.1 copy-done.2
  120.0 6.8 %all-to-all-start.3 = ((f32[8,8,144,128]{3,2,1,0:T(8,128)}), f32[8,8,144,128]{3,2,1,0:T(8,128)}, u32[]{:S(2)}, u32[]{:S(2)}) async-start(f32[8,8,144,128]{3,2,1,0:T(8,128)} %bitcast.45), calls=%async_computation.3 | async-start | bytes 9437184 | tf_op jit(solution)/shard_map/all_to_all | solution.py:267
  126.9 0.1 reshape.45
  127.0 0.7 fusion.14
  127.7 0.8 fusion.11
  128.5 101.3 %all-to-all-done.3.refs_1_ = f32[8,8,144,128]{3,2,1,0:T(8,128)} async-done(((f32[8,8,144,128]{3,2,1,0:T(8,128)}), f32[8,8,144,128]{3,2,1,0:T(8,128)}, u32[]{:S(2)}, u32[]{:S(2)}) %all-to-all-start.3) | async-done | bytes 4718624 | tf_op jit(solution)/shard_map/all_to_all | solution.py:267
  229.8 13.9 %unpack.1 = f32[135,135,80]{2,1,0:T(8,128)} custom-call(f32[8,2,144,128]{3,2,1,0:T(8,128)} %copy-done.2, f32[8,8,144,128]{3,2,1,0:T(8,128)} %all-to-all-done.3.refs_1_), custom_call_target="tpu_custom_call" | custom-call | bytes 11796480 | tf_op jit(solution)/shard_map/unpack/pallas_call | solution.py:212
  (7 shorter events, 0.1 us)
Async XLA Ops:
  0.6 1.9 copy-start
  0.6 1.9 copy-start.1
  4.4 17.9 %all-to-all-start = ((f32[32,16,128]{2,1,0:T(8,128)}), f32[32,16,128]{2,1,0:T(8,128)S(1)}, u32[]{:S(2)}, u32[]{:S(2)}) async-start(f32[32,16,128]{2,1,0:T(8,128)} %broadcast_in_dim.22), calls=%async_computation | async-start | bytes 524288 | tf_op jit(solution)/shard_map/all_to_all | solution.py:251
  23.5 20.2 %copy-start.5 = (s32[40]{0:T(128)S(1)}, s32[40]{0:T(128)}, u32[]{:S(2)}) copy-start(s32[40]{0:T(128)} %get-tuple-element.6) | copy-start | bytes 484
  44.9 22.7 %all-to-all-start.1 = ((f32[32,16,128]{2,1,0:T(8,128)}), f32[32,16,128]{2,1,0:T(8,128)S(1)}, u32[]{:S(2)}, u32[]{:S(2)}) async-start(f32[32,16,128]{2,1,0:T(8,128)} %bitcast.16), calls=%async_computation.1 | async-start | bytes 524288 | tf_op jit(solution)/shard_map/all_to_all | solution.py:280
  67.6 6.0 %copy-start.4 = (s32[80]{0:T(128)S(1)}, s32[80]{0:T(128)}, u32[]{:S(2)}) copy-start(s32[80]{0:T(128)} %get-tuple-element.8) | copy-start | bytes 964
  67.6 6.6 %copy-start.3 = (s32[80]{0:T(128)S(1)}, s32[80]{0:T(128)}, u32[]{:S(2)}) copy-start(s32[80]{0:T(128)} %get-tuple-element.9) | copy-start | bytes 964
  67.6 51.4 %all-to-all-start.2 = ((f32[8,2,144,128]{3,2,1,0:T(8,128)}), f32[8,2,144,128]{3,2,1,0:T(8,128)S(1)}, u32[]{:S(2)}, u32[]{:S(2)}) async-start(f32[8,2,144,128]{3,2,1,0:T(8,128)} %bitcast.48), calls=%async_computation.2 | async-start | bytes 2359296 | tf_op jit(solution)/shard_map/all_to_all | solution.py:267
  119.0 1.1 copy-start.2
  120.0 109.8 %all-to-all-start.3 = ((f32[8,8,144,128]{3,2,1,0:T(8,128)}), f32[8,8,144,128]{3,2,1,0:T(8,128)}, u32[]{:S(2)}, u32[]{:S(2)}) async-start(f32[8,8,144,128]{3,2,1,0:T(8,128)} %bitcast.45), calls=%async_computation.3 | async-start | bytes 9437184 | tf_op jit(solution)/shard_map/all_to_all | solution.py:267

commit v2 on v0

v2 whole, which is shorter than its diff:
```python
import functools

import jax
import jax.numpy as jnp
from jax import lax
from jax.experimental import pallas as pl
from jax.experimental.pallas import tpu as pltpu
from jax.sharding import PartitionSpec as P

DAMPING = 0.7
PRECISE = lax.Precision.HIGHEST
BOTH = ("wide", "narrow")
LANES = 128
PAIR = 2
F32 = jnp.float32
BF16 = jnp.bfloat16


def round_up(value, unit):
    return (value + unit - 1) // unit * unit


def split(x):
    high = x.astype(BF16)
    return high, (x - high.astype(F32)).astype(BF16)


dot = functools.partial(jnp.dot, preferred_element_type=F32)


def send_plan(wide, cap):
    offsets = sorted(range(1, wide), key=lambda k: (-k.bit_length(), k))
    first = min(PAIR, cap)
    plan = [(offsets[0], 0, first)]
    if cap > first:
        plan.append((offsets[0], first, cap - first))
    return plan + [(k, 0, cap) for k in offsets[1:]]


def place_kernel(dev_rows, narrow, cap, elems, slots, me, pt, fetch, count, row, col, ph, pl_, th, tl, wide_pt):
    faces, wide = elems.shape[1], count.shape[0]
    owner_rows = dev_rows * narrow

    def clear(i, c):
        count[i] = 0
        return c

    def moved(r, owner):
        inner = r - owner * owner_rows
        n = lax.div(inner, dev_rows)
        return (n * wide + owner) * dev_rows + inner - n * dev_rows

    def put(f, c):
        r = slots[elems[0, f]]
        s = slots[elems[1, f]]
        owner = lax.div(r, owner_rows)
        row[f] = moved(r, owner)
        col[f] = moved(s, lax.div(s, owner_rows))
        at = owner ^ me[0]
        rank = count[at]
        count[at] = rank + 1
        fetch[at * cap + rank] = f
        return c

    def fill(k, c):
        for r in range(cap):

            @pl.when(r >= count[k])
            def _(r=r):
                fetch[k * cap + r] = fetch[k * cap + r - PAIR] if r >= PAIR else 0

        return c

    lax.fori_loop(0, wide, clear, 0)
    lax.fori_loop(0, faces, put, 0)
    lax.fori_loop(0, wide, fill, 0)
    rows, fine = th.shape
    wide_pt[...] = jnp.zeros_like(wide_pt)
    wide_pt[: pt.shape[0], :fine] = pt[...]
    th[...], tl[...] = split(wide_pt[:rows, :fine])
    ph[...], pl_[...] = split(wide_pt[...].T[:fine])


def place_faces(face_elems, coarse_slot, prolong, dev_rows, narrow, wide, cap):
    faces = face_elems.shape[0]
    fine, coarse = prolong.shape
    rows = round_up(coarse, 8)
    smem = pl.BlockSpec(memory_space=pltpu.SMEM)
    vmem = pl.BlockSpec(memory_space=pltpu.VMEM)
    ints = lambda n: jax.ShapeDtypeStruct((n,), jnp.int32)
    halves = lambda *s: jax.ShapeDtypeStruct(s, BF16)
    me = lax.axis_index("wide").astype(jnp.int32).reshape(1)
    return pl.pallas_call(
        functools.partial(place_kernel, dev_rows, narrow, cap),
        out_shape=(
            ints(wide * cap),
            ints(wide),
            ints(faces),
            ints(faces),
            halves(fine, 2 * LANES),
            halves(fine, 2 * LANES),
            halves(rows, fine),
            halves(rows, fine),
        ),
        in_specs=[smem, smem, smem, vmem],
        out_specs=(smem, smem, smem, smem, vmem, vmem, vmem, vmem),
        scratch_shapes=[pltpu.VMEM((2 * LANES, round_up(fine, LANES)), F32)],
        name="place_faces",
    )(face_elems.T, coarse_slot, me, prolong.T)


def galerkin_kernel(at, first, fetch, count, *refs):
    a_refs, (ph, pl_, th, tl, o_ref) = refs[:PAIR], refs[PAIR:]
    rank = first + pl.program_id(0) * PAIR
    rows = th.shape[0]
    full = ph.shape[0] // (2 * LANES) * 2 * LANES

    @pl.when(rank >= count[at])
    def _():
        o_ref[...] = jnp.zeros_like(o_ref)

    @pl.when(rank < count[at])
    def _():
        for j in range(PAIR):
            ah, al = split(a_refs[j][0])
            left = (ah[:, :full], al[:, :full], ah[:, :full], ah[:, full:], al[:, full:], ah[:, full:])
            right = (ph[:full], ph[:full], pl_[:full], ph[full:], ph[full:], pl_[full:])
            applied = dot(jnp.concatenate(left, axis=1), jnp.concatenate(right, axis=0))
            bh, bl = split(applied)
            block = dot(th[...], bh) + (dot(tl[...], bh) + dot(th[...], bl))
            if j:
                block = jnp.where(rank + j < count[at], block, 0.0)
            o_ref[j, :rows, :] = block[:, :LANES]
            rest = block[:, LANES:]
            turned = rest[:LANES].T[:8]
            corner = pltpu.roll(rest[LANES:rows], 0, 1, stride=8, stride_axis=0)
            corner = jnp.sum(corner, axis=0, keepdims=True)
            last = lax.broadcasted_iota(jnp.int32, (8, LANES), 0) == 7
            o_ref[j, rows:, :] = jnp.where(last, corner, turned)


def galerkin(face_blocks, operands, fetch, count, cap, piece):
    at, first, ranks = piece
    fine = face_blocks.shape[1]
    ph, _, th, _ = operands
    width, rows = ph.shape[1], th.shape[0]
    face = lambda j: lambda s, fetch, count: (fetch[at * cap + first + s * PAIR + j], 0, 0)
    const = lambda shape: pl.BlockSpec(shape, lambda s, fetch, count: (0, 0))
    return pl.pallas_call(
        functools.partial(galerkin_kernel, at, first),
        out_shape=jax.ShapeDtypeStruct((ranks, rows + 8, LANES), F32),
        grid_spec=pltpu.PrefetchScalarGridSpec(
            num_scalar_prefetch=2,
            grid=(ranks // PAIR,),
            in_specs=[pl.BlockSpec((1, fine, fine), face(j)) for j in range(PAIR)]
            + [const((fine, width))] * 2
            + [const((rows, fine))] * 2,
            out_specs=pl.BlockSpec((PAIR, rows + 8, LANES), lambda s, fetch, count: (s, 0, 0)),
        ),
        compiler_params=pltpu.CompilerParams(vmem_limit_bytes=50 << 20),
        cost_estimate=pl.CostEstimate(
            flops=ranks * 6 * fine * fine * width,
            bytes_accessed=ranks * 4 * (fine * fine + rows * LANES),
            transcendentals=0,
        ),
        name="galerkin",
    )(fetch, count, *[face_blocks] * PAIR, *operands)


def unpack_kernel(pieces, cap, coarse, me, *refs):
    parts, out = refs[: len(pieces)], refs[len(pieces)]
    buf, turned, sems = refs[len(pieces) + 1 :]
    step = pl.program_id(0)
    total, rows, _ = buf.shape
    main = rows - 8
    size = out.shape[0]
    groups = [(at, min(size, main - at)) for at in range(0, main, size)] + [(main, 8)]
    tail = len(groups) - 1

    def copies(g):
        at, extent = groups[g]
        for part, (offset, first, ranks) in zip(parts, pieces):
            ranks = min(ranks, cap - first)
            source = part.at[pl.ds(0, ranks), pl.ds(at, extent), :]
            target = buf.at[pl.ds((me[0] ^ offset) * cap + first, ranks), pl.ds(at, extent), :]
            yield pltpu.make_async_copy(source, target, sems.at[g])

    flat = buf.reshape(total * rows, LANES)

    def turn(r):
        x = flat[pl.ds(r, total, stride=rows), :]
        if total < LANES:
            x = jnp.concatenate([x, jnp.zeros((LANES - total, LANES), F32)], axis=0)
        return x.T

    @pl.when(step == 0)
    def _():
        for g in [tail, *range(tail)]:
            for copy in copies(g):
                copy.start()
        for copy in copies(tail):
            copy.wait()
        for k in range(7):
            turned[pl.ds(k, LANES, stride=8), :] = turn(main + k)
        turned[pl.ds(8 * LANES, 64), :] = turn(main + 7)[:64]

    for g in range(tail):

        @pl.when(step == g)
        def _(g=g):
            for copy in copies(g):
                copy.wait()

    for i in range(size):
        a = jnp.minimum(step * size + i, main - 1)
        out[i, :LANES, :] = turn(a)[:, :total]
        out[i, LANES:coarse, :] = turned[pl.ds(pl.multiple_of(a * 8, 8), 8), :][
            : coarse - LANES, :total
        ]


def unpack(parts, pieces, cap, coarse, wide, size=24):
    rows = parts[0].shape[1]
    total = wide * cap
    groups = pl.cdiv(rows - 8, size)
    me = lax.axis_index("wide").astype(jnp.int32).reshape(1)
    out = pl.pallas_call(
        functools.partial(unpack_kernel, pieces, cap, coarse),
        out_shape=jax.ShapeDtypeStruct((coarse, coarse, total), F32),
        grid=(groups,),
        in_specs=[pl.BlockSpec(memory_space=pltpu.SMEM)]
        + [pl.BlockSpec(memory_space=pl.ANY)] * len(parts),
        out_specs=pl.BlockSpec((size, coarse, total), lambda s: (s, 0, 0)),
        scratch_shapes=[
            pltpu.VMEM((total, rows, LANES), F32),
            pltpu.VMEM((8 * LANES + 64, LANES), F32),
            pltpu.SemaphoreType.DMA((groups + 1,)),
        ],
        compiler_params=pltpu.CompilerParams(vmem_limit_bytes=32 << 20),
        cost_estimate=pl.CostEstimate(
            flops=0, bytes_accessed=total * 8 * rows * LANES, transcendentals=0
        ),
        name="unpack",
    )(me, *parts)
    return jnp.transpose(out, (2, 0, 1))


def after(first, *values):
    out = lax.optimization_barrier((first, *values))
    return out[1:] if len(values) > 1 else out[1]


def everyone(x, axis, size):
    return lax.all_to_all(
        jnp.broadcast_to(x[None], (size, *x.shape)), axis, split_axis=0, concat_axis=0, tiled=True
    )


def local(face_blocks, face_elems, coarse_slot, prolong, fine_residual, block_inverse):
    wide = lax.axis_size("wide")
    narrow = lax.axis_size("narrow")
    dev_rows = fine_residual.shape[0]
    faces = face_blocks.shape[0]
    coarse = prolong.shape[1]
    cap = max(2, (2 * faces + wide - 1) // wide)
    slots = round_up(cap, PAIR)
    plan = send_plan(wide, slots)

    fetch, count, row, col, *operands = place_faces(
        face_elems, coarse_slot, prolong, dev_rows, narrow, wide, slots
    )
    parts, iterate = [], None
    for i, piece in enumerate(plan):
        block = galerkin(face_blocks, operands, fetch, count, slots, piece)
        fetch = after(block, fetch)
        pairs = [(w, w ^ piece[0]) for w in range(wide)]
        parts.append(lax.ppermute(block, "wide", pairs))
        if i == 1:
            fine_residual = after(block, fine_residual)
            rhs = jnp.dot(fine_residual, prolong, precision=PRECISE)
            sweep_one = DAMPING * jnp.einsum("snm,sm->sn", block_inverse, rhs, precision=PRECISE)
            fetch = after(sweep_one, fetch)
            iterate = everyone(sweep_one, "wide", wide)
    parts.append(galerkin(face_blocks, operands, fetch, count, slots, (0, 0, slots)))
    pieces = [*plan, (0, 0, slots)]
    iterate = after(parts[-1], iterate)
    iterate = everyone(iterate.reshape(wide * dev_rows, coarse), "narrow", narrow)
    iterate = iterate.reshape(-1, coarse)
    vectors = jnp.dot(jnp.take(iterate, col, axis=0), prolong.T, precision=PRECISE)
    applied = jnp.einsum("fij,fj->fi", face_blocks, vectors, precision=PRECISE)
    results = jnp.dot(applied, prolong, precision=PRECISE)
    total = iterate.shape[0]
    selector = (lax.broadcasted_iota(jnp.int32, (total, faces), 0) == row[None, :]).astype(F32)
    sums = jnp.dot(selector, results, precision=PRECISE).reshape(narrow, wide * dev_rows, coarse)
    sums = lax.all_to_all(sums, "narrow", split_axis=0, concat_axis=0, tiled=True)
    sums = jnp.sum(sums, axis=0).reshape(wide, dev_rows, coarse)
    sums = lax.all_to_all(sums, "wide", split_axis=0, concat_axis=0, tiled=True)
    coupling = jnp.sum(sums, axis=0)
    update = (1.0 - DAMPING) * rhs - coupling
    sweep_two = sweep_one + DAMPING * jnp.einsum(
        "snm,sm->sn", block_inverse, update, precision=PRECISE
    )
    correction = jnp.dot(sweep_two, prolong.T, precision=PRECISE)
    owned = unpack(parts, pieces, cap, coarse, wide)
    return (correction, owned)


def solution(mesh):
    placed = (
        P(BOTH, None, None),
        P(BOTH, None),
        P(),
        P(),
        P(BOTH, None),
        P(BOTH, None, None),
    )
    return jax.shard_map(
        local,
        mesh=mesh,
        in_specs=placed,
        out_specs=(P(BOTH, None), P(BOTH, None, None)),
        check_vma=False,
    )
```

time: 395 us -> 259 us (0.66)
  blocking collectives: 215 us -> 8.39 us
  Pallas kernels: 0 us -> 62.9 us
  waiting for transfers between devices: 56.1 us -> 109 us
  local copies, waits for them, and re-layouts: 41.5 us -> 12.3 us
  matrix products: 51.7 us -> 24.4 us
  starting transfers between devices: 13.7 us -> 39 us
  between operations: 14.2 us -> 1.08 us
    all_gather x1 -> x0, blocking collectives: 215 us -> none  [local(): lax.all_gather(sweep_one, ('wide', 'narrow'), axis=0, tiled=True)]
    ppermute x0 -> x8, waiting for transfers between devices: none -> 103 us  [local(): parts.append(lax.ppermute(block, 'wide', pairs))]
    pallas_call x0 -> x11, Pallas kernels: none -> 62.9 us  [the longest x9 52.4 us: galerkin(): pl.pallas_call(functools.partial(galerkin_kernel, at, first), out_shape=j...]
    reduce_scatter x1 -> x0, waiting for transfers between devices: 31.1 us -> none  [local(): lax.psum_scatter(partial_sums, 'narrow', scatter_dimension=0, tiled=True)]
    dot_general x6 -> x5, matrix products: 50.2 us -> 21.5 us  [the longest x1 19.8 us: local(): applied = jnp.einsum('fij,fj->fi', face_blocks, vectors, precision=PRECISE)]
    all_to_all x2 -> x3, waiting for transfers between devices: 25 us -> 6 us  [the longest x2 6 us: everyone(): lax.all_to_all(jnp.broadcast_to(x[None], (size, *x.shape)), axis, split_a...]
    ppermute x0 -> x8, starting transfers between devices: none -> 12.9 us  [local(): parts.append(lax.ppermute(block, 'wide', pairs))]
    scatter x3 -> x0, local copies, waits for them, and re-layouts: 12.8 us -> none  [the longest x1 12.1 us: local(): send_blocks = jnp.zeros((buffer_rows, coarse_width, coarse_width), jnp.fl...]
  transfers between devices with their start and end apart: 3 -> 11, of which waited for: 2 -> 6; matrix products, arithmetic and copies ran while one was open for 19% -> 12% of each run, Pallas kernels for 0% -> 19%
where the time goes in v2:
time: 259 us; the launch traced here: 258 us
  waiting for transfers between devices  109 us (42%)
  Pallas kernels  62.9 us (24%)
  starting transfers between devices  39 us (15%)
  matrix products  24.4 us (9%)
  local copies, waits for them, and re-layouts  12.3 us (5%)
  blocking collectives  8.39 us (3%)
    ppermute x8, waiting for transfers between devices, local(): parts.append(lax.ppermute(block, 'wide', pairs))  103 us
    pallas_call x9, Pallas kernels, galerkin(): pl.pallas_call(functools.partial(galerkin_kernel, at, first), out_shape=j...  52.4 us
    dot_general x1, matrix products, local(): applied = jnp.einsum('fij,fj->fi', face_blocks, vectors, precision=PRECISE)  19.8 us
    all_to_all x2, starting transfers between devices, everyone(): lax.all_to_all(jnp.broadcast_to(x[None], (size, *x.shape)), axis, split_a...  16 us
    ppermute x8, starting transfers between devices, local(): parts.append(lax.ppermute(block, 'wide', pairs))  12.9 us
    all_to_all x1, starting transfers between devices, local(): sums = lax.all_to_all(sums, 'wide', split_axis=0, concat_axis=0, tiled=True)  10.1 us
    unnamed x43, local copies, waits for them, and re-layouts  9.46 us
    all_to_all x1, blocking collectives, local(): lax.all_to_all(sums, 'narrow', split_axis=0, concat_axis=0, tiled=True)  8.39 us
  transfers between devices with their start and end apart: 11, of which 6 were waited for; matrix products, arithmetic and copies ran while one was open for 12% of the time, Pallas kernels for 19%

profile of v2, /device:TPU:0, one launch (start us, length us, event | category | flops | bytes accessed | tf_op | source)
XLA Modules:
  0.0 258.1 jit_solution(8276403597453940574)
XLA Ops:
  0.6 0.0 copy-start
  0.6 3.3 %place_faces.1 = (s32[80]{0:T(128)}, s32[8]{0:T(128)}, s32[40]{0:T(128)}, s32[40]{0:T(128)}, bf16[320,256]{1,0:T(8,128)(2,1)}, /*index=5*/bf16[320,256]{1,0:T(8,...) custom-call(s32[2,40]{1,0:T(2,128)} %bitcast.40, s32[256]{0:T(256)} %slots.1, s32[1]{0:T(128)} %bitcast.1.me, ...), custom_call_target="tpu_custom_call" | custom-call | tf_op jit(solution)/shard_map/place_faces/pallas_call | solution.py:93
  3.9 0.0 copy-start.1
  3.9 0.9 copy-done.1
  4.8 0.9 copy-done.3
  5.7 0.9 copy-done.5
  6.6 0.9 copy-done.7
  7.5 0.7 copy-done.12
  8.2 0.7 copy-done.14
  8.8 3.9 %galerkin.9 = f32[2,144,128]{2,1,0:T(8,128)} custom-call(s32[80]{0:T(128)S(1)} %copy-done.12, s32[8]{0:T(128)S(1)} %copy-done.14, f32[40,320,320]{2,1,0:T(8,128)} %refs_1_.17, f32[40,320,320]{2,1,0:T(8,128)} %refs_1_.17, bf16[320,256]{1,0:T(8,128)(2,1)S(1)} %copy-done.1, bf16[320,256]{1,0:T(8,128)(2,1)S(1)} %copy-done.3, bf16[136,320]{1,0:T(8,128)(2,1)S(1)} %copy-done.5, ...), custom_call_target="tpu_custom_call" | custom-call | flops 314572800 | bytes 958464 | tf_op jit(solution)/shard_map/galerkin/pallas_call | solution.py:149
  12.8 4.1 %collective-permute-start = (f32[2,144,128]{2,1,0:T(8,128)}, f32[2,144,128]{2,1,0:T(8,128)}, u32[]{:S(2)}, u32[]{:S(2)}) collective-permute-start(f32[2,144,128]{2,1,0:T(8,128)} %galerkin.9), channel_id=1, source_target_pairs={{0,16},{4,20},{8,24},{12,28},{16,0},{20,4},{24,8},{28,12},{1,17},{... | collective-permute-start | bytes 442376 | tf_op jit(solution)/shard_map/ppermute | solution.py:277
  16.9 0.0 copy-done.15
  16.9 4.8 %galerkin.10 = f32[8,144,128]{2,1,0:T(8,128)} custom-call(s32[80]{0:T(128)S(1)} %copy-done.13, s32[8]{0:T(128)S(1)} %copy-done.15, f32[40,320,320]{2,1,0:T(8,128)} %refs_1_.17, f32[40,320,320]{2,1,0:T(8,128)} %refs_1_.17, bf16[320,256]{1,0:T(8,128)(2,1)S(1)} %copy-done.1, bf16[320,256]{1,0:T(8,128)(2,1)S(1)} %copy-done.3, bf16[136,320]{1,0:T(8,128)(2,1)S(1)} %copy-done.5, ...), custom_call_target="tpu_custom_call" | custom-call | flops 1258291200 | bytes 3833856 | tf_op jit(solution)/shard_map/galerkin/pallas_call | solution.py:149
  21.6 0.0 collective-permute-start.1
  21.6 0.0 copy-done.17
  21.6 0.3 fusion.21
  21.9 1.9 copy.14
  23.8 0.0 copy-start.16
  23.9 0.7 fusion.16
  24.5 0.6 broadcast_in_dim.27
  25.2 0.0 copy-done.16
  25.2 7.6 %all-to-all-start = ((f32[8,8,135]{2,1,0:T(8,128)}), f32[8,8,135]{2,1,0:T(8,128)}, u32[]{:S(2)}, u32[]{:S(2)}) async-start(f32[8,8,135]{2,1,0:T(8,128)} %broadcast_in_dim.27), calls=%async_computation | async-start | bytes 131072 | tf_op jit(solution)/shard_map/all_to_all | solution.py:254
  32.8 5.1 %galerkin.11 = f32[10,144,128]{2,1,0:T(8,128)S(1)} custom-call(s32[80]{0:T(128)S(1)} %copy-done.13, s32[8]{0:T(128)S(1)} %copy-done.15, f32[40,320,320]{2,1,0:T(8,128)} %refs_1_.17, f32[40,320,320]{2,1,0:T(8,128)} %refs_1_.17, bf16[320,256]{1,0:T(8,128)(2,1)S(1)} %copy-done.2, bf16[320,256]{1,0:T(8,128)(2,1)S(1)} %copy-done.4, ...), custom_call_target="tpu_custom_call" | custom-call | flops 1572864000 | bytes 4792320 | tf_op jit(solution)/shard_map/galerkin/pallas_call | solution.py:149
  37.9 5.0 %galerkin.12 = f32[10,144,128]{2,1,0:T(8,128)S(1)} custom-call(s32[80]{0:T(128)S(1)} %copy-done.13, s32[8]{0:T(128)S(1)} %copy-done.15, f32[40,320,320]{2,1,0:T(8,128)} %refs_1_.17, f32[40,320,320]{2,1,0:T(8,128)} %refs_1_.17, bf16[320,256]{1,0:T(8,128)(2,1)S(1)} %copy-done.2, bf16[320,256]{1,0:T(8,128)(2,1)S(1)} %copy-done.4, ...), custom_call_target="tpu_custom_call" | custom-call | flops 1572864000 | bytes 4792320 | tf_op jit(solution)/shard_map/galerkin/pallas_call | solution.py:149
  42.9 8.1 %galerkin.13 = f32[10,144,128]{2,1,0:T(8,128)S(1)} custom-call(s32[80]{0:T(128)S(1)} %copy-done.13, s32[8]{0:T(128)S(1)} %copy-done.15, f32[40,320,320]{2,1,0:T(8,128)} %refs_1_.17, f32[40,320,320]{2,1,0:T(8,128)} %refs_1_.17, bf16[320,256]{1,0:T(8,128)(2,1)S(1)} %copy-done.2, bf16[320,256]{1,0:T(8,128)(2,1)S(1)} %copy-done.4, ...), custom_call_target="tpu_custom_call" | custom-call | flops 1572864000 | bytes 4792320 | tf_op jit(solution)/shard_map/galerkin/pallas_call | solution.py:149
  51.1 0.9 copy-done.9
  51.9 3.5 %galerkin.14 = f32[10,144,128]{2,1,0:T(8,128)S(1)} custom-call(s32[80]{0:T(128)S(1)} %copy-done.13, s32[8]{0:T(128)S(1)} %copy-done.15, f32[40,320,320]{2,1,0:T(8,128)} %refs_1_.17, f32[40,320,320]{2,1,0:T(8,128)} %refs_1_.17, bf16[320,256]{1,0:T(8,128)(2,1)S(1)} %copy-done.2, bf16[320,256]{1,0:T(8,128)(2,1)S(1)} %copy-done.4, ...), custom_call_target="tpu_custom_call" | custom-call | flops 1572864000 | bytes 4792320 | tf_op jit(solution)/shard_map/galerkin/pallas_call | solution.py:149
  55.4 0.9 copy-done.10
  56.3 6.6 %galerkin.15 = f32[10,144,128]{2,1,0:T(8,128)S(1)} custom-call(s32[80]{0:T(128)S(1)} %copy-done.13, s32[8]{0:T(128)S(1)} %copy-done.15, f32[40,320,320]{2,1,0:T(8,128)} %refs_1_.17, f32[40,320,320]{2,1,0:T(8,128)} %refs_1_.17, bf16[320,256]{1,0:T(8,128)(2,1)S(1)} %copy-done.2, bf16[320,256]{1,0:T(8,128)(2,1)S(1)} %copy-done.4, ...), custom_call_target="tpu_custom_call" | custom-call | flops 1572864000 | bytes 4792320 | tf_op jit(solution)/shard_map/galerkin/pallas_call | solution.py:149
  62.9 0.0 copy-start.11
  62.9 0.8 copy-done.11
  63.8 10.4 %galerkin.16 = f32[10,144,128]{2,1,0:T(8,128)} custom-call(s32[80]{0:T(128)S(1)} %copy-done.13, s32[8]{0:T(128)S(1)} %copy-done.15, f32[40,320,320]{2,1,0:T(8,128)} %refs_1_.17, f32[40,320,320]{2,1,0:T(8,128)} %refs_1_.17, bf16[320,256]{1,0:T(8,128)(2,1)S(1)} %copy-done.2, bf16[320,256]{1,0:T(8,128)(2,1)S(1)} %copy-done.4, bf16[136,320]{1,0:T(8,128)(2,1)S(1)} %copy-done.6, ...), custom_call_target="tpu_custom_call" | custom-call | flops 1572864000 | bytes 4792320 | tf_op jit(solution)/shard_map/galerkin/pallas_call | solution.py:149
  74.1 0.0 collective-permute-start.7
  74.2 5.1 %galerkin.17.refs_8_ = f32[10,144,128]{2,1,0:T(8,128)S(1)} custom-call(s32[80]{0:T(128)S(1)} %copy-done.13, s32[8]{0:T(128)S(1)} %copy-done.15, f32[40,320,320]{2,1,0:T(8,128)} %refs_1_.17, f32[40,320,320]{2,1,0:T(8,128)} %refs_1_.17, bf16[320,256]{1,0:T(8,128)(2,1)S(1)} %copy-done.2, bf16[320,256]{1,0:T(8,128)(2,1)S(1)} %copy-done.4, ...), custom_call_target="tpu_custom_call" | custom-call | flops 1572864000 | bytes 4792320 | tf_op jit(solution)/shard_map/galerkin/pallas_call | solution.py:149
  79.2 0.0 copy-start.18
  79.2 0.0 all-to-all-done
  79.2 1.6 broadcast_in_dim.29
  80.8 8.4 %all-to-all-start.1 = ((f32[4,64,135]{2,1,0:T(8,128)}), f32[4,64,135]{2,1,0:T(8,128)S(1)}, u32[]{:S(2)}, u32[]{:S(2)}) async-start(f32[4,64,135]{2,1,0:T(8,128)} %broadcast_in_dim.29), calls=%async_computation.1 | async-start | bytes 524288 | tf_op jit(solution)/shard_map/all_to_all | solution.py:254
  89.3 6.0 %all-to-all-done.1 = f32[4,64,135]{2,1,0:T(8,128)S(1)} async-done(((f32[4,64,135]{2,1,0:T(8,128)}), f32[4,64,135]{2,1,0:T(8,128)S(1)}, u32[]{:S(2)}, u32[]{:S(2)}) %all-to-all-start.1) | async-done | bytes 138272 | tf_op jit(solution)/shard_map/all_to_all | solution.py:254
  95.3 0.6 gather_fusion
  95.9 0.3 convolution_bitcast_fusion
  96.2 19.8 %fusion.5 = f32[40,1,320]{2,1,0:T(1,128)S(1)} fusion(f32[40,320,320]{2,1,0:T(8,128)} %refs_1_.17, f32[40,320,1]{1,0,2:T(8,128)S(1)} %convolution_bitcast_fusion), kind=kOutput, calls=%fused_computation.8 | convolution fusion | flops 49152000 | bytes 16486400 | tf_op jit(solution)/shard_map/fij,fj->fi/dot_general | solution.py:290
  116.0 0.4 fusion.2
  116.5 0.2 fusion
  116.7 8.4 %all_to_all.20 = f32[4,64,135]{2,1,0:T(8,128)S(1)} all-to-all(f32[4,64,135]{2,1,0:T(8,128)S(1)} %bitcast.38), channel_id=1, replica_groups=mesh['wide'=8,'narrow'=4] {'narrow'}, dimensions={0} | all-to-all | bytes 276480 | tf_op jit(solution)/shard_map/all_to_all | solution.py:295
  125.1 0.6 reduce_sum.18
  125.7 10.1 %all-to-all-start.3 = ((f32[8,8,135]{2,1,0:T(8,128)}), f32[8,8,135]{2,1,0:T(8,128)S(1)}, u32[]{:S(2)}, u32[]{:S(2)}) async-start(f32[8,8,135]{2,1,0:T(8,128)} %bitcast.10), calls=%async_computation.3 | async-start | bytes 131072 | tf_op jit(solution)/shard_map/all_to_all | solution.py:297
  135.8 2.9 %collective-permute-start.6 = (f32[10,144,128]{2,1,0:T(8,128)}, f32[10,144,128]{2,1,0:T(8,128)}, u32[]{:S(2)}, u32[]{:S(2)}) collective-permute-start(f32[10,144,128]{2,1,0:T(8,128)} %copy-done.11), channel_id=1, source_target_pairs={{0,12},{4,8},{8,4},{12,0},{16,28},{20,24},{24,20},{28,16},{1,13},{... | collective-permute-start | bytes 2211848 | tf_op jit(solution)/shard_map/ppermute | solution.py:277
  138.7 0.6 collective-permute-start.5
  139.3 0.0 collective-permute-done.refs_0_
  139.3 3.3 %collective-permute-start.4 = (f32[10,144,128]{2,1,0:T(8,128)}, f32[10,144,128]{2,1,0:T(8,128)}, u32[]{:S(2)}, u32[]{:S(2)}) collective-permute-start(f32[10,144,128]{2,1,0:T(8,128)} %copy-done.9), channel_id=1, source_target_pairs={{0,28},{4,24},{8,20},{12,16},{16,12},{20,8},{24,4},{28,0},{1,29},{... | collective-permute-start | bytes 2211848 | tf_op jit(solution)/shard_map/ppermute | solution.py:277
  142.6 0.0 collective-permute-done.1.refs_1_
  142.6 0.1 collective-permute-start.3
  142.7 0.0 collective-permute-done.7.refs_7_
  142.7 2.0 collective-permute-start.2
  144.6 0.0 all-to-all-done.3
  144.6 1.9 fusion.14
  146.5 0.8 fusion.11
  147.4 20.1 %collective-permute-done.6.refs_6_ = f32[10,144,128]{2,1,0:T(8,128)} collective-permute-done((f32[10,144,128]{2,1,0:T(8,128)}, f32[10,144,128]{2,1,0:T(8,128)}, u32[]{:S(2)}, u32[]{:S(2)}) %collective-permute-start.6) | collective-permute-done | bytes 737312 | tf_op jit(solution)/shard_map/ppermute | solution.py:277
  167.5 15.8 %collective-permute-done.5.refs_5_ = f32[10,144,128]{2,1,0:T(8,128)} collective-permute-done((f32[10,144,128]{2,1,0:T(8,128)}, f32[10,144,128]{2,1,0:T(8,128)}, u32[]{:S(2)}, u32[]{:S(2)}) %collective-permute-start.5) | collective-permute-done | bytes 737312 | tf_op jit(solution)/shard_map/ppermute | solution.py:277
  183.3 19.0 %collective-permute-done.4.refs_4_ = f32[10,144,128]{2,1,0:T(8,128)} collective-permute-done((f32[10,144,128]{2,1,0:T(8,128)}, f32[10,144,128]{2,1,0:T(8,128)}, u32[]{:S(2)}, u32[]{:S(2)}) %collective-permute-start.4) | collective-permute-done | bytes 737312 | tf_op jit(solution)/shard_map/ppermute | solution.py:277
  202.3 16.2 %collective-permute-done.3.refs_3_ = f32[10,144,128]{2,1,0:T(8,128)} collective-permute-done((f32[10,144,128]{2,1,0:T(8,128)S(1)}, f32[10,144,128]{2,1,0:T(8,128)}, u32[]{:S(2)}, u32[]{:S(2)}) %collective-permute-start.3) | collective-permute-done | bytes 737312 | tf_op jit(solution)/shard_map/ppermute | solution.py:277
  218.5 32.2 %collective-permute-done.2.refs_2_ = f32[10,144,128]{2,1,0:T(8,128)} collective-permute-done((f32[10,144,128]{2,1,0:T(8,128)S(1)}, f32[10,144,128]{2,1,0:T(8,128)}, u32[]{:S(2)}, u32[]{:S(2)}) %collective-permute-start.2) | collective-permute-done | bytes 737312 | tf_op jit(solution)/shard_map/ppermute | solution.py:277
  250.7 7.2 %unpack.1 = f32[135,135,80]{2,1,0:T(8,128)} custom-call(s32[1]{0:T(128)} %bitcast.1.me, f32[2,144,128]{2,1,0:T(8,128)} %collective-permute-done.refs_0_, f32[8,144,128]{2,1,0:T(8,128)} %collective-permute-done.1.refs_1_, f32[10,144,128]{2,1,0:T(8,128)} %collective-permute-done.2.refs_2_, f32[10,144,128]{2,1,0:T(8,128)} %collective-permute-done.3.refs_3_, ...), custom_call_target="tpu_custom_call" | custom-call | bytes 11796480 | tf_op jit(solution)/shard_map/unpack/pallas_call | solution.py:227
  (31 shorter events, 0.1 us)
Async XLA Ops:
  0.6 21.0 %copy-start = (f32[8,320]{1,0:T(8,128)S(1)}, f32[8,320]{1,0:T(8,128)}, u32[]{:S(2)}) copy-start(f32[8,320]{1,0:T(8,128)} %param.10) | copy-start | bytes 30724
  3.9 0.9 copy-start.1
  4.8 0.9 copy-start.3
  5.7 0.9 copy-start.5
  6.6 0.9 copy-start.7
  7.5 0.7 copy-start.12
  8.2 0.7 copy-start.14
  8.8 8.0 %copy-start.13 = (s32[80]{0:T(128)S(1)}, s32[80]{0:T(128)}, u32[]{:S(2)}) copy-start(s32[80]{0:T(128)} %get-tuple-element.38.fetch) | copy-start | bytes 964
  8.8 8.0 %copy-start.15 = (s32[8]{0:T(128)S(1)}, s32[8]{0:T(128)}, u32[]{:S(2)}) copy-start(s32[8]{0:T(128)} %get-tuple-element.22.count) | copy-start | bytes 100
  12.8 8.8 %copy-start.17 = (f32[320,135]{0,1:T(8,128)S(1)}, f32[320,135]{0,1:T(8,128)}, u32[]{:S(2)}) copy-start(f32[320,135]{0,1:T(8,128)} %param.9) | copy-start | bytes 518404
  12.8 126.5 %collective-permute-start = (f32[2,144,128]{2,1,0:T(8,128)}, f32[2,144,128]{2,1,0:T(8,128)}, u32[]{:S(2)}, u32[]{:S(2)}) collective-permute-start(f32[2,144,128]{2,1,0:T(8,128)} %galerkin.9), channel_id=1, source_target_pairs={{0,16},{4,20},{8,24},{12,28},{16,0},{20,4},{24,8},{28,12},{1,17},{... | collective-permute-start | bytes 442376 | tf_op jit(solution)/shard_map/ppermute | solution.py:277
  21.6 121.0 %collective-permute-start.1 = (f32[8,144,128]{2,1,0:T(8,128)}, f32[8,144,128]{2,1,0:T(8,128)}, u32[]{:S(2)}, u32[]{:S(2)}) collective-permute-start(f32[8,144,128]{2,1,0:T(8,128)} %galerkin.10), channel_id=1, source_target_pairs={{0,16},{4,20},{8,24},{12,28},{16,0},{20,4},{24,8},{28,12},{1,17},{... | collective-permute-start | bytes 1769480 | tf_op jit(solution)/shard_map/ppermute | solution.py:277
  23.8 1.3 copy-start.16
  23.8 9.0 %copy-start.2 = (bf16[320,256]{1,0:T(8,128)(2,1)S(1)}, bf16[320,256]{1,0:T(8,128)(2,1)}, u32[]{:S(2)}) copy-start(bf16[320,256]{1,0:T(8,128)(2,1)} %get-tuple-element.23.refs_2_) | copy-start | bytes 491524
  23.8 8.9 %copy-start.4 = (bf16[320,256]{1,0:T(8,128)(2,1)S(1)}, bf16[320,256]{1,0:T(8,128)(2,1)}, u32[]{:S(2)}) copy-start(bf16[320,256]{1,0:T(8,128)(2,1)} %get-tuple-element.24.refs_3_) | copy-start | bytes 491524
  23.8 8.9 %copy-start.6 = (bf16[136,320]{1,0:T(8,128)(2,1)S(1)}, bf16[136,320]{1,0:T(8,128)(2,1)}, u32[]{:S(2)}) copy-start(bf16[136,320]{1,0:T(8,128)(2,1)} %get-tuple-element.25.refs_4_) | copy-start | bytes 261124
  23.9 8.9 %copy-start.8 = (bf16[136,320]{1,0:T(8,128)(2,1)S(1)}, bf16[136,320]{1,0:T(8,128)(2,1)}, u32[]{:S(2)}) copy-start(bf16[136,320]{1,0:T(8,128)(2,1)} %get-tuple-element.26.refs_5_) | copy-start | bytes 261124
  25.2 54.1 %all-to-all-start = ((f32[8,8,135]{2,1,0:T(8,128)}), f32[8,8,135]{2,1,0:T(8,128)}, u32[]{:S(2)}, u32[]{:S(2)}) async-start(f32[8,8,135]{2,1,0:T(8,128)} %broadcast_in_dim.27), calls=%async_computation | async-start | bytes 131072 | tf_op jit(solution)/shard_map/all_to_all | solution.py:254
  51.0 0.9 copy-start.9
  55.4 0.9 copy-start.10
  62.9 0.9 copy-start.11
  63.8 10.4 %copy-start.20 = (s32[40]{0:T(128)S(1)}, s32[40]{0:T(128)}, u32[]{:S(2)}) copy-start(s32[40]{0:T(128)} %get-tuple-element.30) | copy-start | bytes 484
  74.1 68.5 %collective-permute-start.7 = (f32[10,144,128]{2,1,0:T(8,128)}, f32[10,144,128]{2,1,0:T(8,128)S(1)}, u32[]{:S(2)}, u32[]{:S(2)}) collective-permute-start(f32[10,144,128]{2,1,0:T(8,128)} %galerkin.16), channel_id=1, source_target_pairs={{0,4},{4,0},{8,12},{12,8},{16,20},{20,16},{24,28},{28,24},{1,5},{5... | collective-permute-start | bytes 2211848 | tf_op jit(solution)/shard_map/ppermute | solution.py:277
  79.2 16.7 %copy-start.18 = (f32[320,135]{0,1:T(8,128)S(1)}, f32[320,135]{0,1:T(8,128)}, u32[]{:S(2)}) copy-start(f32[320,135]{0,1:T(8,128)} %param.9) | copy-start | bytes 518404
  80.8 14.4 %all-to-all-start.1 = ((f32[4,64,135]{2,1,0:T(8,128)}), f32[4,64,135]{2,1,0:T(8,128)S(1)}, u32[]{:S(2)}, u32[]{:S(2)}) async-start(f32[4,64,135]{2,1,0:T(8,128)} %broadcast_in_dim.29), calls=%async_computation.1 | async-start | bytes 524288 | tf_op jit(solution)/shard_map/all_to_all | solution.py:254
  96.2 20.2 %copy-start.19 = (s32[40]{0:T(128)S(1)}, s32[40]{0:T(128)}, u32[]{:S(2)}) copy-start(s32[40]{0:T(128)} %get-tuple-element.29) | copy-start | bytes 484
  125.7 18.9 %all-to-all-start.3 = ((f32[8,8,135]{2,1,0:T(8,128)}), f32[8,8,135]{2,1,0:T(8,128)S(1)}, u32[]{:S(2)}, u32[]{:S(2)}) async-start(f32[8,8,135]{2,1,0:T(8,128)} %bitcast.10), calls=%async_computation.3 | async-start | bytes 131072 | tf_op jit(solution)/shard_map/all_to_all | solution.py:297
  135.8 31.6 %collective-permute-start.6 = (f32[10,144,128]{2,1,0:T(8,128)}, f32[10,144,128]{2,1,0:T(8,128)}, u32[]{:S(2)}, u32[]{:S(2)}) collective-permute-start(f32[10,144,128]{2,1,0:T(8,128)} %copy-done.11), channel_id=1, source_target_pairs={{0,12},{4,8},{8,4},{12,0},{16,28},{20,24},{24,20},{28,16},{1,13},{... | collective-permute-start | bytes 2211848 | tf_op jit(solution)/shard_map/ppermute | solution.py:277
  138.7 44.5 %collective-permute-start.5 = (f32[10,144,128]{2,1,0:T(8,128)}, f32[10,144,128]{2,1,0:T(8,128)}, u32[]{:S(2)}, u32[]{:S(2)}) collective-permute-start(f32[10,144,128]{2,1,0:T(8,128)} %copy-done.10), channel_id=1, source_target_pairs={{0,8},{4,12},{8,0},{12,4},{16,24},{20,28},{24,16},{28,20},{1,9},{5... | collective-permute-start | bytes 2211848 | tf_op jit(solution)/shard_map/ppermute | solution.py:277
  139.3 63.0 %collective-permute-start.4 = (f32[10,144,128]{2,1,0:T(8,128)}, f32[10,144,128]{2,1,0:T(8,128)}, u32[]{:S(2)}, u32[]{:S(2)}) collective-permute-start(f32[10,144,128]{2,1,0:T(8,128)} %copy-done.9), channel_id=1, source_target_pairs={{0,28},{4,24},{8,20},{12,16},{16,12},{20,8},{24,4},{28,0},{1,29},{... | collective-permute-start | bytes 2211848 | tf_op jit(solution)/shard_map/ppermute | solution.py:277
  142.6 75.9 %collective-permute-start.3 = (f32[10,144,128]{2,1,0:T(8,128)S(1)}, f32[10,144,128]{2,1,0:T(8,128)}, u32[]{:S(2)}, u32[]{:S(2)}) collective-permute-start(f32[10,144,128]{2,1,0:T(8,128)S(1)} %galerkin.12), channel_id=1, source_target_pairs={{0,24},{4,28},{8,16},{12,20},{16,8},{20,12},{24,0},{28,4},{1,25},{... | collective-permute-start | bytes 2211848 | tf_op jit(solution)/shard_map/ppermute | solution.py:277
  142.7 108.0 %collective-permute-start.2 = (f32[10,144,128]{2,1,0:T(8,128)S(1)}, f32[10,144,128]{2,1,0:T(8,128)}, u32[]{:S(2)}, u32[]{:S(2)}) collective-permute-start(f32[10,144,128]{2,1,0:T(8,128)S(1)} %galerkin.11), channel_id=1, source_target_pairs={{0,20},{4,16},{8,28},{12,24},{16,4},{20,0},{24,12},{28,8},{1,21},{... | collective-permute-start | bytes 2211848 | tf_op jit(solution)/shard_map/ppermute | solution.py:277

commit v3 on v2

--- a/solution.py
+++ b/solution.py
@@ -12,6 +12,7 @@
 BOTH = ("wide", "narrow")
 LANES = 128
 PAIR = 2
+EXCHANGE = 4
 F32 = jnp.float32
 BF16 = jnp.bfloat16
 
@@ -30,38 +31,29 @@
 
 def send_plan(wide, cap):
     offsets = sorted(range(1, wide), key=lambda k: (-k.bit_length(), k))
-    first = min(PAIR, cap)
+    offsets = [k for k in offsets if 1 < k < wide - 1] + [wide - 1, 1]
+    first = min(2 * PAIR, cap)
     plan = [(offsets[0], 0, first)]
     if cap > first:
         plan.append((offsets[0], first, cap - first))
     return plan + [(k, 0, cap) for k in offsets[1:]]
 
 
-def place_kernel(dev_rows, narrow, cap, elems, slots, me, pt, fetch, count, row, col, ph, pl_, th, tl, wide_pt):
+def place_kernel(owner_rows, cap, elems, slots, me, pt, fetch, count, ph, pl_, th, tl, p32, wide_pt):
     faces, wide = elems.shape[1], count.shape[0]
-    owner_rows = dev_rows * narrow
-
-    def clear(i, c):
-        count[i] = 0
-        return c
-
-    def moved(r, owner):
-        inner = r - owner * owner_rows
-        n = lax.div(inner, dev_rows)
-        return (n * wide + owner) * dev_rows + inner - n * dev_rows
 
     def put(f, c):
-        r = slots[elems[0, f]]
-        s = slots[elems[1, f]]
-        owner = lax.div(r, owner_rows)
-        row[f] = moved(r, owner)
-        col[f] = moved(s, lax.div(s, owner_rows))
+        owner = lax.div(slots[elems[0, f]], owner_rows)
         at = owner ^ me[0]
         rank = count[at]
         count[at] = rank + 1
         fetch[at * cap + rank] = f
         return c
 
+    for k in range(wide):
+        count[k] = 0
+    lax.fori_loop(0, faces, put, 0, unroll=8)
+
     def fill(k, c):
         for r in range(cap):
 
@@ -71,42 +63,102 @@
 
         return c
 
-    lax.fori_loop(0, wide, clear, 0)
-    lax.fori_loop(0, faces, put, 0)
     lax.fori_loop(0, wide, fill, 0)
     rows, fine = th.shape
     wide_pt[...] = jnp.zeros_like(wide_pt)
     wide_pt[: pt.shape[0], :fine] = pt[...]
     th[...], tl[...] = split(wide_pt[:rows, :fine])
-    ph[...], pl_[...] = split(wide_pt[...].T[:fine])
-
-
-def place_faces(face_elems, coarse_slot, prolong, dev_rows, narrow, wide, cap):
-    faces = face_elems.shape[0]
+    p32[...] = wide_pt[...].T[:fine]
+    ph[...], pl_[...] = split(p32[...])
+
+
+def index_kernel(dev_rows, narrow, wide, elems, slots, row, col):
+    owner_rows = dev_rows * narrow
+
+    def moved(r):
+        owner = lax.div(r, owner_rows)
+        inner = r - owner * owner_rows
+        n = lax.div(inner, dev_rows)
+        return (n * wide + owner) * dev_rows + inner - n * dev_rows
+
+    def put(f, c):
+        row[f] = moved(slots[elems[0, f]])
+        col[f] = moved(slots[elems[1, f]])
+        return c
+
+    lax.fori_loop(0, elems.shape[1], put, 0, unroll=8)
+
+
+SMEM = pl.BlockSpec(memory_space=pltpu.SMEM)
+VMEM = pl.BlockSpec(memory_space=pltpu.VMEM)
+
+
+def ints(n):
+    return jax.ShapeDtypeStruct((n,), jnp.int32)
+
+
+def place_faces(face_elems, coarse_slot, prolong, owner_rows, wide, cap):
     fine, coarse = prolong.shape
     rows = round_up(coarse, 8)
-    smem = pl.BlockSpec(memory_space=pltpu.SMEM)
-    vmem = pl.BlockSpec(memory_space=pltpu.VMEM)
-    ints = lambda n: jax.ShapeDtypeStruct((n,), jnp.int32)
     halves = lambda *s: jax.ShapeDtypeStruct(s, BF16)
     me = lax.axis_index("wide").astype(jnp.int32).reshape(1)
     return pl.pallas_call(
-        functools.partial(place_kernel, dev_rows, narrow, cap),
+        functools.partial(place_kernel, owner_rows, cap),
         out_shape=(
             ints(wide * cap),
             ints(wide),
-            ints(faces),
-            ints(faces),
             halves(fine, 2 * LANES),
             halves(fine, 2 * LANES),
             halves(rows, fine),
             halves(rows, fine),
-        ),
-        in_specs=[smem, smem, smem, vmem],
-        out_specs=(smem, smem, smem, smem, vmem, vmem, vmem, vmem),
+            jax.ShapeDtypeStruct((fine, 2 * LANES), F32),
+        ),
+        in_specs=[SMEM, SMEM, SMEM, VMEM],
+        out_specs=(SMEM, SMEM, VMEM, VMEM, VMEM, VMEM, VMEM),
         scratch_shapes=[pltpu.VMEM((2 * LANES, round_up(fine, LANES)), F32)],
+        compiler_params=pltpu.CompilerParams(vmem_limit_bytes=8 << 20),
         name="place_faces",
     )(face_elems.T, coarse_slot, me, prolong.T)
+
+
+def face_rows(face_elems, coarse_slot, dev_rows, narrow, wide):
+    faces = face_elems.shape[0]
+    return pl.pallas_call(
+        functools.partial(index_kernel, dev_rows, narrow, wide),
+        out_shape=(ints(faces), ints(faces)),
+        in_specs=[SMEM, SMEM],
+        out_specs=(SMEM, SMEM),
+        compiler_params=pltpu.CompilerParams(vmem_limit_bytes=8 << 20),
+        name="face_rows",
+    )(face_elems.T, coarse_slot)
+
+
+def product_kernel(a_ref, v_ref, p_ref, o_ref):
+    for j in range(a_ref.shape[0]):
+        applied = jnp.sum(a_ref[j] * v_ref[j : j + 1, :], axis=1, keepdims=True)
+        o_ref[j : j + 1, :] = jnp.sum(p_ref[...] * applied, axis=0, keepdims=True)
+
+
+def products(face_blocks, vectors, p32):
+    faces, fine, _ = face_blocks.shape
+    group = 8 if faces % 8 == 0 else faces
+    width = p32.shape[1]
+    return pl.pallas_call(
+        product_kernel,
+        out_shape=jax.ShapeDtypeStruct((faces, width), F32),
+        grid=(faces // group,),
+        in_specs=[
+            pl.BlockSpec((group, fine, fine), lambda s: (s, 0, 0)),
+            pl.BlockSpec((group, fine), lambda s: (s, 0)),
+            VMEM,
+        ],
+        out_specs=pl.BlockSpec((group, width), lambda s: (s, 0)),
+        compiler_params=pltpu.CompilerParams(vmem_limit_bytes=48 << 20),
+        cost_estimate=pl.CostEstimate(
+            flops=4 * faces * fine * fine, bytes_accessed=4 * faces * fine * fine, transcendentals=0
+        ),
+        name="products",
+    )(face_blocks, vectors, p32)
 
 
 def galerkin_kernel(at, first, fetch, count, *refs):
@@ -121,12 +173,20 @@
 
     @pl.when(rank < count[at])
     def _():
+        left = []
         for j in range(PAIR):
             ah, al = split(a_refs[j][0])
-            left = (ah[:, :full], al[:, :full], ah[:, :full], ah[:, full:], al[:, full:], ah[:, full:])
-            right = (ph[:full], ph[:full], pl_[:full], ph[full:], ph[full:], pl_[full:])
-            applied = dot(jnp.concatenate(left, axis=1), jnp.concatenate(right, axis=0))
-            bh, bl = split(applied)
+            left.append(
+                jnp.concatenate(
+                    (ah[:, :full], al[:, :full], ah[:, :full], ah[:, full:], al[:, full:], ah[:, full:]),
+                    axis=1,
+                )
+            )
+        right = (ph[:full], ph[:full], pl_[:full], ph[full:], ph[full:], pl_[full:])
+        applied = dot(jnp.concatenate(left, axis=0), jnp.concatenate(right, axis=0))
+        fine = ph.shape[0]
+        for j in range(PAIR):
+            bh, bl = split(applied[j * fine : (j + 1) * fine])
             block = dot(th[...], bh) + (dot(tl[...], bh) + dot(th[...], bl))
             if j:
                 block = jnp.where(rank + j < count[at], block, 0.0)
@@ -145,7 +205,6 @@
     ph, _, th, _ = operands
     width, rows = ph.shape[1], th.shape[0]
     face = lambda j: lambda s, fetch, count: (fetch[at * cap + first + s * PAIR + j], 0, 0)
-    const = lambda shape: pl.BlockSpec(shape, lambda s, fetch, count: (0, 0))
     return pl.pallas_call(
         functools.partial(galerkin_kernel, at, first),
         out_shape=jax.ShapeDtypeStruct((ranks, rows + 8, LANES), F32),
@@ -153,8 +212,7 @@
             num_scalar_prefetch=2,
             grid=(ranks // PAIR,),
             in_specs=[pl.BlockSpec((1, fine, fine), face(j)) for j in range(PAIR)]
-            + [const((fine, width))] * 2
-            + [const((rows, fine))] * 2,
+            + [VMEM] * 4,
             out_specs=pl.BlockSpec((PAIR, rows + 8, LANES), lambda s, fetch, count: (s, 0, 0)),
         ),
         compiler_params=pltpu.CompilerParams(vmem_limit_bytes=50 << 20),
@@ -266,36 +324,43 @@
     slots = round_up(cap, PAIR)
     plan = send_plan(wide, slots)
 
-    fetch, count, row, col, *operands = place_faces(
-        face_elems, coarse_slot, prolong, dev_rows, narrow, wide, slots
-    )
-    parts, iterate = [], None
+    fetch, count, *operands, p32 = place_faces(
+        face_elems, coarse_slot, prolong, dev_rows * narrow, wide, slots
+    )
+    parts = []
     for i, piece in enumerate(plan):
         block = galerkin(face_blocks, operands, fetch, count, slots, piece)
         fetch = after(block, fetch)
         pairs = [(w, w ^ piece[0]) for w in range(wide)]
         parts.append(lax.ppermute(block, "wide", pairs))
-        if i == 1:
-            fine_residual = after(block, fine_residual)
+        if i == 0:
+            fine_residual, face_elems = after(block, fine_residual, face_elems)
             rhs = jnp.dot(fine_residual, prolong, precision=PRECISE)
             sweep_one = DAMPING * jnp.einsum("snm,sm->sn", block_inverse, rhs, precision=PRECISE)
             fetch = after(sweep_one, fetch)
             iterate = everyone(sweep_one, "wide", wide)
+        if i == EXCHANGE - 1:
+            iterate, face_elems = after(block, iterate, face_elems)
+            iterate = everyone(iterate.reshape(wide * dev_rows, coarse), "narrow", narrow)
+            row, col = face_rows(face_elems, coarse_slot, dev_rows, narrow, wide)
+            fetch = after(row, fetch)
+        if i == EXCHANGE:
+            iterate = after(block, iterate).reshape(-1, coarse)
+            vectors = jnp.dot(jnp.take(iterate, col, axis=0), prolong.T, precision=PRECISE)
+            results = products(face_blocks, vectors, p32)
+            total = iterate.shape[0]
+            selector = lax.broadcasted_iota(jnp.int32, (total, faces), 0) == row[None, :]
+            sums = jnp.dot(selector.astype(F32), results, precision=PRECISE)[:, :coarse]
+            sums = sums.reshape(narrow, wide * dev_rows, coarse)
+            fetch = after(sums, fetch)
+            sums = lax.all_to_all(sums, "narrow", split_axis=0, concat_axis=0, tiled=True)
+        if i == EXCHANGE + 1:
+            sums = jnp.sum(after(block, sums), axis=0).reshape(wide, dev_rows, coarse)
+            fetch = after(sums, fetch)
+            sums = lax.all_to_all(sums, "wide", split_axis=0, concat_axis=0, tiled=True)
     parts.append(galerkin(face_blocks, operands, fetch, count, slots, (0, 0, slots)))
     pieces = [*plan, (0, 0, slots)]
-    iterate = after(parts[-1], iterate)
-    iterate = everyone(iterate.reshape(wide * dev_rows, coarse), "narrow", narrow)
-    iterate = iterate.reshape(-1, coarse)
-    vectors = jnp.dot(jnp.take(iterate, col, axis=0), prolong.T, precision=PRECISE)
-    applied = jnp.einsum("fij,fj->fi", face_blocks, vectors, precision=PRECISE)
-    results = jnp.dot(applied, prolong, precision=PRECISE)
-    total = iterate.shape[0]
-    selector = (lax.broadcasted_iota(jnp.int32, (total, faces), 0) == row[None, :]).astype(F32)
-    sums = jnp.dot(selector, results, precision=PRECISE).reshape(narrow, wide * dev_rows, coarse)
-    sums = lax.all_to_all(sums, "narrow", split_axis=0, concat_axis=0, tiled=True)
-    sums = jnp.sum(sums, axis=0).reshape(wide, dev_rows, coarse)
-    sums = lax.all_to_all(sums, "wide", split_axis=0, concat_axis=0, tiled=True)
-    coupling = jnp.sum(sums, axis=0)
+    coupling = jnp.sum(after(parts[-1], sums), axis=0)
     update = (1.0 - DAMPING) * rhs - coupling
     sweep_two = sweep_one + DAMPING * jnp.einsum(
         "snm,sm->sn", block_inverse, update, precision=PRECISE

time: 259 us -> 202 us (0.78)
  waiting for transfers between devices: 109 us -> 45.4 us
  starting transfers between devices: 39 us -> 60.4 us
  matrix products: 24.4 us -> 4.89 us
  Pallas kernels: 62.9 us -> 72.5 us
  blocking collectives: 8.39 us -> 0 us
    ppermute x8, waiting for transfers between devices: 103 us -> 39.3 us  [local(): parts.append(lax.ppermute(block, 'wide', pairs))]
    dot_general x2 -> x1, matrix products: 20.2 us -> 0.92 us  [local(): sums = jnp.dot(selector.astype(F32), results, precision=PRECISE)[:, :coarse]]
    all_to_all x2, starting transfers between devices: 16 us -> 30.1 us  [everyone(): lax.all_to_all(jnp.broadcast_to(x[None], (size, *x.shape)), axis, split_a...]
    pallas_call x1 -> x3, Pallas kernels: 3.25 us -> 11.8 us  [the longest x1 8.35 us: products(): pl.pallas_call(product_kernel, out_shape=jax.ShapeDtypeStruct((faces, wid...]
    all_to_all x1 -> x0, blocking collectives: 8.39 us -> none  [local(): lax.all_to_all(sums, 'narrow', split_axis=0, concat_axis=0, tiled=True)]
    ppermute x8, starting transfers between devices: 12.9 us -> 20.9 us  [local(): parts.append(lax.ppermute(block, 'wide', pairs))]
    all_to_all x1, starting transfers between devices: 10.1 us -> 5.31 us  [local(): sums = lax.all_to_all(sums, 'wide', split_axis=0, concat_axis=0, tiled=True)]
    all_to_all x0 -> x1, starting transfers between devices: none -> 4.04 us  [local(): lax.all_to_all(sums, 'narrow', split_axis=0, concat_axis=0, tiled=True)]
  transfers between devices with their start and end apart: 11 -> 12, of which waited for: 6 -> 3; matrix products, arithmetic and copies ran while one was open for 12% -> 8% of each run, Pallas kernels for 19% -> 29%
where the time goes in v3:
time: 202 us; the launch traced here: 199 us
  Pallas kernels  72.5 us (36%)
  starting transfers between devices  60.4 us (30%)
  waiting for transfers between devices  45.4 us (22%)
  local copies, waits for them, and re-layouts  13.4 us (7%)
  matrix products  4.89 us (2%)
    pallas_call x9, Pallas kernels, galerkin(): pl.pallas_call(functools.partial(galerkin_kernel, at, first), out_shape=j...  53.6 us
    ppermute x8, waiting for transfers between devices, local(): parts.append(lax.ppermute(block, 'wide', pairs))  39.3 us
    all_to_all x2, starting transfers between devices, everyone(): lax.all_to_all(jnp.broadcast_to(x[None], (size, *x.shape)), axis, split_a...  30.1 us
    ppermute x8, starting transfers between devices, local(): parts.append(lax.ppermute(block, 'wide', pairs))  20.9 us
    pallas_call x1, Pallas kernels, products(): pl.pallas_call(product_kernel, out_shape=jax.ShapeDtypeStruct((faces, wid...  8.35 us
    pallas_call x1, Pallas kernels, unpack(): pl.pallas_call(functools.partial(unpack_kernel, pieces, cap, coarse), out...  7.14 us
    unnamed x21, local copies, waits for them, and re-layouts  6.86 us
    all_to_all x2, waiting for transfers between devices, everyone(): lax.all_to_all(jnp.broadcast_to(x[None], (size, *x.shape)), axis, split_a...  6.1 us
  transfers between devices with their start and end apart: 12, of which 3 were waited for; matrix products, arithmetic and copies ran while one was open for 8% of the time, Pallas kernels for 29%

profile of v3, /device:TPU:0, one launch (start us, length us, event | category | flops | bytes accessed | tf_op | source)
XLA Modules:
  0.0 199.2 jit_solution(14605181798396577652)
XLA Ops:
  0.6 0.0 copy-start
  0.6 0.0 copy-start.1
  0.7 0.9 copy-done.1
  1.6 0.7 copy-done.5
  2.3 0.7 copy-done.7
  2.9 1.7 place_faces.1
  4.6 0.0 copy-start.3
  4.7 0.7 copy-done.3
  5.4 5.2 %galerkin.9 = f32[4,144,128]{2,1,0:T(8,128)} custom-call(s32[80]{0:T(128)S(1)} %get-tuple-element.56.fetch, s32[8]{0:T(128)S(1)} %get-tuple-element.31.count, f32[40,320,320]{2,1,0:T(8,128)} %refs_1_.17, f32[40,320,320]{2,1,0:T(8,128)} %refs_1_.17, bf16[320,256]{1,0:T(8,128)(2,1)S(1)} %get-tuple-element.32.refs_2_, ...), custom_call_target="tpu_custom_call" | custom-call | flops 629145600 | bytes 1916928 | tf_op jit(solution)/shard_map/galerkin/pallas_call | solution.py:208
  10.6 4.1 %collective-permute-start = (f32[4,144,128]{2,1,0:T(8,128)}, f32[4,144,128]{2,1,0:T(8,128)}, u32[]{:S(2)}, u32[]{:S(2)}) collective-permute-start(f32[4,144,128]{2,1,0:T(8,128)} %galerkin.9), channel_id=1, source_target_pairs={{0,16},{4,20},{8,24},{12,28},{16,0},{20,4},{24,8},{28,12},{1,17},{... | collective-permute-start | bytes 884744 | tf_op jit(solution)/shard_map/ppermute | solution.py:335
  14.6 0.0 copy-done
  14.6 0.0 copy-done.2
  14.6 0.3 fusion.18
  14.9 1.9 copy.14
  16.8 0.0 copy-start.9
  16.8 1.0 copy-done.9
  17.8 0.7 fusion.13
  18.5 0.6 broadcast_in_dim.26
  19.1 3.8 %all-to-all-start = ((f32[8,8,135]{2,1,0:T(8,128)}), f32[8,8,135]{2,1,0:T(8,128)S(1)}, u32[]{:S(2)}, u32[]{:S(2)}) async-start(f32[8,8,135]{2,1,0:T(8,128)} %broadcast_in_dim.26), calls=%async_computation | async-start | bytes 131072 | tf_op jit(solution)/shard_map/all_to_all | solution.py:312
  22.9 3.1 %galerkin.10 = f32[6,144,128]{2,1,0:T(8,128)} custom-call(s32[80]{0:T(128)S(1)} %get-tuple-element.56.fetch, s32[8]{0:T(128)S(1)} %get-tuple-element.31.count, f32[40,320,320]{2,1,0:T(8,128)} %refs_1_.17, f32[40,320,320]{2,1,0:T(8,128)} %refs_1_.17, bf16[320,256]{1,0:T(8,128)(2,1)S(1)} %get-tuple-element.32.refs_2_, ...), custom_call_target="tpu_custom_call" | custom-call | flops 943718400 | bytes 2875392 | tf_op jit(solution)/shard_map/galerkin/pallas_call | solution.py:208
  26.0 2.9 %collective-permute-start.1 = (f32[6,144,128]{2,1,0:T(8,128)}, f32[6,144,128]{2,1,0:T(8,128)S(1)}, u32[]{:S(2)}, u32[]{:S(2)}) collective-permute-start(f32[6,144,128]{2,1,0:T(8,128)} %galerkin.10), channel_id=1, source_target_pairs={{0,16},{4,20},{8,24},{12,28},{16,0},{20,4},{24,8},{28,12},{1,17},{... | collective-permute-start | bytes 1327112 | tf_op jit(solution)/shard_map/ppermute | solution.py:335
  28.9 6.0 %galerkin.11 = f32[10,144,128]{2,1,0:T(8,128)} custom-call(s32[80]{0:T(128)S(1)} %get-tuple-element.56.fetch, s32[8]{0:T(128)S(1)} %get-tuple-element.31.count, f32[40,320,320]{2,1,0:T(8,128)} %refs_1_.17, f32[40,320,320]{2,1,0:T(8,128)} %refs_1_.17, bf16[320,256]{1,0:T(8,128)(2,1)S(1)} %get-tuple-element.32.refs_2_, ...), custom_call_target="tpu_custom_call" | custom-call | flops 1572864000 | bytes 4792320 | tf_op jit(solution)/shard_map/galerkin/pallas_call | solution.py:208
  34.9 4.4 %collective-permute-start.2 = (f32[10,144,128]{2,1,0:T(8,128)}, f32[10,144,128]{2,1,0:T(8,128)S(1)}, u32[]{:S(2)}, u32[]{:S(2)}) collective-permute-start(f32[10,144,128]{2,1,0:T(8,128)} %galerkin.11), channel_id=1, source_target_pairs={{0,20},{4,16},{8,28},{12,24},{16,4},{20,0},{24,12},{28,8},{1,21},{... | collective-permute-start | bytes 2211848 | tf_op jit(solution)/shard_map/ppermute | solution.py:335
  39.3 4.7 %galerkin.12 = f32[10,144,128]{2,1,0:T(8,128)S(1)} custom-call(s32[80]{0:T(128)S(1)} %get-tuple-element.56.fetch, s32[8]{0:T(128)S(1)} %get-tuple-element.31.count, f32[40,320,320]{2,1,0:T(8,128)} %refs_1_.17, f32[40,320,320]{2,1,0:T(8,128)} %refs_1_.17, bf16[320,256]{1,0:T(8,128)(2,1)S(1)} %get-tuple-element.32.refs_2_, ...), custom_call_target="tpu_custom_call" | custom-call | flops 1572864000 | bytes 4792320 | tf_op jit(solution)/shard_map/galerkin/pallas_call | solution.py:208
  44.0 3.1 %collective-permute-start.3 = (f32[10,144,128]{2,1,0:T(8,128)S(1)}, f32[10,144,128]{2,1,0:T(8,128)S(1)}, u32[]{:S(2)}, u32[]{:S(2)}) collective-permute-start(f32[10,144,128]{2,1,0:T(8,128)S(1)} %galerkin.12), channel_id=1, source_target_pairs={{0,24},{4,28},{8,16},{12,20},{16,8},{20,12},{24,0},{28,4},{1,25},{... | collective-permute-start | bytes 2211848 | tf_op jit(solution)/shard_map/ppermute | solution.py:335
  47.1 0.0 all-to-all-done
  47.1 0.0 copy-done.6
  47.1 0.0 copy-done.8
  47.1 1.7 face_rows.1
  48.9 5.1 %galerkin.13 = f32[10,144,128]{2,1,0:T(8,128)} custom-call(s32[80]{0:T(128)S(1)} %get-tuple-element.56.fetch, s32[8]{0:T(128)S(1)} %get-tuple-element.31.count, f32[40,320,320]{2,1,0:T(8,128)} %refs_1_.17, f32[40,320,320]{2,1,0:T(8,128)} %refs_1_.17, bf16[320,256]{1,0:T(8,128)(2,1)S(1)} %get-tuple-element.32.refs_2_, ...), custom_call_target="tpu_custom_call" | custom-call | flops 1572864000 | bytes 4792320 | tf_op jit(solution)/shard_map/galerkin/pallas_call | solution.py:208
  54.0 2.6 %collective-permute-start.4 = (f32[10,144,128]{2,1,0:T(8,128)}, f32[10,144,128]{2,1,0:T(8,128)}, u32[]{:S(2)}, u32[]{:S(2)}) collective-permute-start(f32[10,144,128]{2,1,0:T(8,128)} %galerkin.13), channel_id=1, source_target_pairs={{0,8},{4,12},{8,0},{12,4},{16,24},{20,28},{24,16},{28,20},{1,9},{5... | collective-permute-start | bytes 2211848 | tf_op jit(solution)/shard_map/ppermute | solution.py:335
  56.6 0.7 broadcast_in_dim.29
  57.4 26.3 %all-to-all-start.1 = ((f32[4,64,135]{2,1,0:T(8,128)}), f32[4,64,135]{2,1,0:T(8,128)}, u32[]{:S(2)}, u32[]{:S(2)}) async-start(f32[4,64,135]{2,1,0:T(8,128)} %broadcast_in_dim.29), calls=%async_computation.1 | async-start | bytes 524288 | tf_op jit(solution)/shard_map/all_to_all | solution.py:312
  83.7 6.1 %all-to-all-done.1 = f32[4,64,135]{2,1,0:T(8,128)} async-done(((f32[4,64,135]{2,1,0:T(8,128)}), f32[4,64,135]{2,1,0:T(8,128)}, u32[]{:S(2)}, u32[]{:S(2)}) %all-to-all-start.1) | async-done | bytes 138272 | tf_op jit(solution)/shard_map/all_to_all | solution.py:312
  89.8 1.6 gather_fusion
  91.4 0.3 fusion.3.v_ref
  91.7 1.0 copy-done.4
  92.7 8.4 %products.1 = f32[40,256]{1,0:T(8,128)S(1)} custom-call(f32[40,320,320]{2,1,0:T(8,128)} %refs_1_.17, f32[40,320]{1,0:T(8,128)S(1)} %fusion.3.v_ref, f32[320,256]{1,0:T(8,128)S(1)} %copy-done.4), custom_call_target="tpu_custom_call" | custom-call | flops 16384000 | bytes 16384000 | tf_op jit(solution)/shard_map/products/pallas_call | solution.py:146
  101.0 0.9 fusion
  101.9 1.8 reshape.27
  103.7 1.9 copy.10
  105.6 4.0 %all-to-all-start.2 = ((f32[4,64,135]{2,1,0:T(8,128)}), f32[4,64,135]{2,1,0:T(8,128)}, u32[]{:S(2)}, u32[]{:S(2)}) async-start(f32[4,64,135]{2,1,0:T(8,128)} %copy.10), calls=%async_computation.2 | async-start | bytes 524288 | tf_op jit(solution)/shard_map/all_to_all | solution.py:356
  109.6 7.3 %galerkin.14 = f32[10,144,128]{2,1,0:T(8,128)} custom-call(s32[80]{0:T(128)S(1)} %get-tuple-element.56.fetch, s32[8]{0:T(128)S(1)} %get-tuple-element.31.count, f32[40,320,320]{2,1,0:T(8,128)} %refs_1_.17, f32[40,320,320]{2,1,0:T(8,128)} %refs_1_.17, bf16[320,256]{1,0:T(8,128)(2,1)S(1)} %get-tuple-element.32.refs_2_, ...), custom_call_target="tpu_custom_call" | custom-call | flops 1572864000 | bytes 4792320 | tf_op jit(solution)/shard_map/galerkin/pallas_call | solution.py:208
  116.9 0.0 all-to-all-done.2
  116.9 1.6 reduce_sum.18
  118.5 5.3 %all-to-all-start.3 = ((f32[8,8,135]{2,1,0:T(8,128)}), f32[8,8,135]{2,1,0:T(8,128)S(1)}, u32[]{:S(2)}, u32[]{:S(2)}) async-start(f32[8,8,135]{2,1,0:T(8,128)} %bitcast.8), calls=%async_computation.3 | async-start | bytes 131072 | tf_op jit(solution)/shard_map/all_to_all | solution.py:360
  123.8 8.1 %galerkin.15 = f32[10,144,128]{2,1,0:T(8,128)} custom-call(s32[80]{0:T(128)S(1)} %get-tuple-element.56.fetch, s32[8]{0:T(128)S(1)} %get-tuple-element.31.count, f32[40,320,320]{2,1,0:T(8,128)} %refs_1_.17, f32[40,320,320]{2,1,0:T(8,128)} %refs_1_.17, bf16[320,256]{1,0:T(8,128)(2,1)S(1)} %get-tuple-element.32.refs_2_, ...), custom_call_target="tpu_custom_call" | custom-call | flops 1572864000 | bytes 4792320 | tf_op jit(solution)/shard_map/galerkin/pallas_call | solution.py:208
  131.9 9.4 %galerkin.16 = f32[10,144,128]{2,1,0:T(8,128)} custom-call(s32[80]{0:T(128)S(1)} %get-tuple-element.56.fetch, s32[8]{0:T(128)S(1)} %get-tuple-element.31.count, f32[40,320,320]{2,1,0:T(8,128)} %refs_1_.17, f32[40,320,320]{2,1,0:T(8,128)} %refs_1_.17, bf16[320,256]{1,0:T(8,128)(2,1)S(1)} %get-tuple-element.32.refs_2_, ...), custom_call_target="tpu_custom_call" | custom-call | flops 1572864000 | bytes 4792320 | tf_op jit(solution)/shard_map/galerkin/pallas_call | solution.py:208
  141.4 0.0 collective-permute-done.refs_0_
  141.4 0.8 collective-permute-start.5
  142.1 0.0 collective-permute-done.1.refs_1_
  142.1 0.0 collective-permute-start.7
  142.1 0.0 collective-permute-done.3.refs_3_
  142.1 3.0 %collective-permute-start.6 = (f32[10,144,128]{2,1,0:T(8,128)}, f32[10,144,128]{2,1,0:T(8,128)}, u32[]{:S(2)}, u32[]{:S(2)}) collective-permute-start(f32[10,144,128]{2,1,0:T(8,128)} %galerkin.15), channel_id=1, source_target_pairs={{0,28},{4,24},{8,20},{12,16},{16,12},{20,8},{24,4},{28,0},{1,29},{... | collective-permute-start | bytes 2211848 | tf_op jit(solution)/shard_map/ppermute | solution.py:335
  145.2 4.7 %galerkin.17.refs_8_ = f32[10,144,128]{2,1,0:T(8,128)S(1)} custom-call(s32[80]{0:T(128)S(1)} %get-tuple-element.56.fetch, s32[8]{0:T(128)S(1)} %get-tuple-element.31.count, f32[40,320,320]{2,1,0:T(8,128)} %refs_1_.17, f32[40,320,320]{2,1,0:T(8,128)} %refs_1_.17, bf16[320,256]{1,0:T(8,128)(2,1)S(1)} %get-tuple-element.32.refs_2_, ...), custom_call_target="tpu_custom_call" | custom-call | flops 1572864000 | bytes 4792320 | tf_op jit(solution)/shard_map/galerkin/pallas_call | solution.py:208
  149.9 0.0 all-to-all-done.3
  149.9 1.9 fusion.11
  151.8 0.8 fusion.8
  152.6 0.0 collective-permute-done.2.refs_2_
  152.6 0.0 collective-permute-done.4.refs_4_
  152.6 20.6 %collective-permute-done.5.refs_5_ = f32[10,144,128]{2,1,0:T(8,128)} collective-permute-done((f32[10,144,128]{2,1,0:T(8,128)}, f32[10,144,128]{2,1,0:T(8,128)}, u32[]{:S(2)}, u32[]{:S(2)}) %collective-permute-start.5) | collective-permute-done | bytes 737312 | tf_op jit(solution)/shard_map/ppermute | solution.py:335
  173.3 18.7 %collective-permute-done.7.refs_7_ = f32[10,144,128]{2,1,0:T(8,128)} collective-permute-done((f32[10,144,128]{2,1,0:T(8,128)}, f32[10,144,128]{2,1,0:T(8,128)}, u32[]{:S(2)}, u32[]{:S(2)}) %collective-permute-start.7) | collective-permute-done | bytes 737312 | tf_op jit(solution)/shard_map/ppermute | solution.py:335
  191.9 0.0 collective-permute-done.6.refs_6_
  191.9 7.1 %unpack.1 = f32[135,135,80]{2,1,0:T(8,128)} custom-call(s32[1]{0:T(128)} %bitcast.1.me, f32[4,144,128]{2,1,0:T(8,128)} %collective-permute-done.refs_0_, f32[6,144,128]{2,1,0:T(8,128)S(1)} %collective-permute-done.1.refs_1_, f32[10,144,128]{2,1,0:T(8,128)S(1)} %collective-permute-done.2.refs_2_, f32[10,144,128]{2,1,0:T(8,128)S(1)} %collective-permute-done.3.refs_3_, ...), custom_call_target="tpu_custom_call" | custom-call | bytes 11796480 | tf_op jit(solution)/shard_map/unpack/pallas_call | solution.py:285
  (12 shorter events, 0.1 us)
Async XLA Ops:
  0.6 14.0 %copy-start = (f32[8,320]{1,0:T(8,128)S(1)}, f32[8,320]{1,0:T(8,128)}, u32[]{:S(2)}) copy-start(f32[8,320]{1,0:T(8,128)} %param.10) | copy-start | bytes 30724
  0.6 0.9 copy-start.1
  1.6 0.7 copy-start.5
  2.3 0.7 copy-start.7
  4.6 0.7 copy-start.3
  5.4 9.3 %copy-start.2 = (f32[320,135]{0,1:T(8,128)S(1)}, f32[320,135]{0,1:T(8,128)}, u32[]{:S(2)}) copy-start(f32[320,135]{0,1:T(8,128)} %param.9) | copy-start | bytes 518404
  10.6 130.8 %collective-permute-start = (f32[4,144,128]{2,1,0:T(8,128)}, f32[4,144,128]{2,1,0:T(8,128)}, u32[]{:S(2)}, u32[]{:S(2)}) collective-permute-start(f32[4,144,128]{2,1,0:T(8,128)} %galerkin.9), channel_id=1, source_target_pairs={{0,16},{4,20},{8,24},{12,28},{16,0},{20,4},{24,8},{28,12},{1,17},{... | collective-permute-start | bytes 884744 | tf_op jit(solution)/shard_map/ppermute | solution.py:335
  16.8 1.0 copy-start.9
  19.1 28.0 %all-to-all-start = ((f32[8,8,135]{2,1,0:T(8,128)}), f32[8,8,135]{2,1,0:T(8,128)S(1)}, u32[]{:S(2)}, u32[]{:S(2)}) async-start(f32[8,8,135]{2,1,0:T(8,128)} %broadcast_in_dim.26), calls=%async_computation | async-start | bytes 131072 | tf_op jit(solution)/shard_map/all_to_all | solution.py:312
  26.0 116.1 %collective-permute-start.1 = (f32[6,144,128]{2,1,0:T(8,128)}, f32[6,144,128]{2,1,0:T(8,128)S(1)}, u32[]{:S(2)}, u32[]{:S(2)}) collective-permute-start(f32[6,144,128]{2,1,0:T(8,128)} %galerkin.10), channel_id=1, source_target_pairs={{0,16},{4,20},{8,24},{12,28},{16,0},{20,4},{24,8},{28,12},{1,17},{... | collective-permute-start | bytes 1327112 | tf_op jit(solution)/shard_map/ppermute | solution.py:335
  34.9 12.2 %copy-start.6 = (s32[40,2]{0,1:T(2,128)S(1)}, s32[40,2]{0,1:T(2,128)}, u32[]{:S(2)}) copy-start(s32[40,2]{0,1:T(2,128)} %param.7) | copy-start | bytes 964
  34.9 12.2 %copy-start.8 = (s32[256]{0:T(256)S(1)}, s32[256]{0:T(256)}, u32[]{:S(2)}) copy-start(s32[256]{0:T(256)} %slots.3) | copy-start | bytes 3076
  34.9 117.7 %collective-permute-start.2 = (f32[10,144,128]{2,1,0:T(8,128)}, f32[10,144,128]{2,1,0:T(8,128)S(1)}, u32[]{:S(2)}, u32[]{:S(2)}) collective-permute-start(f32[10,144,128]{2,1,0:T(8,128)} %galerkin.11), channel_id=1, source_target_pairs={{0,20},{4,16},{8,28},{12,24},{16,4},{20,0},{24,12},{28,8},{1,21},{... | collective-permute-start | bytes 2211848 | tf_op jit(solution)/shard_map/ppermute | solution.py:335
  44.0 98.1 %collective-permute-start.3 = (f32[10,144,128]{2,1,0:T(8,128)S(1)}, f32[10,144,128]{2,1,0:T(8,128)S(1)}, u32[]{:S(2)}, u32[]{:S(2)}) collective-permute-start(f32[10,144,128]{2,1,0:T(8,128)S(1)} %galerkin.12), channel_id=1, source_target_pairs={{0,24},{4,28},{8,16},{12,20},{16,8},{20,12},{24,0},{28,4},{1,25},{... | collective-permute-start | bytes 2211848 | tf_op jit(solution)/shard_map/ppermute | solution.py:335
  54.0 98.6 %collective-permute-start.4 = (f32[10,144,128]{2,1,0:T(8,128)}, f32[10,144,128]{2,1,0:T(8,128)}, u32[]{:S(2)}, u32[]{:S(2)}) collective-permute-start(f32[10,144,128]{2,1,0:T(8,128)} %galerkin.13), channel_id=1, source_target_pairs={{0,8},{4,12},{8,0},{12,4},{16,24},{20,28},{24,16},{28,20},{1,9},{5... | collective-permute-start | bytes 2211848 | tf_op jit(solution)/shard_map/ppermute | solution.py:335
  57.4 32.4 %all-to-all-start.1 = ((f32[4,64,135]{2,1,0:T(8,128)}), f32[4,64,135]{2,1,0:T(8,128)}, u32[]{:S(2)}, u32[]{:S(2)}) async-start(f32[4,64,135]{2,1,0:T(8,128)} %broadcast_in_dim.29), calls=%async_computation.1 | async-start | bytes 524288 | tf_op jit(solution)/shard_map/all_to_all | solution.py:312
  91.7 1.0 copy-start.4
  105.6 11.3 %all-to-all-start.2 = ((f32[4,64,135]{2,1,0:T(8,128)}), f32[4,64,135]{2,1,0:T(8,128)}, u32[]{:S(2)}, u32[]{:S(2)}) async-start(f32[4,64,135]{2,1,0:T(8,128)} %copy.10), calls=%async_computation.2 | async-start | bytes 524288 | tf_op jit(solution)/shard_map/all_to_all | solution.py:356
  118.5 31.3 %all-to-all-start.3 = ((f32[8,8,135]{2,1,0:T(8,128)}), f32[8,8,135]{2,1,0:T(8,128)S(1)}, u32[]{:S(2)}, u32[]{:S(2)}) async-start(f32[8,8,135]{2,1,0:T(8,128)} %bitcast.8), calls=%async_computation.3 | async-start | bytes 131072 | tf_op jit(solution)/shard_map/all_to_all | solution.py:360
  141.4 31.9 %collective-permute-start.5 = (f32[10,144,128]{2,1,0:T(8,128)}, f32[10,144,128]{2,1,0:T(8,128)}, u32[]{:S(2)}, u32[]{:S(2)}) collective-permute-start(f32[10,144,128]{2,1,0:T(8,128)} %galerkin.14), channel_id=1, source_target_pairs={{0,12},{4,8},{8,4},{12,0},{16,28},{20,24},{24,20},{28,16},{1,13},{... | collective-permute-start | bytes 2211848 | tf_op jit(solution)/shard_map/ppermute | solution.py:335
  142.1 49.8 %collective-permute-start.7 = (f32[10,144,128]{2,1,0:T(8,128)}, f32[10,144,128]{2,1,0:T(8,128)}, u32[]{:S(2)}, u32[]{:S(2)}) collective-permute-start(f32[10,144,128]{2,1,0:T(8,128)} %galerkin.16), channel_id=1, source_target_pairs={{0,4},{4,0},{8,12},{12,8},{16,20},{20,16},{24,28},{28,24},{1,5},{5... | collective-permute-start | bytes 2211848 | tf_op jit(solution)/shard_map/ppermute | solution.py:335
  142.1 49.8 %collective-permute-start.6 = (f32[10,144,128]{2,1,0:T(8,128)}, f32[10,144,128]{2,1,0:T(8,128)}, u32[]{:S(2)}, u32[]{:S(2)}) collective-permute-start(f32[10,144,128]{2,1,0:T(8,128)} %galerkin.15), channel_id=1, source_target_pairs={{0,28},{4,24},{8,20},{12,16},{16,12},{20,8},{24,4},{28,0},{1,29},{... | collective-permute-start | bytes 2211848 | tf_op jit(solution)/shard_map/ppermute | solution.py:335

commit v4 on v3

--- a/solution.py
+++ b/solution.py
@@ -13,6 +13,7 @@
 LANES = 128
 PAIR = 2
 EXCHANGE = 4
+WHOLE_VMEM = 67043328
 F32 = jnp.float32
 BF16 = jnp.bfloat16
 
@@ -31,7 +32,6 @@
 
 def send_plan(wide, cap):
     offsets = sorted(range(1, wide), key=lambda k: (-k.bit_length(), k))
-    offsets = [k for k in offsets if 1 < k < wide - 1] + [wide - 1, 1]
     first = min(2 * PAIR, cap)
     plan = [(offsets[0], 0, first)]
     if cap > first:
@@ -39,8 +39,17 @@
     return plan + [(k, 0, cap) for k in offsets[1:]]
 
 
-def place_kernel(owner_rows, cap, elems, slots, me, pt, fetch, count, ph, pl_, th, tl, p32, wide_pt):
+def place_kernel(
+    owner_rows, cap, elems_in, slots_in, me, pt_in, fetch, count, ph, pl_, th, tl, p32, elems, slots, pt, wide_pt, sems
+):
     faces, wide = elems.shape[1], count.shape[0]
+    sources = ((elems_in, elems), (slots_in, slots), (pt_in, pt))
+    copies = [pltpu.make_async_copy(a, b, sems.at[i]) for i, (a, b) in enumerate(sources)]
+    for copy in copies:
+        copy.start()
+    wide_pt[...] = jnp.zeros_like(wide_pt)
+    for copy in copies:
+        copy.wait()
 
     def put(f, c):
         owner = lax.div(slots[elems[0, f]], owner_rows)
@@ -65,7 +74,6 @@
 
     lax.fori_loop(0, wide, fill, 0)
     rows, fine = th.shape
-    wide_pt[...] = jnp.zeros_like(wide_pt)
     wide_pt[: pt.shape[0], :fine] = pt[...]
     th[...], tl[...] = split(wide_pt[:rows, :fine])
     p32[...] = wide_pt[...].T[:fine]
@@ -91,6 +99,7 @@
 
 SMEM = pl.BlockSpec(memory_space=pltpu.SMEM)
 VMEM = pl.BlockSpec(memory_space=pltpu.VMEM)
+HBM = pl.BlockSpec(memory_space=pltpu.HBM)
 
 
 def ints(n):
@@ -113,10 +122,16 @@
             halves(rows, fine),
             jax.ShapeDtypeStruct((fine, 2 * LANES), F32),
         ),
-        in_specs=[SMEM, SMEM, SMEM, VMEM],
+        in_specs=[HBM, HBM, SMEM, HBM],
         out_specs=(SMEM, SMEM, VMEM, VMEM, VMEM, VMEM, VMEM),
-        scratch_shapes=[pltpu.VMEM((2 * LANES, round_up(fine, LANES)), F32)],
-        compiler_params=pltpu.CompilerParams(vmem_limit_bytes=8 << 20),
+        scratch_shapes=[
+            pltpu.SMEM(face_elems.shape[::-1], jnp.int32),
+            pltpu.SMEM(coarse_slot.shape, jnp.int32),
+            pltpu.VMEM((coarse, fine), F32),
+            pltpu.VMEM((2 * LANES, round_up(fine, LANES)), F32),
+            pltpu.SemaphoreType.DMA((3,)),
+        ],
+        compiler_params=pltpu.CompilerParams(vmem_limit_bytes=WHOLE_VMEM),
         name="place_faces",
     )(face_elems.T, coarse_slot, me, prolong.T)
 
@@ -131,6 +146,55 @@
         compiler_params=pltpu.CompilerParams(vmem_limit_bytes=8 << 20),
         name="face_rows",
     )(face_elems.T, coarse_slot)
+
+
+def apply_blocks(blocks, vectors):
+    coarse = blocks.shape[0]
+    lane = lax.broadcasted_iota(jnp.int32, vectors.shape, 1)
+
+    def add(n, out):
+        value = jnp.sum(blocks[n] * vectors, axis=1, keepdims=True)
+        return jnp.where(lane == n, value, out)
+
+    return lax.fori_loop(0, coarse, add, jnp.zeros_like(vectors), unroll=9)
+
+
+def sweep_one_kernel(residual, p32, blocks, rhs, sweep):
+    rhs[...] = jnp.dot(residual[...], p32[...], precision=PRECISE, preferred_element_type=F32)
+    sweep[...] = DAMPING * apply_blocks(blocks, rhs[:, : blocks.shape[0]])
+
+
+def sweep_one_of(residual, p32, blocks):
+    rows, coarse = residual.shape[0], blocks.shape[0]
+    return pl.pallas_call(
+        sweep_one_kernel,
+        out_shape=(
+            jax.ShapeDtypeStruct((rows, p32.shape[1]), F32),
+            jax.ShapeDtypeStruct((rows, coarse), F32),
+        ),
+        in_specs=[VMEM] * 3,
+        out_specs=(VMEM, VMEM),
+        compiler_params=pltpu.CompilerParams(vmem_limit_bytes=8 << 20),
+        name="sweep_one",
+    )(residual, p32, blocks)
+
+
+def sweep_two_kernel(sums, rhs, sweep, pt, blocks, out):
+    coarse = blocks.shape[0]
+    update = (1.0 - DAMPING) * rhs[:, :coarse] - jnp.sum(sums[...], axis=0)
+    last = sweep[...] + DAMPING * apply_blocks(blocks, update)
+    out[...] = jnp.dot(last, pt[...], precision=PRECISE, preferred_element_type=F32)
+
+
+def sweep_two_of(sums, rhs, sweep, pt, blocks):
+    return pl.pallas_call(
+        sweep_two_kernel,
+        out_shape=jax.ShapeDtypeStruct((rhs.shape[0], pt.shape[1]), F32),
+        in_specs=[VMEM] * 5,
+        out_specs=VMEM,
+        compiler_params=pltpu.CompilerParams(vmem_limit_bytes=8 << 20),
+        name="sweep_two",
+    )(sums, rhs, sweep, pt, blocks)
 
 
 def product_kernel(a_ref, v_ref, p_ref, o_ref):
@@ -199,7 +263,7 @@
             o_ref[j, rows:, :] = jnp.where(last, corner, turned)
 
 
-def galerkin(face_blocks, operands, fetch, count, cap, piece):
+def galerkin(face_blocks, operands, fetch, count, cap, piece, grant=50 << 20):
     at, first, ranks = piece
     fine = face_blocks.shape[1]
     ph, _, th, _ = operands
@@ -215,7 +279,7 @@
             + [VMEM] * 4,
             out_specs=pl.BlockSpec((PAIR, rows + 8, LANES), lambda s, fetch, count: (s, 0, 0)),
         ),
-        compiler_params=pltpu.CompilerParams(vmem_limit_bytes=50 << 20),
+        compiler_params=pltpu.CompilerParams(vmem_limit_bytes=grant),
         cost_estimate=pl.CostEstimate(
             flops=ranks * 6 * fine * fine * width,
             bytes_accessed=ranks * 4 * (fine * fine + rows * LANES),
@@ -329,14 +393,15 @@
     )
     parts = []
     for i, piece in enumerate(plan):
-        block = galerkin(face_blocks, operands, fetch, count, slots, piece)
+        grant = 50 << 20 if i else WHOLE_VMEM
+        block = galerkin(face_blocks, operands, fetch, count, slots, piece, grant)
         fetch = after(block, fetch)
         pairs = [(w, w ^ piece[0]) for w in range(wide)]
         parts.append(lax.ppermute(block, "wide", pairs))
         if i == 0:
             fine_residual, face_elems = after(block, fine_residual, face_elems)
-            rhs = jnp.dot(fine_residual, prolong, precision=PRECISE)
-            sweep_one = DAMPING * jnp.einsum("snm,sm->sn", block_inverse, rhs, precision=PRECISE)
+            inverse = jnp.transpose(block_inverse, (1, 0, 2))
+            rhs, sweep_one = sweep_one_of(fine_residual, p32, inverse)
             fetch = after(sweep_one, fetch)
             iterate = everyone(sweep_one, "wide", wide)
         if i == EXCHANGE - 1:
@@ -344,7 +409,7 @@
             iterate = everyone(iterate.reshape(wide * dev_rows, coarse), "narrow", narrow)
             row, col = face_rows(face_elems, coarse_slot, dev_rows, narrow, wide)
             fetch = after(row, fetch)
-        if i == EXCHANGE:
+        if i == EXCHANGE + 1:
             iterate = after(block, iterate).reshape(-1, coarse)
             vectors = jnp.dot(jnp.take(iterate, col, axis=0), prolong.T, precision=PRECISE)
             results = products(face_blocks, vectors, p32)
@@ -354,18 +419,14 @@
             sums = sums.reshape(narrow, wide * dev_rows, coarse)
             fetch = after(sums, fetch)
             sums = lax.all_to_all(sums, "narrow", split_axis=0, concat_axis=0, tiled=True)
-        if i == EXCHANGE + 1:
+        if i == len(plan) - 1:
             sums = jnp.sum(after(block, sums), axis=0).reshape(wide, dev_rows, coarse)
             fetch = after(sums, fetch)
             sums = lax.all_to_all(sums, "wide", split_axis=0, concat_axis=0, tiled=True)
     parts.append(galerkin(face_blocks, operands, fetch, count, slots, (0, 0, slots)))
     pieces = [*plan, (0, 0, slots)]
-    coupling = jnp.sum(after(parts[-1], sums), axis=0)
-    update = (1.0 - DAMPING) * rhs - coupling
-    sweep_two = sweep_one + DAMPING * jnp.einsum(
-        "snm,sm->sn", block_inverse, update, precision=PRECISE
-    )
-    correction = jnp.dot(sweep_two, prolong.T, precision=PRECISE)
+    sums = after(parts[-1], sums)
+    correction = sweep_two_of(sums, rhs, sweep_one, prolong.T, inverse)
     owned = unpack(parts, pieces, cap, coarse, wide)
     return (correction, owned)
 

time: 202 us -> 178 us (0.88)
  waiting for transfers between devices: 45.4 us -> 25.1 us
  Pallas kernels: 72.5 us -> 76.9 us
  matrix products: 4.89 us -> 1.22 us
    ppermute x8, waiting for transfers between devices: 39.3 us -> 0.02 us  [local(): parts.append(lax.ppermute(block, 'wide', pairs))]
    ppermute x8, starting transfers between devices: 20.9 us -> 43.8 us  [local(): parts.append(lax.ppermute(block, 'wide', pairs))]
    all_to_all x2, starting transfers between devices: 30.1 us -> 7.85 us  [everyone(): lax.all_to_all(jnp.broadcast_to(x[None], (size, *x.shape)), axis, split_a...]
    all_to_all x1, waiting for transfers between devices: 0.01 us -> 13 us  [local(): sums = lax.all_to_all(sums, 'wide', split_axis=0, concat_axis=0, tiled=True)]
    all_to_all x1, waiting for transfers between devices: 0.01 us -> 6 us  [local(): lax.all_to_all(sums, 'narrow', split_axis=0, concat_axis=0, tiled=True)]
    pallas_call x0 -> x2, Pallas kernels: none -> 3.76 us  [the longest x1 2.17 us: sweep_two_of(): pl.pallas_call(sweep_two_kernel, out_shape=jax.ShapeDtypeStruct((rhs.shap...]
    dot_general x4 -> x0, matrix products: 3.67 us -> none  [the longest x1 1.9 us: local(): jnp.einsum('snm,sm->sn', block_inverse, update, precision=PRECISE)]
    unnamed x21 -> x44, local copies, waits for them, and re-layouts: 6.86 us -> 9.03 us
  transfers between devices with their start and end apart: 12 -> 12, of which waited for: 3 -> 3; matrix products, arithmetic and copies ran while one was open for 8% -> 4% of each run, Pallas kernels for 29% -> 35%
where the time goes in v4:
time: 178 us; the launch traced here: 177 us
  Pallas kernels  76.9 us (43%)
  starting transfers between devices  58.5 us (33%)
  waiting for transfers between devices  25.1 us (14%)
  local copies, waits for them, and re-layouts  13.9 us (8%)
    pallas_call x9, Pallas kernels, galerkin(): pl.pallas_call(functools.partial(galerkin_kernel, at, first), out_shape=j...  53.7 us
    ppermute x8, starting transfers between devices, local(): parts.append(lax.ppermute(block, 'wide', pairs))  43.8 us
    all_to_all x1, waiting for transfers between devices, local(): sums = lax.all_to_all(sums, 'wide', split_axis=0, concat_axis=0, tiled=True)  13 us
    unnamed x44, local copies, waits for them, and re-layouts  9.03 us
    pallas_call x1, Pallas kernels, products(): pl.pallas_call(product_kernel, out_shape=jax.ShapeDtypeStruct((faces, wid...  8.22 us
    all_to_all x2, starting transfers between devices, everyone(): lax.all_to_all(jnp.broadcast_to(x[None], (size, *x.shape)), axis, split_a...  7.85 us
    pallas_call x1, Pallas kernels, unpack(): pl.pallas_call(functools.partial(unpack_kernel, pieces, cap, coarse), out...  7.16 us
    all_to_all x2, waiting for transfers between devices, everyone(): lax.all_to_all(jnp.broadcast_to(x[None], (size, *x.shape)), axis, split_a...  6.05 us
  transfers between devices with their start and end apart: 12, of which 3 were waited for; matrix products, arithmetic and copies ran while one was open for 4% of the time, Pallas kernels for 35%

profile of v4, /device:TPU:0, one launch (start us, length us, event | category | flops | bytes accessed | tf_op | source)
XLA Modules:
  0.0 177.2 jit_solution(3009071508576051522)
XLA Ops:
  0.6 2.3 %place_faces.1 = (s32[80]{0:T(128)}, s32[8]{0:T(128)}, bf16[320,256]{1,0:T(8,128)(2,1)}, bf16[320,256]{1,0:T(8,128)(2,1)}, bf16[136,320]{1,0:T(8,128)(2,1)}, /*i...) custom-call(s32[2,40]{1,0:T(2,128)} %bitcast.16, s32[256]{0:T(256)} %slots.1, s32[1]{0:T(128)} %bitcast.1.me, f32[135,320]{1,0:T(8,128)} %bitcast.14), custom_call_target="tpu_custom_call" | custom-call | tf_op jit(solution)/shard_map/place_faces/pallas_call | solution.py:114
  2.9 5.5 %galerkin.9 = f32[4,144,128]{2,1,0:T(8,128)} custom-call(s32[80]{0:T(128)} %get-tuple-element.59.fetch, s32[8]{0:T(128)} %get-tuple-element.33.count, f32[40,320,320]{2,1,0:T(8,128)} %refs_1_.17, f32[40,320,320]{2,1,0:T(8,128)} %refs_1_.17, bf16[320,256]{1,0:T(8,128)(2,1)} %get-tuple-element.34.refs_2_, bf16[320,256]{1,0:T(8,128)(2,1)} %get-tuple-element.35.refs_3_, ...), custom_call_target="tpu_custom_call" | custom-call | flops 629145600 | bytes 1916928 | tf_op jit(solution)/shard_map/galerkin/pallas_call | solution.py:272
  8.4 4.1 %collective-permute-start = (f32[4,144,128]{2,1,0:T(8,128)}, f32[4,144,128]{2,1,0:T(8,128)}, u32[]{:S(2)}, u32[]{:S(2)}) collective-permute-start(f32[4,144,128]{2,1,0:T(8,128)} %galerkin.9), channel_id=1, source_target_pairs={{0,16},{4,20},{8,24},{12,28},{16,0},{20,4},{24,8},{28,12},{1,17},{... | collective-permute-start | bytes 884744 | tf_op jit(solution)/shard_map/ppermute | solution.py:400
  12.5 1.2 copy-done.8
  13.7 1.0 copy-done.11
  14.7 0.7 copy-done.19
  15.4 1.6 sweep_one.1
  17.0 0.6 broadcast_in_dim.26
  17.7 3.8 %all-to-all-start = ((f32[8,8,135]{2,1,0:T(8,128)}), f32[8,8,135]{2,1,0:T(8,128)S(1)}, u32[]{:S(2)}, u32[]{:S(2)}) async-start(f32[8,8,135]{2,1,0:T(8,128)} %broadcast_in_dim.26), calls=%async_computation | async-start | bytes 131072 | tf_op jit(solution)/shard_map/all_to_all | solution.py:376
  21.5 0.9 copy-done
  22.4 0.9 copy-done.2
  23.3 0.9 copy-done.4
  24.2 0.9 copy-done.6
  25.1 0.7 copy-done.15
  25.7 0.7 copy-done.17
  26.4 3.1 %galerkin.10 = f32[6,144,128]{2,1,0:T(8,128)} custom-call(s32[80]{0:T(128)S(1)} %copy-done.15, s32[8]{0:T(128)S(1)} %copy-done.17, f32[40,320,320]{2,1,0:T(8,128)} %refs_1_.17, f32[40,320,320]{2,1,0:T(8,128)} %refs_1_.17, bf16[320,256]{1,0:T(8,128)(2,1)S(1)} %copy-done, bf16[320,256]{1,0:T(8,128)(2,1)S(1)} %copy-done.2, bf16[136,320]{1,0:T(8,128)(2,1)S(1)} %copy-done.4, ...), custom_call_target="tpu_custom_call" | custom-call | flops 943718400 | bytes 2875392 | tf_op jit(solution)/shard_map/galerkin/pallas_call | solution.py:272
  29.5 2.9 %collective-permute-start.1 = (f32[6,144,128]{2,1,0:T(8,128)}, f32[6,144,128]{2,1,0:T(8,128)}, u32[]{:S(2)}, u32[]{:S(2)}) collective-permute-start(f32[6,144,128]{2,1,0:T(8,128)} %galerkin.10), channel_id=1, source_target_pairs={{0,16},{4,20},{8,24},{12,28},{16,0},{20,4},{24,8},{28,12},{1,17},{... | collective-permute-start | bytes 1327112 | tf_op jit(solution)/shard_map/ppermute | solution.py:400
  32.4 6.0 %galerkin.11 = f32[10,144,128]{2,1,0:T(8,128)} custom-call(s32[80]{0:T(128)S(1)} %copy-done.15, s32[8]{0:T(128)S(1)} %copy-done.17, f32[40,320,320]{2,1,0:T(8,128)} %refs_1_.17, f32[40,320,320]{2,1,0:T(8,128)} %refs_1_.17, bf16[320,256]{1,0:T(8,128)(2,1)S(1)} %copy-done, bf16[320,256]{1,0:T(8,128)(2,1)S(1)} %copy-done.2, bf16[136,320]{1,0:T(8,128)(2,1)S(1)} %copy-done.4, ...), custom_call_target="tpu_custom_call" | custom-call | flops 1572864000 | bytes 4792320 | tf_op jit(solution)/shard_map/galerkin/pallas_call | solution.py:272
  38.4 0.0 copy-start.3
  38.4 0.0 copy-start.5
  38.4 0.0 copy-start.7
  38.4 0.0 copy-start.16
  38.5 4.5 %collective-permute-start.2 = (f32[10,144,128]{2,1,0:T(8,128)}, f32[10,144,128]{2,1,0:T(8,128)S(1)}, u32[]{:S(2)}, u32[]{:S(2)}) collective-permute-start(f32[10,144,128]{2,1,0:T(8,128)} %galerkin.11), channel_id=1, source_target_pairs={{0,20},{4,16},{8,28},{12,24},{16,4},{20,0},{24,12},{28,8},{1,21},{... | collective-permute-start | bytes 2211848 | tf_op jit(solution)/shard_map/ppermute | solution.py:400
  43.0 4.7 %galerkin.12 = f32[10,144,128]{2,1,0:T(8,128)S(1)} custom-call(s32[80]{0:T(128)S(1)} %copy-done.15, s32[8]{0:T(128)S(1)} %copy-done.17, f32[40,320,320]{2,1,0:T(8,128)} %refs_1_.17, f32[40,320,320]{2,1,0:T(8,128)} %refs_1_.17, bf16[320,256]{1,0:T(8,128)(2,1)S(1)} %copy-done, bf16[320,256]{1,0:T(8,128)(2,1)S(1)} %copy-done.2, bf16[136,320]{1,0:T(8,128)(2,1)S(1)} %copy-done.4, ...), custom_call_target="tpu_custom_call" | custom-call | flops 1572864000 | bytes 4792320 | tf_op jit(solution)/shard_map/galerkin/pallas_call | solution.py:272
  47.7 3.1 %collective-permute-start.3 = (f32[10,144,128]{2,1,0:T(8,128)S(1)}, f32[10,144,128]{2,1,0:T(8,128)S(1)}, u32[]{:S(2)}, u32[]{:S(2)}) collective-permute-start(f32[10,144,128]{2,1,0:T(8,128)S(1)} %galerkin.12), channel_id=1, source_target_pairs={{0,24},{4,28},{8,16},{12,20},{16,8},{20,12},{24,0},{28,4},{1,25},{... | collective-permute-start | bytes 2211848 | tf_op jit(solution)/shard_map/ppermute | solution.py:400
  50.7 0.0 all-to-all-done
  50.7 0.0 copy-done.21
  50.7 1.7 face_rows.1
  52.6 8.0 %galerkin.13 = f32[10,144,128]{2,1,0:T(8,128)} custom-call(s32[80]{0:T(128)S(1)} %copy-done.16, s32[8]{0:T(128)S(1)} %copy-done.18, f32[40,320,320]{2,1,0:T(8,128)} %refs_1_.17, f32[40,320,320]{2,1,0:T(8,128)} %refs_1_.17, bf16[320,256]{1,0:T(8,128)(2,1)S(1)} %copy-done.1, bf16[320,256]{1,0:T(8,128)(2,1)S(1)} %copy-done.3, bf16[136,320]{1,0:T(8,128)(2,1)S(1)} %copy-done.5, ...), custom_call_target="tpu_custom_call" | custom-call | flops 1572864000 | bytes 4792320 | tf_op jit(solution)/shard_map/galerkin/pallas_call | solution.py:272
  60.6 5.1 %galerkin.14 = f32[10,144,128]{2,1,0:T(8,128)} custom-call(s32[80]{0:T(128)S(1)} %copy-done.16, s32[8]{0:T(128)S(1)} %copy-done.18, f32[40,320,320]{2,1,0:T(8,128)} %refs_1_.17, f32[40,320,320]{2,1,0:T(8,128)} %refs_1_.17, bf16[320,256]{1,0:T(8,128)(2,1)S(1)} %copy-done.1, bf16[320,256]{1,0:T(8,128)(2,1)S(1)} %copy-done.3, bf16[136,320]{1,0:T(8,128)(2,1)S(1)} %copy-done.5, ...), custom_call_target="tpu_custom_call" | custom-call | flops 1572864000 | bytes 4792320 | tf_op jit(solution)/shard_map/galerkin/pallas_call | solution.py:272
  65.8 1.8 %collective-permute-start.5 = (f32[10,144,128]{2,1,0:T(8,128)}, f32[10,144,128]{2,1,0:T(8,128)}, u32[]{:S(2)}, u32[]{:S(2)}) collective-permute-start(f32[10,144,128]{2,1,0:T(8,128)} %galerkin.14), channel_id=1, source_target_pairs={{0,8},{4,12},{8,0},{12,4},{16,24},{20,28},{24,16},{28,20},{1,9},{5... | collective-permute-start | bytes 2211848 | tf_op jit(solution)/shard_map/ppermute | solution.py:400
  67.6 0.7 broadcast_in_dim.29
  68.3 4.0 %all-to-all-start.1 = ((f32[4,64,135]{2,1,0:T(8,128)}), f32[4,64,135]{2,1,0:T(8,128)}, u32[]{:S(2)}, u32[]{:S(2)}) async-start(f32[4,64,135]{2,1,0:T(8,128)} %broadcast_in_dim.29), calls=%async_computation.1 | async-start | bytes 524288 | tf_op jit(solution)/shard_map/all_to_all | solution.py:376
  72.3 6.1 %all-to-all-done.1 = f32[4,64,135]{2,1,0:T(8,128)} async-done(((f32[4,64,135]{2,1,0:T(8,128)}), f32[4,64,135]{2,1,0:T(8,128)}, u32[]{:S(2)}, u32[]{:S(2)}) %all-to-all-start.1) | async-done | bytes 138272 | tf_op jit(solution)/shard_map/all_to_all | solution.py:376
  78.4 1.6 gather_fusion
  80.0 0.3 fusion.3.v_ref
  80.3 8.2 %products.1 = f32[40,256]{1,0:T(8,128)S(1)} custom-call(f32[40,320,320]{2,1,0:T(8,128)} %refs_1_.17, f32[40,320]{1,0:T(8,128)S(1)} %fusion.3.v_ref, f32[320,256]{1,0:T(8,128)S(1)} %copy-done.12), custom_call_target="tpu_custom_call" | custom-call | flops 16384000 | bytes 16384000 | tf_op jit(solution)/shard_map/products/pallas_call | solution.py:210
  88.5 0.9 fusion
  89.4 1.1 reshape.27
  90.5 7.3 %galerkin.15 = f32[10,144,128]{2,1,0:T(8,128)} custom-call(s32[80]{0:T(128)S(1)} %copy-done.16, s32[8]{0:T(128)S(1)} %copy-done.18, f32[40,320,320]{2,1,0:T(8,128)} %refs_1_.17, f32[40,320,320]{2,1,0:T(8,128)} %refs_1_.17, bf16[320,256]{1,0:T(8,128)(2,1)S(1)} %copy-done.1, bf16[320,256]{1,0:T(8,128)(2,1)S(1)} %copy-done.3, bf16[136,320]{1,0:T(8,128)(2,1)S(1)} %copy-done.5, ...), custom_call_target="tpu_custom_call" | custom-call | flops 1572864000 | bytes 4792320 | tf_op jit(solution)/shard_map/galerkin/pallas_call | solution.py:272
  97.8 9.4 %galerkin.16 = f32[10,144,128]{2,1,0:T(8,128)} custom-call(s32[80]{0:T(128)S(1)} %copy-done.16, s32[8]{0:T(128)S(1)} %copy-done.18, f32[40,320,320]{2,1,0:T(8,128)} %refs_1_.17, f32[40,320,320]{2,1,0:T(8,128)} %refs_1_.17, bf16[320,256]{1,0:T(8,128)(2,1)S(1)} %copy-done.1, bf16[320,256]{1,0:T(8,128)(2,1)S(1)} %copy-done.3, bf16[136,320]{1,0:T(8,128)(2,1)S(1)} %copy-done.5, ...), custom_call_target="tpu_custom_call" | custom-call | flops 1572864000 | bytes 4792320 | tf_op jit(solution)/shard_map/galerkin/pallas_call | solution.py:272
  107.2 0.0 collective-permute-done.refs_0_
  107.2 0.0 collective-permute-start.4
  107.2 0.0 collective-permute-done.1.refs_1_
  107.2 0.1 collective-permute-start.7
  107.3 0.0 collective-permute-done.3.refs_3_
  107.3 27.3 %collective-permute-start.6 = (f32[10,144,128]{2,1,0:T(8,128)}, f32[10,144,128]{2,1,0:T(8,128)}, u32[]{:S(2)}, u32[]{:S(2)}) collective-permute-start(f32[10,144,128]{2,1,0:T(8,128)} %galerkin.15), channel_id=1, source_target_pairs={{0,12},{4,8},{8,4},{12,0},{16,28},{20,24},{24,20},{28,16},{1,13},{... | collective-permute-start | bytes 2211848 | tf_op jit(solution)/shard_map/ppermute | solution.py:400
  134.6 0.9 copy.8
  135.5 3.5 %all-to-all-start.2 = ((f32[4,64,135]{2,1,0:T(8,128)}), f32[4,64,135]{2,1,0:T(8,128)S(1)}, u32[]{:S(2)}, u32[]{:S(2)}) async-start(f32[4,64,135]{2,1,0:T(8,128)} %copy.8), calls=%async_computation.2 | async-start | bytes 524288 | tf_op jit(solution)/shard_map/all_to_all | solution.py:421
  139.0 6.0 %all-to-all-done.2 = f32[4,64,135]{2,1,0:T(8,128)S(1)} async-done(((f32[4,64,135]{2,1,0:T(8,128)}), f32[4,64,135]{2,1,0:T(8,128)S(1)}, u32[]{:S(2)}, u32[]{:S(2)}) %all-to-all-start.2) | async-done | bytes 138272 | tf_op jit(solution)/shard_map/all_to_all | solution.py:421
  145.0 0.6 reduce_sum.9
  145.7 0.0 copy-done.13
  145.7 3.3 %all-to-all-start.3 = ((f32[8,8,135]{2,1,0:T(8,128)}), f32[8,8,135]{2,1,0:T(8,128)S(1)}, u32[]{:S(2)}, u32[]{:S(2)}) async-start(f32[8,8,135]{2,1,0:T(8,128)} %bitcast.7), calls=%async_computation.3 | async-start | bytes 131072 | tf_op jit(solution)/shard_map/all_to_all | solution.py:425
  149.0 0.0 copy-start.9
  149.0 4.7 %galerkin.17.refs_8_ = f32[10,144,128]{2,1,0:T(8,128)S(1)} custom-call(s32[80]{0:T(128)S(1)} %copy-done.16, s32[8]{0:T(128)S(1)} %copy-done.18, f32[40,320,320]{2,1,0:T(8,128)} %refs_1_.17, f32[40,320,320]{2,1,0:T(8,128)} %refs_1_.17, bf16[320,256]{1,0:T(8,128)(2,1)S(1)} %copy-done.1, bf16[320,256]{1,0:T(8,128)(2,1)S(1)} %copy-done.3, ...), custom_call_target="tpu_custom_call" | custom-call | flops 1572864000 | bytes 4792320 | tf_op jit(solution)/shard_map/galerkin/pallas_call | solution.py:272
  153.7 13.0 %all-to-all-done.3.sums = f32[8,8,135]{2,1,0:T(8,128)S(1)} async-done(((f32[8,8,135]{2,1,0:T(8,128)}), f32[8,8,135]{2,1,0:T(8,128)S(1)}, u32[]{:S(2)}, u32[]{:S(2)}) %all-to-all-start.3) | async-done | bytes 34592 | tf_op jit(solution)/shard_map/all_to_all | solution.py:425
  166.7 2.2 %sweep_two.1 = f32[8,320]{1,0:T(8,128)} custom-call(f32[8,8,135]{2,1,0:T(8,128)S(1)} %all-to-all-done.3.sums, f32[8,256]{1,0:T(8,128)S(1)} %get-tuple-element.61.rhs, f32[8,135]{1,0:T(8,128)S(1)} %get-tuple-element.40.sweep, f32[135,320]{1,0:T(8,128)S(1)} %bitcast.15, f32[135,8,135]{2,1,0:T(8,128)S(1)} %bitcast.13), custom_call_target="tpu_custom_call" | custom-call | tf_op jit(solution)/shard_map/sweep_two/pallas_call | solution.py:190
  168.9 0.0 collective-permute-done.2.refs_2_
  168.9 0.0 collective-permute-done.5.refs_5_
  168.9 0.0 collective-permute-done.4.refs_4_
  168.9 0.0 collective-permute-done.7.refs_7_
  168.9 0.0 collective-permute-done.6.refs_6_
  168.9 1.1 copy-done.14
  170.1 7.2 %unpack.1 = f32[135,135,80]{2,1,0:T(8,128)} custom-call(s32[1]{0:T(128)} %bitcast.1.me, f32[4,144,128]{2,1,0:T(8,128)} %collective-permute-done.refs_0_, f32[6,144,128]{2,1,0:T(8,128)} %collective-permute-done.1.refs_1_, f32[10,144,128]{2,1,0:T(8,128)S(1)} %collective-permute-done.2.refs_2_, f32[10,144,128]{2,1,0:T(8,128)S(1)} %copy-done.14, ...), custom_call_target="tpu_custom_call" | custom-call | bytes 11796480 | tf_op jit(solution)/shard_map/unpack/pallas_call | solution.py:349
  (30 shorter events, 0.1 us)
Async XLA Ops:
  8.4 98.7 %collective-permute-start = (f32[4,144,128]{2,1,0:T(8,128)}, f32[4,144,128]{2,1,0:T(8,128)}, u32[]{:S(2)}, u32[]{:S(2)}) collective-permute-start(f32[4,144,128]{2,1,0:T(8,128)} %galerkin.9), channel_id=1, source_target_pairs={{0,16},{4,20},{8,24},{12,28},{16,0},{20,4},{24,8},{28,12},{1,17},{... | collective-permute-start | bytes 884744 | tf_op jit(solution)/shard_map/ppermute | solution.py:400
  12.5 1.2 copy-start.8
  13.7 1.0 copy-start.11
  14.7 0.7 copy-start.19
  17.7 33.1 %all-to-all-start = ((f32[8,8,135]{2,1,0:T(8,128)}), f32[8,8,135]{2,1,0:T(8,128)S(1)}, u32[]{:S(2)}, u32[]{:S(2)}) async-start(f32[8,8,135]{2,1,0:T(8,128)} %broadcast_in_dim.26), calls=%async_computation | async-start | bytes 131072 | tf_op jit(solution)/shard_map/all_to_all | solution.py:376
  21.5 0.9 copy-start
  22.4 0.9 copy-start.2
  23.3 0.9 copy-start.4
  24.2 0.9 copy-start.6
  25.1 0.7 copy-start.15
  25.7 0.7 copy-start.17
  29.5 77.7 %collective-permute-start.1 = (f32[6,144,128]{2,1,0:T(8,128)}, f32[6,144,128]{2,1,0:T(8,128)}, u32[]{:S(2)}, u32[]{:S(2)}) collective-permute-start(f32[6,144,128]{2,1,0:T(8,128)} %galerkin.10), channel_id=1, source_target_pairs={{0,16},{4,20},{8,24},{12,28},{16,0},{20,4},{24,8},{28,12},{1,17},{... | collective-permute-start | bytes 1327112 | tf_op jit(solution)/shard_map/ppermute | solution.py:400
  38.4 12.3 %copy-start.20 = (s32[40,2]{0,1:T(2,128)S(1)}, s32[40,2]{0,1:T(2,128)}, u32[]{:S(2)}) copy-start(s32[40,2]{0,1:T(2,128)} %param.7) | copy-start | bytes 964
  38.4 12.3 %copy-start.21 = (s32[256]{0:T(256)S(1)}, s32[256]{0:T(256)}, u32[]{:S(2)}) copy-start(s32[256]{0:T(256)} %slots.1) | copy-start | bytes 3076
  38.4 14.1 %copy-start.1 = (bf16[320,256]{1,0:T(8,128)(2,1)S(1)}, bf16[320,256]{1,0:T(8,128)(2,1)}, u32[]{:S(2)}) copy-start(bf16[320,256]{1,0:T(8,128)(2,1)} %get-tuple-element.34.refs_2_) | copy-start | bytes 491524
  38.4 14.1 %copy-start.3 = (bf16[320,256]{1,0:T(8,128)(2,1)S(1)}, bf16[320,256]{1,0:T(8,128)(2,1)}, u32[]{:S(2)}) copy-start(bf16[320,256]{1,0:T(8,128)(2,1)} %get-tuple-element.35.refs_3_) | copy-start | bytes 491524
  38.4 14.1 %copy-start.5 = (bf16[136,320]{1,0:T(8,128)(2,1)S(1)}, bf16[136,320]{1,0:T(8,128)(2,1)}, u32[]{:S(2)}) copy-start(bf16[136,320]{1,0:T(8,128)(2,1)} %get-tuple-element.36.refs_4_) | copy-start | bytes 261124
  38.4 14.1 %copy-start.7 = (bf16[136,320]{1,0:T(8,128)(2,1)S(1)}, bf16[136,320]{1,0:T(8,128)(2,1)}, u32[]{:S(2)}) copy-start(bf16[136,320]{1,0:T(8,128)(2,1)} %get-tuple-element.37.refs_5_) | copy-start | bytes 261124
  38.4 14.1 %copy-start.16 = (s32[80]{0:T(128)S(1)}, s32[80]{0:T(128)}, u32[]{:S(2)}) copy-start(s32[80]{0:T(128)} %get-tuple-element.59.fetch) | copy-start | bytes 964
  38.4 14.1 %copy-start.18 = (s32[8]{0:T(128)S(1)}, s32[8]{0:T(128)}, u32[]{:S(2)}) copy-start(s32[8]{0:T(128)} %get-tuple-element.33.count) | copy-start | bytes 100
  38.5 130.5 %collective-permute-start.2 = (f32[10,144,128]{2,1,0:T(8,128)}, f32[10,144,128]{2,1,0:T(8,128)S(1)}, u32[]{:S(2)}, u32[]{:S(2)}) collective-permute-start(f32[10,144,128]{2,1,0:T(8,128)} %galerkin.11), channel_id=1, source_target_pairs={{0,20},{4,16},{8,28},{12,24},{16,4},{20,0},{24,12},{28,8},{1,21},{... | collective-permute-start | bytes 2211848 | tf_op jit(solution)/shard_map/ppermute | solution.py:400
  47.7 59.6 %collective-permute-start.3 = (f32[10,144,128]{2,1,0:T(8,128)S(1)}, f32[10,144,128]{2,1,0:T(8,128)S(1)}, u32[]{:S(2)}, u32[]{:S(2)}) collective-permute-start(f32[10,144,128]{2,1,0:T(8,128)S(1)} %galerkin.12), channel_id=1, source_target_pairs={{0,24},{4,28},{8,16},{12,20},{16,8},{20,12},{24,0},{28,4},{1,25},{... | collective-permute-start | bytes 2211848 | tf_op jit(solution)/shard_map/ppermute | solution.py:400
  60.6 19.4 %copy-start.10 = (f32[320,135]{0,1:T(8,128)S(1)}, f32[320,135]{0,1:T(8,128)}, u32[]{:S(2)}) copy-start(f32[320,135]{0,1:T(8,128)} %param.9) | copy-start | bytes 518404
  60.6 19.7 %copy-start.12 = (f32[320,256]{1,0:T(8,128)S(1)}, f32[320,256]{1,0:T(8,128)}, u32[]{:S(2)}) copy-start(f32[320,256]{1,0:T(8,128)} %get-tuple-element.39.p32.p_ref) | copy-start | bytes 983044
  65.8 103.2 %collective-permute-start.5 = (f32[10,144,128]{2,1,0:T(8,128)}, f32[10,144,128]{2,1,0:T(8,128)}, u32[]{:S(2)}, u32[]{:S(2)}) collective-permute-start(f32[10,144,128]{2,1,0:T(8,128)} %galerkin.14), channel_id=1, source_target_pairs={{0,8},{4,12},{8,0},{12,4},{16,24},{20,28},{24,16},{28,20},{1,9},{5... | collective-permute-start | bytes 2211848 | tf_op jit(solution)/shard_map/ppermute | solution.py:400
  68.3 10.1 %all-to-all-start.1 = ((f32[4,64,135]{2,1,0:T(8,128)}), f32[4,64,135]{2,1,0:T(8,128)}, u32[]{:S(2)}, u32[]{:S(2)}) async-start(f32[4,64,135]{2,1,0:T(8,128)} %broadcast_in_dim.29), calls=%async_computation.1 | async-start | bytes 524288 | tf_op jit(solution)/shard_map/all_to_all | solution.py:376
  107.2 61.7 %collective-permute-start.4 = (f32[10,144,128]{2,1,0:T(8,128)}, f32[10,144,128]{2,1,0:T(8,128)}, u32[]{:S(2)}, u32[]{:S(2)}) collective-permute-start(f32[10,144,128]{2,1,0:T(8,128)} %galerkin.13), channel_id=1, source_target_pairs={{0,28},{4,24},{8,20},{12,16},{16,12},{20,8},{24,4},{28,0},{1,29},{... | collective-permute-start | bytes 2211848 | tf_op jit(solution)/shard_map/ppermute | solution.py:400
  107.2 61.7 %collective-permute-start.7 = (f32[10,144,128]{2,1,0:T(8,128)}, f32[10,144,128]{2,1,0:T(8,128)}, u32[]{:S(2)}, u32[]{:S(2)}) collective-permute-start(f32[10,144,128]{2,1,0:T(8,128)} %galerkin.16), channel_id=1, source_target_pairs={{0,4},{4,0},{8,12},{12,8},{16,20},{20,16},{24,28},{28,24},{1,5},{5... | collective-permute-start | bytes 2211848 | tf_op jit(solution)/shard_map/ppermute | solution.py:400
  107.3 38.4 %copy-start.13 = (f32[10,144,128]{2,1,0:T(8,128)}, f32[10,144,128]{2,1,0:T(8,128)S(1)}, u32[]{:S(2)}) copy-start(f32[10,144,128]{2,1,0:T(8,128)S(1)} %collective-permute-done.3.refs_3_) | copy-start | bytes 2211844
  107.3 61.6 %collective-permute-start.6 = (f32[10,144,128]{2,1,0:T(8,128)}, f32[10,144,128]{2,1,0:T(8,128)}, u32[]{:S(2)}, u32[]{:S(2)}) collective-permute-start(f32[10,144,128]{2,1,0:T(8,128)} %galerkin.15), channel_id=1, source_target_pairs={{0,12},{4,8},{8,4},{12,0},{16,28},{20,24},{24,20},{28,16},{1,13},{... | collective-permute-start | bytes 2211848 | tf_op jit(solution)/shard_map/ppermute | solution.py:400
  135.5 9.5 %all-to-all-start.2 = ((f32[4,64,135]{2,1,0:T(8,128)}), f32[4,64,135]{2,1,0:T(8,128)S(1)}, u32[]{:S(2)}, u32[]{:S(2)}) async-start(f32[4,64,135]{2,1,0:T(8,128)} %copy.8), calls=%async_computation.2 | async-start | bytes 524288 | tf_op jit(solution)/shard_map/all_to_all | solution.py:421
  145.7 21.1 %all-to-all-start.3 = ((f32[8,8,135]{2,1,0:T(8,128)}), f32[8,8,135]{2,1,0:T(8,128)S(1)}, u32[]{:S(2)}, u32[]{:S(2)}) async-start(f32[8,8,135]{2,1,0:T(8,128)} %bitcast.7), calls=%async_computation.3 | async-start | bytes 131072 | tf_op jit(solution)/shard_map/all_to_all | solution.py:425
  149.0 17.7 %copy-start.9 = (f32[8,135,135]{2,0,1:T(8,128)S(1)}, f32[8,135,135]{2,0,1:T(8,128)}, u32[]{:S(2)}) copy-start(f32[8,135,135]{2,0,1:T(8,128)} %param.11) | copy-start | bytes 1749604
  168.9 1.1 copy-start.14

commit v5 on v4

--- a/solution.py
+++ b/solution.py
@@ -12,7 +12,6 @@
 BOTH = ("wide", "narrow")
 LANES = 128
 PAIR = 2
-EXCHANGE = 4
 WHOLE_VMEM = 67043328
 F32 = jnp.float32
 BF16 = jnp.bfloat16
@@ -32,7 +31,7 @@
 
 def send_plan(wide, cap):
     offsets = sorted(range(1, wide), key=lambda k: (-k.bit_length(), k))
-    first = min(2 * PAIR, cap)
+    first = min(3 * PAIR, cap)
     plan = [(offsets[0], 0, first)]
     if cap > first:
         plan.append((offsets[0], first, cap - first))
@@ -159,22 +158,24 @@
     return lax.fori_loop(0, coarse, add, jnp.zeros_like(vectors), unroll=9)
 
 
-def sweep_one_kernel(residual, p32, blocks, rhs, sweep):
+def sweep_one_kernel(residual, p32, blocks, rhs, sweep, copies):
     rhs[...] = jnp.dot(residual[...], p32[...], precision=PRECISE, preferred_element_type=F32)
     sweep[...] = DAMPING * apply_blocks(blocks, rhs[:, : blocks.shape[0]])
-
-
-def sweep_one_of(residual, p32, blocks):
+    copies[...] = jnp.broadcast_to(sweep[...][None], copies.shape)
+
+
+def sweep_one_of(residual, p32, blocks, wide):
     rows, coarse = residual.shape[0], blocks.shape[0]
     return pl.pallas_call(
         sweep_one_kernel,
         out_shape=(
             jax.ShapeDtypeStruct((rows, p32.shape[1]), F32),
             jax.ShapeDtypeStruct((rows, coarse), F32),
+            jax.ShapeDtypeStruct((wide, rows, coarse), F32),
         ),
         in_specs=[VMEM] * 3,
-        out_specs=(VMEM, VMEM),
-        compiler_params=pltpu.CompilerParams(vmem_limit_bytes=8 << 20),
+        out_specs=(VMEM, VMEM, VMEM),
+        compiler_params=pltpu.CompilerParams(vmem_limit_bytes=WHOLE_VMEM),
         name="sweep_one",
     )(residual, p32, blocks)
 
@@ -263,7 +264,7 @@
             o_ref[j, rows:, :] = jnp.where(last, corner, turned)
 
 
-def galerkin(face_blocks, operands, fetch, count, cap, piece, grant=50 << 20):
+def galerkin(face_blocks, operands, fetch, count, cap, piece):
     at, first, ranks = piece
     fine = face_blocks.shape[1]
     ph, _, th, _ = operands
@@ -279,7 +280,7 @@
             + [VMEM] * 4,
             out_specs=pl.BlockSpec((PAIR, rows + 8, LANES), lambda s, fetch, count: (s, 0, 0)),
         ),
-        compiler_params=pltpu.CompilerParams(vmem_limit_bytes=grant),
+        compiler_params=pltpu.CompilerParams(vmem_limit_bytes=WHOLE_VMEM),
         cost_estimate=pl.CostEstimate(
             flops=ranks * 6 * fine * fine * width,
             bytes_accessed=ranks * 4 * (fine * fine + rows * LANES),
@@ -393,39 +394,31 @@
     )
     parts = []
     for i, piece in enumerate(plan):
-        grant = 50 << 20 if i else WHOLE_VMEM
-        block = galerkin(face_blocks, operands, fetch, count, slots, piece, grant)
+        block = galerkin(face_blocks, operands, fetch, count, slots, piece)
         fetch = after(block, fetch)
         pairs = [(w, w ^ piece[0]) for w in range(wide)]
         parts.append(lax.ppermute(block, "wide", pairs))
         if i == 0:
             fine_residual, face_elems = after(block, fine_residual, face_elems)
             inverse = jnp.transpose(block_inverse, (1, 0, 2))
-            rhs, sweep_one = sweep_one_of(fine_residual, p32, inverse)
+            rhs, sweep_one, copies = sweep_one_of(fine_residual, p32, inverse, wide)
             fetch = after(sweep_one, fetch)
-            iterate = everyone(sweep_one, "wide", wide)
-        if i == EXCHANGE - 1:
-            iterate, face_elems = after(block, iterate, face_elems)
-            iterate = everyone(iterate.reshape(wide * dev_rows, coarse), "narrow", narrow)
-            row, col = face_rows(face_elems, coarse_slot, dev_rows, narrow, wide)
-            fetch = after(row, fetch)
-        if i == EXCHANGE + 1:
-            iterate = after(block, iterate).reshape(-1, coarse)
-            vectors = jnp.dot(jnp.take(iterate, col, axis=0), prolong.T, precision=PRECISE)
-            results = products(face_blocks, vectors, p32)
-            total = iterate.shape[0]
-            selector = lax.broadcasted_iota(jnp.int32, (total, faces), 0) == row[None, :]
-            sums = jnp.dot(selector.astype(F32), results, precision=PRECISE)[:, :coarse]
-            sums = sums.reshape(narrow, wide * dev_rows, coarse)
-            fetch = after(sums, fetch)
-            sums = lax.all_to_all(sums, "narrow", split_axis=0, concat_axis=0, tiled=True)
-        if i == len(plan) - 1:
-            sums = jnp.sum(after(block, sums), axis=0).reshape(wide, dev_rows, coarse)
-            fetch = after(sums, fetch)
-            sums = lax.all_to_all(sums, "wide", split_axis=0, concat_axis=0, tiled=True)
+            iterate = lax.all_to_all(copies, "wide", split_axis=0, concat_axis=0, tiled=True)
     parts.append(galerkin(face_blocks, operands, fetch, count, slots, (0, 0, slots)))
     pieces = [*plan, (0, 0, slots)]
-    sums = after(parts[-1], sums)
+    iterate, face_elems = after(parts[-1], iterate, face_elems)
+    iterate = everyone(iterate.reshape(wide * dev_rows, coarse), "narrow", narrow)
+    row, col = face_rows(face_elems, coarse_slot, dev_rows, narrow, wide)
+    iterate = iterate.reshape(-1, coarse)
+    vectors = jnp.dot(jnp.take(iterate, col, axis=0), prolong.T, precision=PRECISE)
+    results = products(face_blocks, vectors, p32)
+    total = iterate.shape[0]
+    selector = lax.broadcasted_iota(jnp.int32, (total, faces), 0) == row[None, :]
+    sums = jnp.dot(selector.astype(F32), results, precision=PRECISE)[:, :coarse]
+    sums = sums.reshape(narrow, wide * dev_rows, coarse)
+    sums = lax.all_to_all(sums, "narrow", split_axis=0, concat_axis=0, tiled=True)
+    sums = jnp.sum(sums, axis=0).reshape(wide, dev_rows, coarse)
+    sums = lax.all_to_all(sums, "wide", split_axis=0, concat_axis=0, tiled=True)
     correction = sweep_two_of(sums, rhs, sweep_one, prolong.T, inverse)
     owned = unpack(parts, pieces, cap, coarse, wide)
     return (correction, owned)

time: 178 us -> 236 us (1.33)
  blocking collectives: 0 us -> 81.3 us
  starting transfers between devices: 58.5 us -> 23 us
  waiting for transfers between devices: 25.1 us -> 38.6 us
  local copies, waits for them, and re-layouts: 13.9 us -> 4.52 us
  Pallas kernels: 76.9 us -> 83.7 us
    all_to_all x0 -> x2, blocking collectives: none -> 81.3 us  [the longest x1 72.2 us: local(): sums = lax.all_to_all(sums, 'wide', split_axis=0, concat_axis=0, tiled=True)]
    ppermute x8, starting transfers between devices: 43.8 us -> 14 us  [local(): parts.append(lax.ppermute(block, 'wide', pairs))]
    all_to_all x2 -> x1, waiting for transfers between devices: 19 us -> 37 us  [local(): lax.all_to_all(copies, 'wide', split_axis=0, concat_axis=0, tiled=True)]
    unnamed x44 -> x16, local copies, waits for them, and re-layouts: 9.03 us -> 2.34 us
    all_to_all x2 -> x1, waiting for transfers between devices: 6.05 us -> 1.49 us  [everyone(): lax.all_to_all(jnp.broadcast_to(x[None], (size, *x.shape)), axis, split_a...]
    all_to_all x2 -> x1, starting transfers between devices: 7.85 us -> 3.4 us  [everyone(): lax.all_to_all(jnp.broadcast_to(x[None], (size, *x.shape)), axis, split_a...]
    pallas_call x9, Pallas kernels: 53.7 us -> 58.1 us  [galerkin(): pl.pallas_call(functools.partial(galerkin_kernel, at, first), out_shape=j...]
    all_to_all x2 -> x1, starting transfers between devices: 6.86 us -> 5.59 us  [local(): lax.all_to_all(copies, 'wide', split_axis=0, concat_axis=0, tiled=True)]
  transfers between devices with their start and end apart: 12 -> 10, of which waited for: 3 -> 2; matrix products, arithmetic and copies ran while one was open for 4% -> 2% of each run, Pallas kernels for 35% -> 8%
where the time goes in v5:
time: 236 us; the launch traced here: 235 us
  Pallas kernels  83.7 us (35%)
  blocking collectives  81.3 us (34%)
  waiting for transfers between devices  38.6 us (16%)
  starting transfers between devices  23 us (10%)
  local copies, waits for them, and re-layouts  4.52 us (2%)
    all_to_all x1, blocking collectives, local(): sums = lax.all_to_all(sums, 'wide', split_axis=0, concat_axis=0, tiled=True)  72.2 us
    pallas_call x9, Pallas kernels, galerkin(): pl.pallas_call(functools.partial(galerkin_kernel, at, first), out_shape=j...  58.1 us
    all_to_all x1, waiting for transfers between devices, local(): lax.all_to_all(copies, 'wide', split_axis=0, concat_axis=0, tiled=True)  37 us
    ppermute x8, starting transfers between devices, local(): parts.append(lax.ppermute(block, 'wide', pairs))  14 us
    all_to_all x1, blocking collectives, local(): lax.all_to_all(sums, 'narrow', split_axis=0, concat_axis=0, tiled=True)  9.08 us
    pallas_call x1, Pallas kernels, products(): pl.pallas_call(product_kernel, out_shape=jax.ShapeDtypeStruct((faces, wid...  8.59 us
    pallas_call x1, Pallas kernels, unpack(): pl.pallas_call(functools.partial(unpack_kernel, pieces, cap, coarse), out...  7.2 us
    all_to_all x1, starting transfers between devices, local(): lax.all_to_all(copies, 'wide', split_axis=0, concat_axis=0, tiled=True)  5.59 us
  transfers between devices with their start and end apart: 10, of which 2 were waited for; matrix products, arithmetic and copies ran while one was open for 2% of the time, Pallas kernels for 8%

profile of v5, /device:TPU:0, one launch (start us, length us, event | category | flops | bytes accessed | tf_op | source)
XLA Modules:
  0.0 234.9 jit_solution(8214276330892026164)
XLA Ops:
  0.6 2.4 %place_faces.1 = (s32[80]{0:T(128)}, s32[8]{0:T(128)}, bf16[320,256]{1,0:T(8,128)(2,1)}, bf16[320,256]{1,0:T(8,128)(2,1)}, bf16[136,320]{1,0:T(8,128)(2,1)}, /*i...) custom-call(s32[2,40]{1,0:T(2,128)} %bitcast.15, s32[256]{0:T(256)} %slots.1, s32[1]{0:T(128)} %bitcast.1.me, f32[135,320]{1,0:T(8,128)} %bitcast.13), custom_call_target="tpu_custom_call" | custom-call | tf_op jit(solution)/shard_map/place_faces/pallas_call | solution.py:113
  3.0 5.5 %galerkin.9 = f32[6,144,128]{2,1,0:T(8,128)} custom-call(s32[80]{0:T(128)} %get-tuple-element.44.fetch, s32[8]{0:T(128)} %get-tuple-element.28.count, f32[40,320,320]{2,1,0:T(8,128)} %a_ref.1, f32[40,320,320]{2,1,0:T(8,128)} %a_ref.1, bf16[320,256]{1,0:T(8,128)(2,1)} %get-tuple-element.29.refs_2_, bf16[320,256]{1,0:T(8,128)(2,1)} %get-tuple-element.30.refs_3_, ...), custom_call_target="tpu_custom_call" | custom-call | flops 943718400 | bytes 2875392 | tf_op jit(solution)/shard_map/galerkin/pallas_call | solution.py:273
  8.5 3.6 %sweep_one.1 = (f32[8,256]{1,0:T(8,128)}, f32[8,135]{1,0:T(8,128)}, f32[8,8,135]{2,1,0:T(8,128)}) custom-call(f32[8,320]{1,0:T(8,128)} %residual, f32[320,256]{1,0:T(8,128)} %get-tuple-element.34.p32.p_ref, f32[135,8,135]{2,1,0:T(8,128)} %bitcast.11), custom_call_target="tpu_custom_call" | custom-call | tf_op jit(solution)/shard_map/sweep_one/pallas_call | solution.py:169
  12.1 2.8 %galerkin.10 = f32[4,144,128]{2,1,0:T(8,128)} custom-call(s32[80]{0:T(128)} %get-tuple-element.44.fetch, s32[8]{0:T(128)} %get-tuple-element.28.count, f32[40,320,320]{2,1,0:T(8,128)} %a_ref.1, f32[40,320,320]{2,1,0:T(8,128)} %a_ref.1, bf16[320,256]{1,0:T(8,128)(2,1)} %get-tuple-element.29.refs_2_, bf16[320,256]{1,0:T(8,128)(2,1)} %get-tuple-element.30.refs_3_, ...), custom_call_target="tpu_custom_call" | custom-call | flops 629145600 | bytes 1916928 | tf_op jit(solution)/shard_map/galerkin/pallas_call | solution.py:273
  14.9 6.2 %galerkin.11 = f32[10,144,128]{2,1,0:T(8,128)} custom-call(s32[80]{0:T(128)} %get-tuple-element.44.fetch, s32[8]{0:T(128)} %get-tuple-element.28.count, f32[40,320,320]{2,1,0:T(8,128)} %a_ref.1, f32[40,320,320]{2,1,0:T(8,128)} %a_ref.1, bf16[320,256]{1,0:T(8,128)(2,1)} %get-tuple-element.29.refs_2_, bf16[320,256]{1,0:T(8,128)(2,1)} %get-tuple-element.30.refs_3_, ...), custom_call_target="tpu_custom_call" | custom-call | flops 1572864000 | bytes 4792320 | tf_op jit(solution)/shard_map/galerkin/pallas_call | solution.py:273
  21.2 6.2 %galerkin.12 = f32[10,144,128]{2,1,0:T(8,128)} custom-call(s32[80]{0:T(128)} %get-tuple-element.44.fetch, s32[8]{0:T(128)} %get-tuple-element.28.count, f32[40,320,320]{2,1,0:T(8,128)} %a_ref.1, f32[40,320,320]{2,1,0:T(8,128)} %a_ref.1, bf16[320,256]{1,0:T(8,128)(2,1)} %get-tuple-element.29.refs_2_, bf16[320,256]{1,0:T(8,128)(2,1)} %get-tuple-element.30.refs_3_, ...), custom_call_target="tpu_custom_call" | custom-call | flops 1572864000 | bytes 4792320 | tf_op jit(solution)/shard_map/galerkin/pallas_call | solution.py:273
  27.4 8.3 %galerkin.13 = f32[10,144,128]{2,1,0:T(8,128)} custom-call(s32[80]{0:T(128)} %get-tuple-element.44.fetch, s32[8]{0:T(128)} %get-tuple-element.28.count, f32[40,320,320]{2,1,0:T(8,128)} %a_ref.1, f32[40,320,320]{2,1,0:T(8,128)} %a_ref.1, bf16[320,256]{1,0:T(8,128)(2,1)} %get-tuple-element.29.refs_2_, bf16[320,256]{1,0:T(8,128)(2,1)} %get-tuple-element.30.refs_3_, ...), custom_call_target="tpu_custom_call" | custom-call | flops 1572864000 | bytes 4792320 | tf_op jit(solution)/shard_map/galerkin/pallas_call | solution.py:273
  35.7 5.4 %galerkin.14 = f32[10,144,128]{2,1,0:T(8,128)} custom-call(s32[80]{0:T(128)} %get-tuple-element.44.fetch, s32[8]{0:T(128)} %get-tuple-element.28.count, f32[40,320,320]{2,1,0:T(8,128)} %a_ref.1, f32[40,320,320]{2,1,0:T(8,128)} %a_ref.1, bf16[320,256]{1,0:T(8,128)(2,1)} %get-tuple-element.29.refs_2_, bf16[320,256]{1,0:T(8,128)(2,1)} %get-tuple-element.30.refs_3_, ...), custom_call_target="tpu_custom_call" | custom-call | flops 1572864000 | bytes 4792320 | tf_op jit(solution)/shard_map/galerkin/pallas_call | solution.py:273
  41.2 7.6 %galerkin.15 = f32[10,144,128]{2,1,0:T(8,128)} custom-call(s32[80]{0:T(128)} %get-tuple-element.44.fetch, s32[8]{0:T(128)} %get-tuple-element.28.count, f32[40,320,320]{2,1,0:T(8,128)} %a_ref.1, f32[40,320,320]{2,1,0:T(8,128)} %a_ref.1, bf16[320,256]{1,0:T(8,128)(2,1)} %get-tuple-element.29.refs_2_, bf16[320,256]{1,0:T(8,128)(2,1)} %get-tuple-element.30.refs_3_, ...), custom_call_target="tpu_custom_call" | custom-call | flops 1572864000 | bytes 4792320 | tf_op jit(solution)/shard_map/galerkin/pallas_call | solution.py:273
  48.7 9.7 %galerkin.16 = f32[10,144,128]{2,1,0:T(8,128)} custom-call(s32[80]{0:T(128)} %get-tuple-element.44.fetch, s32[8]{0:T(128)} %get-tuple-element.28.count, f32[40,320,320]{2,1,0:T(8,128)} %a_ref.1, f32[40,320,320]{2,1,0:T(8,128)} %a_ref.1, bf16[320,256]{1,0:T(8,128)(2,1)} %get-tuple-element.29.refs_2_, bf16[320,256]{1,0:T(8,128)(2,1)} %get-tuple-element.30.refs_3_, ...), custom_call_target="tpu_custom_call" | custom-call | flops 1572864000 | bytes 4792320 | tf_op jit(solution)/shard_map/galerkin/pallas_call | solution.py:273
  58.4 1.4 collective-permute-start.7
  59.9 6.6 %collective-permute-start.1 = (f32[4,144,128]{2,1,0:T(8,128)}, f32[4,144,128]{2,1,0:T(8,128)}, u32[]{:S(2)}, u32[]{:S(2)}) collective-permute-start(f32[4,144,128]{2,1,0:T(8,128)} %galerkin.10), channel_id=1, source_target_pairs={{0,16},{4,20},{8,24},{12,28},{16,0},{20,4},{24,8},{28,12},{1,17},{... | collective-permute-start | bytes 884744 | tf_op jit(solution)/shard_map/ppermute | solution.py:400
  66.4 0.0 collective-permute-start
  66.4 1.2 collective-permute-start.6
  67.7 0.3 collective-permute-start.5
  68.0 5.6 %all-to-all-start = ((f32[8,8,135]{2,1,0:T(8,128)}), f32[8,8,135]{2,1,0:T(8,128)}, u32[]{:S(2)}, u32[]{:S(2)}) async-start(f32[8,8,135]{2,1,0:T(8,128)} %get-tuple-element.45), calls=%async_computation | async-start | bytes 131072 | tf_op jit(solution)/shard_map/all_to_all | solution.py:406
  73.5 6.2 %galerkin.17.refs_8_ = f32[10,144,128]{2,1,0:T(8,128)} custom-call(s32[80]{0:T(128)} %get-tuple-element.44.fetch, s32[8]{0:T(128)} %get-tuple-element.28.count, f32[40,320,320]{2,1,0:T(8,128)} %a_ref.1, f32[40,320,320]{2,1,0:T(8,128)} %a_ref.1, bf16[320,256]{1,0:T(8,128)(2,1)} %get-tuple-element.29.refs_2_, bf16[320,256]{1,0:T(8,128)(2,1)} %get-tuple-element.30.refs_3_, ...), custom_call_target="tpu_custom_call" | custom-call | flops 1572864000 | bytes 4792320 | tf_op jit(solution)/shard_map/galerkin/pallas_call | solution.py:273
  79.8 37.0 %all-to-all-done = f32[8,8,135]{2,1,0:T(8,128)} async-done(((f32[8,8,135]{2,1,0:T(8,128)}), f32[8,8,135]{2,1,0:T(8,128)}, u32[]{:S(2)}, u32[]{:S(2)}) %all-to-all-start) | async-done | bytes 34592 | tf_op jit(solution)/shard_map/all_to_all | solution.py:406
  116.8 0.0 copy-start.6
  116.8 0.7 copy-done.6
  117.5 0.0 copy-start.7
  117.5 0.7 copy-done.7
  118.2 1.7 face_rows.1
  119.9 1.6 broadcast_in_dim.22
  121.5 3.4 %all-to-all-start.1 = ((f32[4,64,135]{2,1,0:T(8,128)}), f32[4,64,135]{2,1,0:T(8,128)S(1)}, u32[]{:S(2)}, u32[]{:S(2)}) async-start(f32[4,64,135]{2,1,0:T(8,128)} %broadcast_in_dim.22), calls=%async_computation.1 | async-start | bytes 524288 | tf_op jit(solution)/shard_map/all_to_all | solution.py:377
  124.9 0.0 collective-permute-done.1.refs_1_
  125.0 3.3 %collective-permute-start.4 = (f32[10,144,128]{2,1,0:T(8,128)}, f32[10,144,128]{2,1,0:T(8,128)S(1)}, u32[]{:S(2)}, u32[]{:S(2)}) collective-permute-start(f32[10,144,128]{2,1,0:T(8,128)} %galerkin.13), channel_id=1, source_target_pairs={{0,28},{4,24},{8,20},{12,16},{16,12},{20,8},{24,4},{28,0},{1,29},{... | collective-permute-start | bytes 2211848 | tf_op jit(solution)/shard_map/ppermute | solution.py:400
  128.3 0.0 collective-permute-done.refs_0_
  128.3 1.1 collective-permute-start.3
  129.4 0.0 collective-permute-done.7.refs_7_
  129.4 0.0 collective-permute-start.2
  129.4 1.5 all-to-all-done.1
  130.9 0.6 gather_fusion
  131.5 1.2 fusion.3.v_ref
  132.8 0.0 copy-start.3
  132.8 1.0 copy-done.3
  133.7 0.0 copy-start
  133.7 0.0 copy-start.2
  133.7 0.0 copy-start.4
  133.7 0.0 copy-start.5
  133.7 0.0 copy-start.1
  133.8 8.6 %products.1 = f32[40,256]{1,0:T(8,128)S(1)} custom-call(f32[40,320,320]{2,1,0:T(8,128)} %a_ref.1, f32[40,320]{1,0:T(8,128)S(1)} %fusion.3.v_ref, f32[320,256]{1,0:T(8,128)S(1)} %copy-done.3), custom_call_target="tpu_custom_call" | custom-call | flops 16384000 | bytes 16384000 | tf_op jit(solution)/shard_map/products/pallas_call | solution.py:211
  142.3 0.2 fusion
  142.6 9.1 %all_to_all.20 = f32[4,64,135]{2,1,0:T(8,128)} all-to-all(f32[4,64,135]{2,1,0:T(8,128)S(1)} %bitcast.19), channel_id=1, replica_groups=mesh['wide'=8,'narrow'=4] {'narrow'}, dimensions={0} | all-to-all | bytes 276480 | tf_op jit(solution)/shard_map/all_to_all | solution.py:419
  151.7 1.6 reduce_sum.9
  153.3 72.2 %all_to_all.21.sums = f32[8,8,135]{2,1,0:T(8,128)S(1)} all-to-all(f32[8,8,135]{2,1,0:T(8,128)} %bitcast.20), channel_id=1, replica_groups=mesh['wide'=8,'narrow'=4] {'wide'}, dimensions={0} | all-to-all | bytes 69120 | tf_op jit(solution)/shard_map/all_to_all | solution.py:421
  225.5 0.0 copy-done
  225.5 0.0 copy-done.2
  225.5 0.0 copy-done.4
  225.5 0.0 copy-done.5
  225.5 2.2 sweep_two.1
  227.7 0.0 collective-permute-done.6.refs_6_
  227.7 0.0 collective-permute-done.5.refs_5_
  227.7 0.0 collective-permute-done.4.refs_4_
  227.7 0.0 collective-permute-done.3.refs_3_
  227.7 0.0 collective-permute-done.2.refs_2_
  227.7 0.0 copy-done.1
  227.7 7.2 %unpack.1 = f32[135,135,80]{2,1,0:T(8,128)} custom-call(s32[1]{0:T(128)} %bitcast.1.me, f32[6,144,128]{2,1,0:T(8,128)} %collective-permute-done.refs_0_, f32[4,144,128]{2,1,0:T(8,128)} %collective-permute-done.1.refs_1_, f32[10,144,128]{2,1,0:T(8,128)} %collective-permute-done.2.refs_2_, f32[10,144,128]{2,1,0:T(8,128)S(1)} %collective-permute-done.3.refs_3_, ...), custom_call_target="tpu_custom_call" | custom-call | bytes 11796480 | tf_op jit(solution)/shard_map/unpack/pallas_call | solution.py:350
  (3 shorter events, 0.0 us)
Async XLA Ops:
  58.4 71.0 %collective-permute-start.7 = (f32[10,144,128]{2,1,0:T(8,128)}, f32[10,144,128]{2,1,0:T(8,128)}, u32[]{:S(2)}, u32[]{:S(2)}) collective-permute-start(f32[10,144,128]{2,1,0:T(8,128)} %galerkin.16), channel_id=1, source_target_pairs={{0,4},{4,0},{8,12},{12,8},{16,20},{20,16},{24,28},{28,24},{1,5},{5... | collective-permute-start | bytes 2211848 | tf_op jit(solution)/shard_map/ppermute | solution.py:400
  59.9 65.1 %collective-permute-start.1 = (f32[4,144,128]{2,1,0:T(8,128)}, f32[4,144,128]{2,1,0:T(8,128)}, u32[]{:S(2)}, u32[]{:S(2)}) collective-permute-start(f32[4,144,128]{2,1,0:T(8,128)} %galerkin.10), channel_id=1, source_target_pairs={{0,16},{4,20},{8,24},{12,28},{16,0},{20,4},{24,8},{28,12},{1,17},{... | collective-permute-start | bytes 884744 | tf_op jit(solution)/shard_map/ppermute | solution.py:400
  66.4 61.9 %collective-permute-start = (f32[6,144,128]{2,1,0:T(8,128)}, f32[6,144,128]{2,1,0:T(8,128)}, u32[]{:S(2)}, u32[]{:S(2)}) collective-permute-start(f32[6,144,128]{2,1,0:T(8,128)} %galerkin.9), channel_id=1, source_target_pairs={{0,16},{4,20},{8,24},{12,28},{16,0},{20,4},{24,8},{28,12},{1,17},{... | collective-permute-start | bytes 1327112 | tf_op jit(solution)/shard_map/ppermute | solution.py:400
  66.4 161.2 %collective-permute-start.6 = (f32[10,144,128]{2,1,0:T(8,128)}, f32[10,144,128]{2,1,0:T(8,128)}, u32[]{:S(2)}, u32[]{:S(2)}) collective-permute-start(f32[10,144,128]{2,1,0:T(8,128)} %galerkin.15), channel_id=1, source_target_pairs={{0,12},{4,8},{8,4},{12,0},{16,28},{20,24},{24,20},{28,16},{1,13},{... | collective-permute-start | bytes 2211848 | tf_op jit(solution)/shard_map/ppermute | solution.py:400
  67.7 160.0 %collective-permute-start.5 = (f32[10,144,128]{2,1,0:T(8,128)}, f32[10,144,128]{2,1,0:T(8,128)}, u32[]{:S(2)}, u32[]{:S(2)}) collective-permute-start(f32[10,144,128]{2,1,0:T(8,128)} %galerkin.14), channel_id=1, source_target_pairs={{0,8},{4,12},{8,0},{12,4},{16,24},{20,28},{24,16},{28,20},{1,9},{5... | collective-permute-start | bytes 2211848 | tf_op jit(solution)/shard_map/ppermute | solution.py:400
  68.0 48.9 %all-to-all-start = ((f32[8,8,135]{2,1,0:T(8,128)}), f32[8,8,135]{2,1,0:T(8,128)}, u32[]{:S(2)}, u32[]{:S(2)}) async-start(f32[8,8,135]{2,1,0:T(8,128)} %get-tuple-element.45), calls=%async_computation | async-start | bytes 131072 | tf_op jit(solution)/shard_map/all_to_all | solution.py:406
  116.8 0.7 copy-start.6
  117.5 0.7 copy-start.7
  121.5 9.4 %all-to-all-start.1 = ((f32[4,64,135]{2,1,0:T(8,128)}), f32[4,64,135]{2,1,0:T(8,128)S(1)}, u32[]{:S(2)}, u32[]{:S(2)}) async-start(f32[4,64,135]{2,1,0:T(8,128)} %broadcast_in_dim.22), calls=%async_computation.1 | async-start | bytes 524288 | tf_op jit(solution)/shard_map/all_to_all | solution.py:377
  125.0 102.7 %collective-permute-start.4 = (f32[10,144,128]{2,1,0:T(8,128)}, f32[10,144,128]{2,1,0:T(8,128)S(1)}, u32[]{:S(2)}, u32[]{:S(2)}) collective-permute-start(f32[10,144,128]{2,1,0:T(8,128)} %galerkin.13), channel_id=1, source_target_pairs={{0,28},{4,24},{8,20},{12,16},{16,12},{20,8},{24,4},{28,0},{1,29},{... | collective-permute-start | bytes 2211848 | tf_op jit(solution)/shard_map/ppermute | solution.py:400
  128.3 99.4 %collective-permute-start.3 = (f32[10,144,128]{2,1,0:T(8,128)}, f32[10,144,128]{2,1,0:T(8,128)S(1)}, u32[]{:S(2)}, u32[]{:S(2)}) collective-permute-start(f32[10,144,128]{2,1,0:T(8,128)} %galerkin.12), channel_id=1, source_target_pairs={{0,24},{4,28},{8,16},{12,20},{16,8},{20,12},{24,0},{28,4},{1,25},{... | collective-permute-start | bytes 2211848 | tf_op jit(solution)/shard_map/ppermute | solution.py:400
  129.4 98.3 %collective-permute-start.2 = (f32[10,144,128]{2,1,0:T(8,128)}, f32[10,144,128]{2,1,0:T(8,128)}, u32[]{:S(2)}, u32[]{:S(2)}) collective-permute-start(f32[10,144,128]{2,1,0:T(8,128)} %galerkin.11), channel_id=1, source_target_pairs={{0,20},{4,16},{8,28},{12,24},{16,4},{20,0},{24,12},{28,8},{1,21},{... | collective-permute-start | bytes 2211848 | tf_op jit(solution)/shard_map/ppermute | solution.py:400
  132.8 1.0 copy-start.3
  133.7 91.7 %copy-start = (f32[8,135,135]{2,0,1:T(8,128)S(1)}, f32[8,135,135]{2,0,1:T(8,128)}, u32[]{:S(2)}) copy-start(f32[8,135,135]{2,0,1:T(8,128)} %param.11) | copy-start | bytes 1749604
  133.7 91.7 %copy-start.2 = (f32[320,135]{0,1:T(8,128)S(1)}, f32[320,135]{0,1:T(8,128)}, u32[]{:S(2)}) copy-start(f32[320,135]{0,1:T(8,128)} %param.9) | copy-start | bytes 518404
  133.7 91.7 %copy-start.4 = (f32[8,256]{1,0:T(8,128)S(1)}, f32[8,256]{1,0:T(8,128)}, u32[]{:S(2)}) copy-start(f32[8,256]{1,0:T(8,128)} %get-tuple-element.51.rhs) | copy-start | bytes 24580
  133.7 91.7 %copy-start.5 = (f32[8,135]{1,0:T(8,128)S(1)}, f32[8,135]{1,0:T(8,128)}, u32[]{:S(2)}) copy-start(f32[8,135]{1,0:T(8,128)} %get-tuple-element.35.sweep) | copy-start | bytes 12964
  133.7 93.9 %copy-start.1 = (f32[10,144,128]{2,1,0:T(8,128)S(1)}, f32[10,144,128]{2,1,0:T(8,128)}, u32[]{:S(2)}) copy-start(f32[10,144,128]{2,1,0:T(8,128)} %galerkin.17.refs_8_) | copy-start | bytes 2211844

commit v6 on v5

--- a/solution.py
+++ b/solution.py
@@ -31,7 +31,7 @@
 
 def send_plan(wide, cap):
     offsets = sorted(range(1, wide), key=lambda k: (-k.bit_length(), k))
-    first = min(3 * PAIR, cap)
+    first = min(PAIR, cap)
     plan = [(offsets[0], 0, first)]
     if cap > first:
         plan.append((offsets[0], first, cap - first))
@@ -77,23 +77,6 @@
     th[...], tl[...] = split(wide_pt[:rows, :fine])
     p32[...] = wide_pt[...].T[:fine]
     ph[...], pl_[...] = split(p32[...])
-
-
-def index_kernel(dev_rows, narrow, wide, elems, slots, row, col):
-    owner_rows = dev_rows * narrow
-
-    def moved(r):
-        owner = lax.div(r, owner_rows)
-        inner = r - owner * owner_rows
-        n = lax.div(inner, dev_rows)
-        return (n * wide + owner) * dev_rows + inner - n * dev_rows
-
-    def put(f, c):
-        row[f] = moved(slots[elems[0, f]])
-        col[f] = moved(slots[elems[1, f]])
-        return c
-
-    lax.fori_loop(0, elems.shape[1], put, 0, unroll=8)
 
 
 SMEM = pl.BlockSpec(memory_space=pltpu.SMEM)
@@ -135,18 +118,6 @@
     )(face_elems.T, coarse_slot, me, prolong.T)
 
 
-def face_rows(face_elems, coarse_slot, dev_rows, narrow, wide):
-    faces = face_elems.shape[0]
-    return pl.pallas_call(
-        functools.partial(index_kernel, dev_rows, narrow, wide),
-        out_shape=(ints(faces), ints(faces)),
-        in_specs=[SMEM, SMEM],
-        out_specs=(SMEM, SMEM),
-        compiler_params=pltpu.CompilerParams(vmem_limit_bytes=8 << 20),
-        name="face_rows",
-    )(face_elems.T, coarse_slot)
-
-
 def apply_blocks(blocks, vectors):
     coarse = blocks.shape[0]
     lane = lax.broadcasted_iota(jnp.int32, vectors.shape, 1)
@@ -182,7 +153,7 @@
 
 def sweep_two_kernel(sums, rhs, sweep, pt, blocks, out):
     coarse = blocks.shape[0]
-    update = (1.0 - DAMPING) * rhs[:, :coarse] - jnp.sum(sums[...], axis=0)
+    update = (1.0 - DAMPING) * rhs[:, :coarse] - jnp.sum(sums[...], axis=0)[:, :coarse]
     last = sweep[...] + DAMPING * apply_blocks(blocks, update)
     out[...] = jnp.dot(last, pt[...], precision=PRECISE, preferred_element_type=F32)
 
@@ -198,32 +169,53 @@
     )(sums, rhs, sweep, pt, blocks)
 
 
-def product_kernel(a_ref, v_ref, p_ref, o_ref):
-    for j in range(a_ref.shape[0]):
-        applied = jnp.sum(a_ref[j] * v_ref[j : j + 1, :], axis=1, keepdims=True)
-        o_ref[j : j + 1, :] = jnp.sum(p_ref[...] * applied, axis=0, keepdims=True)
-
-
-def products(face_blocks, vectors, p32):
+def product_kernel(dev_rows, narrow, wide, elems, slots, a_ref, x_ref, p_ref, pt_ref, sums):
+    step = pl.program_id(0)
+    group = a_ref.shape[0]
+    owner_rows = dev_rows * narrow
+
+    def moved(r):
+        owner = lax.div(r, owner_rows)
+        inner = r - owner * owner_rows
+        n = lax.div(inner, dev_rows)
+        return (n * wide + owner) * dev_rows + inner - n * dev_rows
+
+    @pl.when(step == 0)
+    def _():
+        sums[...] = jnp.zeros_like(sums)
+
+    faces = [step * group + j for j in range(group)]
+    vectors = [x_ref[pl.ds(moved(slots[elems[1, f]]), 1), :] for f in faces]
+    vectors = jnp.concatenate(vectors, axis=0)
+    vectors = jnp.dot(vectors, pt_ref[...], precision=PRECISE, preferred_element_type=F32)
+    for j, f in enumerate(faces):
+        applied = jnp.sum(a_ref[j] * vectors[j : j + 1, :], axis=1, keepdims=True)
+        row = pl.ds(moved(slots[elems[0, f]]), 1)
+        sums[row, :] = sums[row, :] + jnp.sum(p_ref[...] * applied, axis=0, keepdims=True)
+
+
+def products(face_blocks, face_elems, coarse_slot, iterate, p32, pt, dev_rows, narrow, wide):
     faces, fine, _ = face_blocks.shape
     group = 8 if faces % 8 == 0 else faces
-    width = p32.shape[1]
     return pl.pallas_call(
-        product_kernel,
-        out_shape=jax.ShapeDtypeStruct((faces, width), F32),
+        functools.partial(product_kernel, dev_rows, narrow, wide),
+        out_shape=jax.ShapeDtypeStruct((iterate.shape[0], p32.shape[1]), F32),
         grid=(faces // group,),
         in_specs=[
+            SMEM,
+            SMEM,
             pl.BlockSpec((group, fine, fine), lambda s: (s, 0, 0)),
-            pl.BlockSpec((group, fine), lambda s: (s, 0)),
+            VMEM,
+            VMEM,
             VMEM,
         ],
-        out_specs=pl.BlockSpec((group, width), lambda s: (s, 0)),
+        out_specs=VMEM,
         compiler_params=pltpu.CompilerParams(vmem_limit_bytes=48 << 20),
         cost_estimate=pl.CostEstimate(
             flops=4 * faces * fine * fine, bytes_accessed=4 * faces * fine * fine, transcendentals=0
         ),
         name="products",
-    )(face_blocks, vectors, p32)
+    )(face_elems.T, coarse_slot, face_blocks, iterate, p32, pt)
 
 
 def galerkin_kernel(at, first, fetch, count, *refs):
@@ -398,29 +390,25 @@
         fetch = after(block, fetch)
         pairs = [(w, w ^ piece[0]) for w in range(wide)]
         parts.append(lax.ppermute(block, "wide", pairs))
-        if i == 0:
+        if i == 1:
             fine_residual, face_elems = after(block, fine_residual, face_elems)
             inverse = jnp.transpose(block_inverse, (1, 0, 2))
             rhs, sweep_one, copies = sweep_one_of(fine_residual, p32, inverse, wide)
             fetch = after(sweep_one, fetch)
             iterate = lax.all_to_all(copies, "wide", split_axis=0, concat_axis=0, tiled=True)
+    iterate = after(block, iterate)
+    iterate = everyone(iterate.reshape(wide * dev_rows, coarse), "narrow", narrow)
     parts.append(galerkin(face_blocks, operands, fetch, count, slots, (0, 0, slots)))
     pieces = [*plan, (0, 0, slots)]
-    iterate, face_elems = after(parts[-1], iterate, face_elems)
-    iterate = everyone(iterate.reshape(wide * dev_rows, coarse), "narrow", narrow)
-    row, col = face_rows(face_elems, coarse_slot, dev_rows, narrow, wide)
-    iterate = iterate.reshape(-1, coarse)
-    vectors = jnp.dot(jnp.take(iterate, col, axis=0), prolong.T, precision=PRECISE)
-    results = products(face_blocks, vectors, p32)
-    total = iterate.shape[0]
-    selector = lax.broadcasted_iota(jnp.int32, (total, faces), 0) == row[None, :]
-    sums = jnp.dot(selector.astype(F32), results, precision=PRECISE)[:, :coarse]
-    sums = sums.reshape(narrow, wide * dev_rows, coarse)
+    iterate = after(parts[-1], iterate).reshape(-1, coarse)
+    sums = products(
+        face_blocks, face_elems, coarse_slot, iterate, p32, prolong.T, dev_rows, narrow, wide
+    ).reshape(narrow, wide * dev_rows, -1)
     sums = lax.all_to_all(sums, "narrow", split_axis=0, concat_axis=0, tiled=True)
-    sums = jnp.sum(sums, axis=0).reshape(wide, dev_rows, coarse)
+    sums = jnp.sum(sums, axis=0).reshape(wide, dev_rows, -1)
     sums = lax.all_to_all(sums, "wide", split_axis=0, concat_axis=0, tiled=True)
-    correction = sweep_two_of(sums, rhs, sweep_one, prolong.T, inverse)
     owned = unpack(parts, pieces, cap, coarse, wide)
+    correction = sweep_two_of(after(owned, sums), rhs, sweep_one, prolong.T, inverse)
     return (correction, owned)
 
 

time: 236 us -> 249 us (1.055)
  waiting for transfers between devices: 38.6 us -> 116 us
  blocking collectives: 81.3 us -> 11.4 us
  starting transfers between devices: 23 us -> 27.3 us
  local copies, waits for them, and re-layouts: 4.52 us -> 7.27 us
    all_to_all x1 -> x0, blocking collectives: 72.2 us -> none  [local(): sums = lax.all_to_all(sums, 'wide', split_axis=0, concat_axis=0, tiled=True)]
    all_to_all x1, waiting for transfers between devices: 37 us -> 87.1 us  [local(): lax.all_to_all(copies, 'wide', split_axis=0, concat_axis=0, tiled=True)]
    ppermute x8, waiting for transfers between devices: 0.02 us -> 29.2 us  [local(): parts.append(lax.ppermute(block, 'wide', pairs))]
    unnamed x16 -> x30, local copies, waits for them, and re-layouts: 2.34 us -> 6.56 us
    all_to_all x0 -> x1, starting transfers between devices: none -> 3.88 us  [local(): sums = lax.all_to_all(sums, 'wide', split_axis=0, concat_axis=0, tiled=True)]
    pallas_call x2 -> x1, Pallas kernels: 10.3 us -> 9.2 us  [products(): pl.pallas_call(functools.partial(product_kernel, dev_rows, narrow, wide),...]
  transfers between devices with their start and end apart: 10 -> 11, of which waited for: 2 -> 2; matrix products, arithmetic and copies ran while one was open for 2% -> 1% of each run, Pallas kernels for 8% -> 9%
where the time goes in v6:
time: 249 us; the launch traced here: 248 us
  waiting for transfers between devices  116 us (47%)
  Pallas kernels  83.1 us (33%)
  starting transfers between devices  27.3 us (11%)
  blocking collectives  11.4 us (5%)
  local copies, waits for them, and re-layouts  7.27 us (3%)
    all_to_all x1, waiting for transfers between devices, local(): lax.all_to_all(copies, 'wide', split_axis=0, concat_axis=0, tiled=True)  87.1 us
    pallas_call x9, Pallas kernels, galerkin(): pl.pallas_call(functools.partial(galerkin_kernel, at, first), out_shape=j...  58.7 us
    ppermute x8, waiting for transfers between devices, local(): parts.append(lax.ppermute(block, 'wide', pairs))  29.2 us
    ppermute x8, starting transfers between devices, local(): parts.append(lax.ppermute(block, 'wide', pairs))  14.3 us
    all_to_all x1, blocking collectives, local(): lax.all_to_all(sums, 'narrow', split_axis=0, concat_axis=0, tiled=True)  11.4 us
    pallas_call x1, Pallas kernels, products(): pl.pallas_call(functools.partial(product_kernel, dev_rows, narrow, wide),...  9.2 us
    pallas_call x1, Pallas kernels, unpack(): pl.pallas_call(functools.partial(unpack_kernel, pieces, cap, coarse), out...  7.15 us
    unnamed x30, local copies, waits for them, and re-layouts  6.56 us
  transfers between devices with their start and end apart: 11, of which 2 were waited for; matrix products, arithmetic and copies ran while one was open for 1% of the time, Pallas kernels for 9%

profile of v6, /device:TPU:0, one launch (start us, length us, event | category | flops | bytes accessed | tf_op | source)
XLA Modules:
  0.0 247.9 jit_solution(13612602375318901048)
XLA Ops:
  0.6 2.3 place_faces.1
  2.9 4.1 %galerkin.9 = f32[2,144,128]{2,1,0:T(8,128)} custom-call(s32[80]{0:T(128)} %get-tuple-element.43.fetch, s32[8]{0:T(128)} %get-tuple-element.27.count, f32[40,320,320]{2,1,0:T(8,128)} %a_ref.1, f32[40,320,320]{2,1,0:T(8,128)} %a_ref.1, bf16[320,256]{1,0:T(8,128)(2,1)} %get-tuple-element.28.refs_2_, bf16[320,256]{1,0:T(8,128)(2,1)} %get-tuple-element.29.refs_3_, ...), custom_call_target="tpu_custom_call" | custom-call | flops 314572800 | bytes 958464 | tf_op jit(solution)/shard_map/galerkin/pallas_call | solution.py:265
  7.0 4.8 %galerkin.10 = f32[8,144,128]{2,1,0:T(8,128)} custom-call(s32[80]{0:T(128)} %get-tuple-element.43.fetch, s32[8]{0:T(128)} %get-tuple-element.27.count, f32[40,320,320]{2,1,0:T(8,128)} %a_ref.1, f32[40,320,320]{2,1,0:T(8,128)} %a_ref.1, bf16[320,256]{1,0:T(8,128)(2,1)} %get-tuple-element.28.refs_2_, bf16[320,256]{1,0:T(8,128)(2,1)} %get-tuple-element.29.refs_3_, ...), custom_call_target="tpu_custom_call" | custom-call | flops 1258291200 | bytes 3833856 | tf_op jit(solution)/shard_map/galerkin/pallas_call | solution.py:265
  11.8 3.6 %sweep_one.1 = (f32[8,256]{1,0:T(8,128)}, f32[8,135]{1,0:T(8,128)}, f32[8,8,135]{2,1,0:T(8,128)}) custom-call(f32[8,320]{1,0:T(8,128)} %residual, f32[320,256]{1,0:T(8,128)} %get-tuple-element.34.p32.p_ref, f32[135,8,135]{2,1,0:T(8,128)} %bitcast.10), custom_call_target="tpu_custom_call" | custom-call | tf_op jit(solution)/shard_map/sweep_one/pallas_call | solution.py:140
  15.4 6.2 %galerkin.11 = f32[10,144,128]{2,1,0:T(8,128)} custom-call(s32[80]{0:T(128)} %get-tuple-element.43.fetch, s32[8]{0:T(128)} %get-tuple-element.27.count, f32[40,320,320]{2,1,0:T(8,128)} %a_ref.1, f32[40,320,320]{2,1,0:T(8,128)} %a_ref.1, bf16[320,256]{1,0:T(8,128)(2,1)} %get-tuple-element.28.refs_2_, bf16[320,256]{1,0:T(8,128)(2,1)} %get-tuple-element.29.refs_3_, ...), custom_call_target="tpu_custom_call" | custom-call | flops 1572864000 | bytes 4792320 | tf_op jit(solution)/shard_map/galerkin/pallas_call | solution.py:265
  21.7 6.2 %galerkin.12 = f32[10,144,128]{2,1,0:T(8,128)} custom-call(s32[80]{0:T(128)} %get-tuple-element.43.fetch, s32[8]{0:T(128)} %get-tuple-element.27.count, f32[40,320,320]{2,1,0:T(8,128)} %a_ref.1, f32[40,320,320]{2,1,0:T(8,128)} %a_ref.1, bf16[320,256]{1,0:T(8,128)(2,1)} %get-tuple-element.28.refs_2_, bf16[320,256]{1,0:T(8,128)(2,1)} %get-tuple-element.29.refs_3_, ...), custom_call_target="tpu_custom_call" | custom-call | flops 1572864000 | bytes 4792320 | tf_op jit(solution)/shard_map/galerkin/pallas_call | solution.py:265
  27.9 8.4 %galerkin.13 = f32[10,144,128]{2,1,0:T(8,128)} custom-call(s32[80]{0:T(128)} %get-tuple-element.43.fetch, s32[8]{0:T(128)} %get-tuple-element.27.count, f32[40,320,320]{2,1,0:T(8,128)} %a_ref.1, f32[40,320,320]{2,1,0:T(8,128)} %a_ref.1, bf16[320,256]{1,0:T(8,128)(2,1)} %get-tuple-element.28.refs_2_, bf16[320,256]{1,0:T(8,128)(2,1)} %get-tuple-element.29.refs_3_, ...), custom_call_target="tpu_custom_call" | custom-call | flops 1572864000 | bytes 4792320 | tf_op jit(solution)/shard_map/galerkin/pallas_call | solution.py:265
  36.2 5.5 %galerkin.14 = f32[10,144,128]{2,1,0:T(8,128)} custom-call(s32[80]{0:T(128)} %get-tuple-element.43.fetch, s32[8]{0:T(128)} %get-tuple-element.27.count, f32[40,320,320]{2,1,0:T(8,128)} %a_ref.1, f32[40,320,320]{2,1,0:T(8,128)} %a_ref.1, bf16[320,256]{1,0:T(8,128)(2,1)} %get-tuple-element.28.refs_2_, bf16[320,256]{1,0:T(8,128)(2,1)} %get-tuple-element.29.refs_3_, ...), custom_call_target="tpu_custom_call" | custom-call | flops 1572864000 | bytes 4792320 | tf_op jit(solution)/shard_map/galerkin/pallas_call | solution.py:265
  41.7 7.5 %galerkin.15 = f32[10,144,128]{2,1,0:T(8,128)} custom-call(s32[80]{0:T(128)} %get-tuple-element.43.fetch, s32[8]{0:T(128)} %get-tuple-element.27.count, f32[40,320,320]{2,1,0:T(8,128)} %a_ref.1, f32[40,320,320]{2,1,0:T(8,128)} %a_ref.1, bf16[320,256]{1,0:T(8,128)(2,1)} %get-tuple-element.28.refs_2_, bf16[320,256]{1,0:T(8,128)(2,1)} %get-tuple-element.29.refs_3_, ...), custom_call_target="tpu_custom_call" | custom-call | flops 1572864000 | bytes 4792320 | tf_op jit(solution)/shard_map/galerkin/pallas_call | solution.py:265
  49.3 9.7 %galerkin.16 = f32[10,144,128]{2,1,0:T(8,128)} custom-call(s32[80]{0:T(128)} %get-tuple-element.43.fetch, s32[8]{0:T(128)} %get-tuple-element.27.count, f32[40,320,320]{2,1,0:T(8,128)} %a_ref.1, f32[40,320,320]{2,1,0:T(8,128)} %a_ref.1, bf16[320,256]{1,0:T(8,128)(2,1)} %get-tuple-element.28.refs_2_, bf16[320,256]{1,0:T(8,128)(2,1)} %get-tuple-element.29.refs_3_, ...), custom_call_target="tpu_custom_call" | custom-call | flops 1572864000 | bytes 4792320 | tf_op jit(solution)/shard_map/galerkin/pallas_call | solution.py:265
  58.9 0.9 collective-permute-start.7
  59.8 6.6 %collective-permute-start.1 = (f32[8,144,128]{2,1,0:T(8,128)}, f32[8,144,128]{2,1,0:T(8,128)S(1)}, u32[]{:S(2)}, u32[]{:S(2)}) collective-permute-start(f32[8,144,128]{2,1,0:T(8,128)} %galerkin.10), channel_id=1, source_target_pairs={{0,16},{4,20},{8,24},{12,28},{16,0},{20,4},{24,8},{28,12},{1,17},{... | collective-permute-start | bytes 1769480 | tf_op jit(solution)/shard_map/ppermute | solution.py:392
  66.4 0.0 collective-permute-start
  66.4 1.8 collective-permute-start.6
  68.3 0.0 collective-permute-start.5
  68.3 29.2 %collective-permute-done.refs_0_ = f32[2,144,128]{2,1,0:T(8,128)S(1)} collective-permute-done((f32[2,144,128]{2,1,0:T(8,128)}, f32[2,144,128]{2,1,0:T(8,128)S(1)}, u32[]{:S(2)}, u32[]{:S(2)}) %collective-permute-start) | collective-permute-done | bytes 147488 | tf_op jit(solution)/shard_map/ppermute | solution.py:392
  97.5 0.0 copy-start.9
  97.5 0.7 copy-done.9
  98.1 2.8 %collective-permute-start.4 = (f32[10,144,128]{2,1,0:T(8,128)}, f32[10,144,128]{2,1,0:T(8,128)}, u32[]{:S(2)}, u32[]{:S(2)}) collective-permute-start(f32[10,144,128]{2,1,0:T(8,128)} %galerkin.13), channel_id=1, source_target_pairs={{0,28},{4,24},{8,20},{12,16},{16,12},{20,8},{24,4},{28,0},{1,29},{... | collective-permute-start | bytes 2211848 | tf_op jit(solution)/shard_map/ppermute | solution.py:392
  100.9 0.0 collective-permute-done.1.refs_1_
  100.9 0.0 copy-start.7
  100.9 0.9 copy-done.7
  101.8 2.2 collective-permute-start.3
  104.0 0.0 collective-permute-done.7.refs_7_
  104.0 0.0 copy-start.5
  104.0 0.9 copy-done.5
  104.9 0.0 collective-permute-start.2
  104.9 5.1 %all-to-all-start = ((f32[8,8,135]{2,1,0:T(8,128)}), f32[8,8,135]{2,1,0:T(8,128)S(1)}, u32[]{:S(2)}, u32[]{:S(2)}) async-start(f32[8,8,135]{2,1,0:T(8,128)} %get-tuple-element.45), calls=%async_computation | async-start | bytes 131072 | tf_op jit(solution)/shard_map/all_to_all | solution.py:398
  110.0 87.1 %all-to-all-done = f32[8,8,135]{2,1,0:T(8,128)S(1)} async-done(((f32[8,8,135]{2,1,0:T(8,128)}), f32[8,8,135]{2,1,0:T(8,128)S(1)}, u32[]{:S(2)}, u32[]{:S(2)}) %all-to-all-start) | async-done | bytes 34592 | tf_op jit(solution)/shard_map/all_to_all | solution.py:398
  197.1 0.7 broadcast_in_dim.8
  197.8 4.0 %all-to-all-start.1 = ((f32[4,64,135]{2,1,0:T(8,128)}), f32[4,64,135]{2,1,0:T(8,128)}, u32[]{:S(2)}, u32[]{:S(2)}) async-start(f32[4,64,135]{2,1,0:T(8,128)} %broadcast_in_dim.8), calls=%async_computation.1 | async-start | bytes 524288 | tf_op jit(solution)/shard_map/all_to_all | solution.py:369
  201.9 6.3 %galerkin.17.refs_8_ = f32[10,144,128]{2,1,0:T(8,128)} custom-call(s32[80]{0:T(128)} %get-tuple-element.43.fetch, s32[8]{0:T(128)} %get-tuple-element.27.count, f32[40,320,320]{2,1,0:T(8,128)} %a_ref.1, f32[40,320,320]{2,1,0:T(8,128)} %a_ref.1, bf16[320,256]{1,0:T(8,128)(2,1)} %get-tuple-element.28.refs_2_, bf16[320,256]{1,0:T(8,128)(2,1)} %get-tuple-element.29.refs_3_, ...), custom_call_target="tpu_custom_call" | custom-call | flops 1572864000 | bytes 4792320 | tf_op jit(solution)/shard_map/galerkin/pallas_call | solution.py:265
  208.1 0.0 all-to-all-done.1
  208.1 0.0 copy-start.2
  208.1 0.9 copy-done.2
  209.1 0.0 copy-start.4
  209.1 1.0 copy-done.4
  210.0 0.0 copy-start.13
  210.0 0.7 copy-done.13
  210.7 0.7 copy-done.14
  211.4 0.0 copy-start.12
  211.4 9.2 %products.1 = f32[256,256]{1,0:T(8,128)S(1)} custom-call(s32[2,40]{1,0:T(2,128)S(1)} %bitcast.17, s32[256]{0:T(256)S(1)} %copy-done.14, f32[40,320,320]{2,1,0:T(8,128)} %a_ref.1, f32[256,135]{1,0:T(8,128)} %bitcast.7.x_ref, f32[320,256]{1,0:T(8,128)S(1)} %copy-done.4, f32[135,320]{1,0:T(8,128)S(1)} %bitcast.13), custom_call_target="tpu_custom_call" | custom-call | flops 16384000 | bytes 16384000 | tf_op jit(solution)/shard_map/products/pallas_call | solution.py:200
  220.6 0.0 copy-start
  220.6 0.0 copy-start.3
  220.6 11.4 %all_to_all.20 = f32[4,64,256]{2,1,0:T(8,128)} all-to-all(f32[4,64,256]{2,1,0:T(8,128)S(1)} %bitcast.15), channel_id=1, replica_groups=mesh['wide'=8,'narrow'=4] {'narrow'}, dimensions={0} | all-to-all | bytes 524288 | tf_op jit(solution)/shard_map/all_to_all | solution.py:407
  232.1 1.6 reduce_sum.9
  233.6 3.9 %all-to-all-start.3 = ((f32[8,8,256]{2,1,0:T(8,128)}), f32[8,8,256]{2,1,0:T(8,128)S(1)}, u32[]{:S(2)}, u32[]{:S(2)}) async-start(f32[8,8,256]{2,1,0:T(8,128)} %bitcast.9), calls=%async_computation.3 | async-start | bytes 131072 | tf_op jit(solution)/shard_map/all_to_all | solution.py:409
  237.5 0.0 collective-permute-done.6.refs_6_
  237.5 0.0 collective-permute-done.5.refs_5_
  237.5 0.0 collective-permute-done.4.refs_4_
  237.5 0.0 collective-permute-done.3.refs_3_
  237.6 0.0 collective-permute-done.2.refs_2_
  237.6 0.0 copy-done.1
  237.6 0.0 copy-done.6
  237.6 0.0 copy-done.8
  237.6 0.0 copy-start.10
  237.6 0.9 copy-done.10
  238.5 7.1 %unpack.1 = f32[135,135,80]{2,1,0:T(8,128)} custom-call(s32[1]{0:T(128)} %bitcast.me, f32[2,144,128]{2,1,0:T(8,128)S(1)} %copy-done.10, f32[8,144,128]{2,1,0:T(8,128)S(1)} %copy-done.8, f32[10,144,128]{2,1,0:T(8,128)} %collective-permute-done.2.refs_2_, f32[10,144,128]{2,1,0:T(8,128)} %collective-permute-done.3.refs_3_, ...), custom_call_target="tpu_custom_call" | custom-call | bytes 11796480 | tf_op jit(solution)/shard_map/unpack/pallas_call | solution.py:342
  245.7 0.0 all-to-all-done.3.sums
  245.7 0.0 copy-done.11
  245.7 0.0 copy-done.12
  245.7 0.0 copy-done
  245.7 0.0 copy-done.3
  245.7 2.2 sweep_two.1
  (5 shorter events, 0.0 us)
Async XLA Ops:
  58.9 45.1 %collective-permute-start.7 = (f32[10,144,128]{2,1,0:T(8,128)}, f32[10,144,128]{2,1,0:T(8,128)S(1)}, u32[]{:S(2)}, u32[]{:S(2)}) collective-permute-start(f32[10,144,128]{2,1,0:T(8,128)} %galerkin.16), channel_id=1, source_target_pairs={{0,4},{4,0},{8,12},{12,8},{16,20},{20,16},{24,28},{28,24},{1,5},{5... | collective-permute-start | bytes 2211848 | tf_op jit(solution)/shard_map/ppermute | solution.py:392
  59.8 41.1 %collective-permute-start.1 = (f32[8,144,128]{2,1,0:T(8,128)}, f32[8,144,128]{2,1,0:T(8,128)S(1)}, u32[]{:S(2)}, u32[]{:S(2)}) collective-permute-start(f32[8,144,128]{2,1,0:T(8,128)} %galerkin.10), channel_id=1, source_target_pairs={{0,16},{4,20},{8,24},{12,28},{16,0},{20,4},{24,8},{28,12},{1,17},{... | collective-permute-start | bytes 1769480 | tf_op jit(solution)/shard_map/ppermute | solution.py:392
  66.4 31.1 %collective-permute-start = (f32[2,144,128]{2,1,0:T(8,128)}, f32[2,144,128]{2,1,0:T(8,128)S(1)}, u32[]{:S(2)}, u32[]{:S(2)}) collective-permute-start(f32[2,144,128]{2,1,0:T(8,128)} %galerkin.9), channel_id=1, source_target_pairs={{0,16},{4,20},{8,24},{12,28},{16,0},{20,4},{24,8},{28,12},{1,17},{... | collective-permute-start | bytes 442376 | tf_op jit(solution)/shard_map/ppermute | solution.py:392
  66.4 171.1 %collective-permute-start.6 = (f32[10,144,128]{2,1,0:T(8,128)}, f32[10,144,128]{2,1,0:T(8,128)}, u32[]{:S(2)}, u32[]{:S(2)}) collective-permute-start(f32[10,144,128]{2,1,0:T(8,128)} %galerkin.15), channel_id=1, source_target_pairs={{0,12},{4,8},{8,4},{12,0},{16,28},{20,24},{24,20},{28,16},{1,13},{... | collective-permute-start | bytes 2211848 | tf_op jit(solution)/shard_map/ppermute | solution.py:392
  68.3 169.3 %collective-permute-start.5 = (f32[10,144,128]{2,1,0:T(8,128)}, f32[10,144,128]{2,1,0:T(8,128)}, u32[]{:S(2)}, u32[]{:S(2)}) collective-permute-start(f32[10,144,128]{2,1,0:T(8,128)} %galerkin.14), channel_id=1, source_target_pairs={{0,8},{4,12},{8,0},{12,4},{16,24},{20,28},{24,16},{28,20},{1,9},{5... | collective-permute-start | bytes 2211848 | tf_op jit(solution)/shard_map/ppermute | solution.py:392
  97.5 0.7 copy-start.9
  98.1 139.4 %collective-permute-start.4 = (f32[10,144,128]{2,1,0:T(8,128)}, f32[10,144,128]{2,1,0:T(8,128)}, u32[]{:S(2)}, u32[]{:S(2)}) collective-permute-start(f32[10,144,128]{2,1,0:T(8,128)} %galerkin.13), channel_id=1, source_target_pairs={{0,28},{4,24},{8,20},{12,16},{16,12},{20,8},{24,4},{28,0},{1,29},{... | collective-permute-start | bytes 2211848 | tf_op jit(solution)/shard_map/ppermute | solution.py:392
  100.9 0.9 copy-start.7
  101.8 135.8 %collective-permute-start.3 = (f32[10,144,128]{2,1,0:T(8,128)}, f32[10,144,128]{2,1,0:T(8,128)}, u32[]{:S(2)}, u32[]{:S(2)}) collective-permute-start(f32[10,144,128]{2,1,0:T(8,128)} %galerkin.12), channel_id=1, source_target_pairs={{0,24},{4,28},{8,16},{12,20},{16,8},{20,12},{24,0},{28,4},{1,25},{... | collective-permute-start | bytes 2211848 | tf_op jit(solution)/shard_map/ppermute | solution.py:392
  104.0 0.9 copy-start.5
  104.9 132.7 %collective-permute-start.2 = (f32[10,144,128]{2,1,0:T(8,128)}, f32[10,144,128]{2,1,0:T(8,128)}, u32[]{:S(2)}, u32[]{:S(2)}) collective-permute-start(f32[10,144,128]{2,1,0:T(8,128)} %galerkin.11), channel_id=1, source_target_pairs={{0,20},{4,16},{8,28},{12,24},{16,4},{20,0},{24,12},{28,8},{1,21},{... | collective-permute-start | bytes 2211848 | tf_op jit(solution)/shard_map/ppermute | solution.py:392
  104.9 92.2 %all-to-all-start = ((f32[8,8,135]{2,1,0:T(8,128)}), f32[8,8,135]{2,1,0:T(8,128)S(1)}, u32[]{:S(2)}, u32[]{:S(2)}) async-start(f32[8,8,135]{2,1,0:T(8,128)} %get-tuple-element.45), calls=%async_computation | async-start | bytes 131072 | tf_op jit(solution)/shard_map/all_to_all | solution.py:398
  197.8 10.3 %all-to-all-start.1 = ((f32[4,64,135]{2,1,0:T(8,128)}), f32[4,64,135]{2,1,0:T(8,128)}, u32[]{:S(2)}, u32[]{:S(2)}) async-start(f32[4,64,135]{2,1,0:T(8,128)} %broadcast_in_dim.8), calls=%async_computation.1 | async-start | bytes 524288 | tf_op jit(solution)/shard_map/all_to_all | solution.py:369
  208.1 0.9 copy-start.2
  209.1 1.0 copy-start.4
  210.0 0.7 copy-start.13
  210.7 0.7 copy-start.14
  211.4 26.2 %copy-start.1 = (f32[10,144,128]{2,1,0:T(8,128)S(1)}, f32[10,144,128]{2,1,0:T(8,128)}, u32[]{:S(2)}) copy-start(f32[10,144,128]{2,1,0:T(8,128)} %galerkin.17.refs_8_) | copy-start | bytes 2211844
  211.4 26.2 %copy-start.6 = (f32[10,144,128]{2,1,0:T(8,128)S(1)}, f32[10,144,128]{2,1,0:T(8,128)}, u32[]{:S(2)}) copy-start(f32[10,144,128]{2,1,0:T(8,128)} %copy-done.5) | copy-start | bytes 2211844
  211.4 26.2 %copy-start.8 = (f32[8,144,128]{2,1,0:T(8,128)S(1)}, f32[8,144,128]{2,1,0:T(8,128)}, u32[]{:S(2)}) copy-start(f32[8,144,128]{2,1,0:T(8,128)} %copy-done.7) | copy-start | bytes 1769476
  211.4 34.3 %copy-start.11 = (f32[8,256]{1,0:T(8,128)S(1)}, f32[8,256]{1,0:T(8,128)}, u32[]{:S(2)}) copy-start(f32[8,256]{1,0:T(8,128)} %get-tuple-element.49.rhs) | copy-start | bytes 24580
  211.4 34.3 %copy-start.12 = (f32[8,135]{1,0:T(8,128)S(1)}, f32[8,135]{1,0:T(8,128)}, u32[]{:S(2)}) copy-start(f32[8,135]{1,0:T(8,128)} %get-tuple-element.35.sweep) | copy-start | bytes 12964
  220.6 25.1 %copy-start = (f32[8,135,135]{2,0,1:T(8,128)S(1)}, f32[8,135,135]{2,0,1:T(8,128)}, u32[]{:S(2)}) copy-start(f32[8,135,135]{2,0,1:T(8,128)} %param.11) | copy-start | bytes 1749604
  220.6 25.1 %copy-start.3 = (f32[320,135]{0,1:T(8,128)S(1)}, f32[320,135]{0,1:T(8,128)}, u32[]{:S(2)}) copy-start(f32[320,135]{0,1:T(8,128)} %param.9) | copy-start | bytes 518404
  233.6 12.0 %all-to-all-start.3 = ((f32[8,8,256]{2,1,0:T(8,128)}), f32[8,8,256]{2,1,0:T(8,128)S(1)}, u32[]{:S(2)}, u32[]{:S(2)}) async-start(f32[8,8,256]{2,1,0:T(8,128)} %bitcast.9), calls=%async_computation.3 | async-start | bytes 131072 | tf_op jit(solution)/shard_map/all_to_all | solution.py:409
  237.6 0.9 copy-start.10

commit v7 on v6

--- a/solution.py
+++ b/solution.py
@@ -156,17 +156,6 @@
     update = (1.0 - DAMPING) * rhs[:, :coarse] - jnp.sum(sums[...], axis=0)[:, :coarse]
     last = sweep[...] + DAMPING * apply_blocks(blocks, update)
     out[...] = jnp.dot(last, pt[...], precision=PRECISE, preferred_element_type=F32)
-
-
-def sweep_two_of(sums, rhs, sweep, pt, blocks):
-    return pl.pallas_call(
-        sweep_two_kernel,
-        out_shape=jax.ShapeDtypeStruct((rhs.shape[0], pt.shape[1]), F32),
-        in_specs=[VMEM] * 5,
-        out_specs=VMEM,
-        compiler_params=pltpu.CompilerParams(vmem_limit_bytes=8 << 20),
-        name="sweep_two",
-    )(sums, rhs, sweep, pt, blocks)
 
 
 def product_kernel(dev_rows, narrow, wide, elems, slots, a_ref, x_ref, p_ref, pt_ref, sums):
@@ -282,9 +271,9 @@
     )(fetch, count, *[face_blocks] * PAIR, *operands)
 
 
-def unpack_kernel(pieces, cap, coarse, me, *refs):
-    parts, out = refs[: len(pieces)], refs[len(pieces)]
-    buf, turned, sems = refs[len(pieces) + 1 :]
+def unpack_kernel(pieces, cap, coarse, me, sums, rhs, sweep, pt, blocks, *refs):
+    parts, (out, correction) = refs[: len(pieces)], refs[len(pieces) : len(pieces) + 2]
+    buf, turned, sems = refs[len(pieces) + 2 :]
     step = pl.program_id(0)
     total, rows, _ = buf.shape
     main = rows - 8
@@ -313,6 +302,7 @@
         for g in [tail, *range(tail)]:
             for copy in copies(g):
                 copy.start()
+        sweep_two_kernel(sums, rhs, sweep, pt, blocks, correction)
         for copy in copies(tail):
             copy.wait()
         for k in range(7):
@@ -334,18 +324,21 @@
         ]
 
 
-def unpack(parts, pieces, cap, coarse, wide, size=24):
+def unpack(parts, pieces, cap, coarse, wide, sweep_operands, size=24):
     rows = parts[0].shape[1]
     total = wide * cap
     groups = pl.cdiv(rows - 8, size)
     me = lax.axis_index("wide").astype(jnp.int32).reshape(1)
-    out = pl.pallas_call(
+    _, rhs, _, pt, _ = sweep_operands
+    out, correction = pl.pallas_call(
         functools.partial(unpack_kernel, pieces, cap, coarse),
-        out_shape=jax.ShapeDtypeStruct((coarse, coarse, total), F32),
+        out_shape=(
+            jax.ShapeDtypeStruct((coarse, coarse, total), F32),
+            jax.ShapeDtypeStruct((rhs.shape[0], pt.shape[1]), F32),
+        ),
         grid=(groups,),
-        in_specs=[pl.BlockSpec(memory_space=pltpu.SMEM)]
-        + [pl.BlockSpec(memory_space=pl.ANY)] * len(parts),
-        out_specs=pl.BlockSpec((size, coarse, total), lambda s: (s, 0, 0)),
+        in_specs=[SMEM] + [VMEM] * 5 + [pl.BlockSpec(memory_space=pl.ANY)] * len(parts),
+        out_specs=(pl.BlockSpec((size, coarse, total), lambda s: (s, 0, 0)), VMEM),
         scratch_shapes=[
             pltpu.VMEM((total, rows, LANES), F32),
             pltpu.VMEM((8 * LANES + 64, LANES), F32),
@@ -356,8 +349,8 @@
             flops=0, bytes_accessed=total * 8 * rows * LANES, transcendentals=0
         ),
         name="unpack",
-    )(me, *parts)
-    return jnp.transpose(out, (2, 0, 1))
+    )(me, *sweep_operands, *parts)
+    return correction, jnp.transpose(out, (2, 0, 1))
 
 
 def after(first, *values):
@@ -407,8 +400,9 @@
     sums = lax.all_to_all(sums, "narrow", split_axis=0, concat_axis=0, tiled=True)
     sums = jnp.sum(sums, axis=0).reshape(wide, dev_rows, -1)
     sums = lax.all_to_all(sums, "wide", split_axis=0, concat_axis=0, tiled=True)
-    owned = unpack(parts, pieces, cap, coarse, wide)
-    correction = sweep_two_of(after(owned, sums), rhs, sweep_one, prolong.T, inverse)
+    correction, owned = unpack(
+        parts, pieces, cap, coarse, wide, (sums, rhs, sweep_one, prolong.T, inverse)
+    )
     return (correction, owned)
 
 

time: 249 us -> 254 us (1.020)
  blocking collectives: 11.4 us -> 22.1 us
  starting transfers between devices: 27.3 us -> 23.4 us
    all_to_all x0 -> x1, blocking collectives: none -> 10.8 us  [local(): sums = lax.all_to_all(sums, 'wide', split_axis=0, concat_axis=0, tiled=True)]
    all_to_all x1 -> x0, starting transfers between devices: 3.88 us -> none  [local(): sums = lax.all_to_all(sums, 'wide', split_axis=0, concat_axis=0, tiled=True)]
  transfers between devices with their start and end apart: 11 -> 10, of which waited for: 2 -> 2; matrix products, arithmetic and copies ran while one was open for 1% -> 1% of each run, Pallas kernels for 9% -> 6%
where the time goes in v7:
time: 254 us; the launch traced here: 253 us
  waiting for transfers between devices  116 us (46%)
  Pallas kernels  82.5 us (32%)
  starting transfers between devices  23.4 us (9%)
  blocking collectives  22.1 us (9%)
  local copies, waits for them, and re-layouts  6.38 us (3%)
    all_to_all x1, waiting for transfers between devices, local(): lax.all_to_all(copies, 'wide', split_axis=0, concat_axis=0, tiled=True)  87.1 us
    pallas_call x9, Pallas kernels, galerkin(): pl.pallas_call(functools.partial(galerkin_kernel, at, first), out_shape=j...  58.8 us
    ppermute x8, waiting for transfers between devices, local(): parts.append(lax.ppermute(block, 'wide', pairs))  29.3 us
    ppermute x8, starting transfers between devices, local(): parts.append(lax.ppermute(block, 'wide', pairs))  14.3 us
    all_to_all x1, blocking collectives, local(): lax.all_to_all(sums, 'narrow', split_axis=0, concat_axis=0, tiled=True)  11.3 us
    all_to_all x1, blocking collectives, local(): sums = lax.all_to_all(sums, 'wide', split_axis=0, concat_axis=0, tiled=True)  10.8 us
    pallas_call x1, Pallas kernels, products(): pl.pallas_call(functools.partial(product_kernel, dev_rows, narrow, wide),...  9.47 us
    pallas_call x1, Pallas kernels, unpack(): pl.pallas_call(functools.partial(unpack_kernel, pieces, cap, coarse), out...  8.33 us
  transfers between devices with their start and end apart: 10, of which 2 were waited for; matrix products, arithmetic and copies ran while one was open for 1% of the time, Pallas kernels for 6%

profile of v7, /device:TPU:0, one launch (start us, length us, event | category | flops | bytes accessed | tf_op | source)
XLA Modules:
  0.0 253.1 jit_solution(16017335352986808295)
XLA Ops:
  0.6 2.3 place_faces.1
  3.0 4.1 %galerkin.9 = f32[2,144,128]{2,1,0:T(8,128)} custom-call(s32[80]{0:T(128)} %get-tuple-element.45.fetch, s32[8]{0:T(128)} %get-tuple-element.28.count, f32[40,320,320]{2,1,0:T(8,128)} %a_ref.1, f32[40,320,320]{2,1,0:T(8,128)} %a_ref.1, bf16[320,256]{1,0:T(8,128)(2,1)} %get-tuple-element.29.refs_2_, bf16[320,256]{1,0:T(8,128)(2,1)} %get-tuple-element.30.refs_3_, ...), custom_call_target="tpu_custom_call" | custom-call | flops 314572800 | bytes 958464 | tf_op jit(solution)/shard_map/galerkin/pallas_call | solution.py:254
  7.1 4.8 %galerkin.10 = f32[8,144,128]{2,1,0:T(8,128)} custom-call(s32[80]{0:T(128)} %get-tuple-element.45.fetch, s32[8]{0:T(128)} %get-tuple-element.28.count, f32[40,320,320]{2,1,0:T(8,128)} %a_ref.1, f32[40,320,320]{2,1,0:T(8,128)} %a_ref.1, bf16[320,256]{1,0:T(8,128)(2,1)} %get-tuple-element.29.refs_2_, bf16[320,256]{1,0:T(8,128)(2,1)} %get-tuple-element.30.refs_3_, ...), custom_call_target="tpu_custom_call" | custom-call | flops 1258291200 | bytes 3833856 | tf_op jit(solution)/shard_map/galerkin/pallas_call | solution.py:254
  11.9 3.6 %sweep_one.1 = (f32[8,256]{1,0:T(8,128)}, f32[8,135]{1,0:T(8,128)}, f32[8,8,135]{2,1,0:T(8,128)}) custom-call(f32[8,320]{1,0:T(8,128)} %residual, f32[320,256]{1,0:T(8,128)} %get-tuple-element.36.p32.p_ref, f32[135,8,135]{2,1,0:T(8,128)} %bitcast.10), custom_call_target="tpu_custom_call" | custom-call | tf_op jit(solution)/shard_map/sweep_one/pallas_call | solution.py:140
  15.5 6.2 %galerkin.11 = f32[10,144,128]{2,1,0:T(8,128)} custom-call(s32[80]{0:T(128)} %get-tuple-element.45.fetch, s32[8]{0:T(128)} %get-tuple-element.28.count, f32[40,320,320]{2,1,0:T(8,128)} %a_ref.1, f32[40,320,320]{2,1,0:T(8,128)} %a_ref.1, bf16[320,256]{1,0:T(8,128)(2,1)} %get-tuple-element.29.refs_2_, bf16[320,256]{1,0:T(8,128)(2,1)} %get-tuple-element.30.refs_3_, ...), custom_call_target="tpu_custom_call" | custom-call | flops 1572864000 | bytes 4792320 | tf_op jit(solution)/shard_map/galerkin/pallas_call | solution.py:254
  21.7 6.3 %galerkin.12 = f32[10,144,128]{2,1,0:T(8,128)} custom-call(s32[80]{0:T(128)} %get-tuple-element.45.fetch, s32[8]{0:T(128)} %get-tuple-element.28.count, f32[40,320,320]{2,1,0:T(8,128)} %a_ref.1, f32[40,320,320]{2,1,0:T(8,128)} %a_ref.1, bf16[320,256]{1,0:T(8,128)(2,1)} %get-tuple-element.29.refs_2_, bf16[320,256]{1,0:T(8,128)(2,1)} %get-tuple-element.30.refs_3_, ...), custom_call_target="tpu_custom_call" | custom-call | flops 1572864000 | bytes 4792320 | tf_op jit(solution)/shard_map/galerkin/pallas_call | solution.py:254
  28.0 8.4 %galerkin.13 = f32[10,144,128]{2,1,0:T(8,128)} custom-call(s32[80]{0:T(128)} %get-tuple-element.45.fetch, s32[8]{0:T(128)} %get-tuple-element.28.count, f32[40,320,320]{2,1,0:T(8,128)} %a_ref.1, f32[40,320,320]{2,1,0:T(8,128)} %a_ref.1, bf16[320,256]{1,0:T(8,128)(2,1)} %get-tuple-element.29.refs_2_, bf16[320,256]{1,0:T(8,128)(2,1)} %get-tuple-element.30.refs_3_, ...), custom_call_target="tpu_custom_call" | custom-call | flops 1572864000 | bytes 4792320 | tf_op jit(solution)/shard_map/galerkin/pallas_call | solution.py:254
  36.3 5.4 %galerkin.14 = f32[10,144,128]{2,1,0:T(8,128)} custom-call(s32[80]{0:T(128)} %get-tuple-element.45.fetch, s32[8]{0:T(128)} %get-tuple-element.28.count, f32[40,320,320]{2,1,0:T(8,128)} %a_ref.1, f32[40,320,320]{2,1,0:T(8,128)} %a_ref.1, bf16[320,256]{1,0:T(8,128)(2,1)} %get-tuple-element.29.refs_2_, bf16[320,256]{1,0:T(8,128)(2,1)} %get-tuple-element.30.refs_3_, ...), custom_call_target="tpu_custom_call" | custom-call | flops 1572864000 | bytes 4792320 | tf_op jit(solution)/shard_map/galerkin/pallas_call | solution.py:254
  41.8 7.6 %galerkin.15 = f32[10,144,128]{2,1,0:T(8,128)} custom-call(s32[80]{0:T(128)} %get-tuple-element.45.fetch, s32[8]{0:T(128)} %get-tuple-element.28.count, f32[40,320,320]{2,1,0:T(8,128)} %a_ref.1, f32[40,320,320]{2,1,0:T(8,128)} %a_ref.1, bf16[320,256]{1,0:T(8,128)(2,1)} %get-tuple-element.29.refs_2_, bf16[320,256]{1,0:T(8,128)(2,1)} %get-tuple-element.30.refs_3_, ...), custom_call_target="tpu_custom_call" | custom-call | flops 1572864000 | bytes 4792320 | tf_op jit(solution)/shard_map/galerkin/pallas_call | solution.py:254
  49.3 9.7 %galerkin.16 = f32[10,144,128]{2,1,0:T(8,128)} custom-call(s32[80]{0:T(128)} %get-tuple-element.45.fetch, s32[8]{0:T(128)} %get-tuple-element.28.count, f32[40,320,320]{2,1,0:T(8,128)} %a_ref.1, f32[40,320,320]{2,1,0:T(8,128)} %a_ref.1, bf16[320,256]{1,0:T(8,128)(2,1)} %get-tuple-element.29.refs_2_, bf16[320,256]{1,0:T(8,128)(2,1)} %get-tuple-element.30.refs_3_, ...), custom_call_target="tpu_custom_call" | custom-call | flops 1572864000 | bytes 4792320 | tf_op jit(solution)/shard_map/galerkin/pallas_call | solution.py:254
  59.0 0.8 collective-permute-start.7
  59.9 6.6 %collective-permute-start.1 = (f32[8,144,128]{2,1,0:T(8,128)}, f32[8,144,128]{2,1,0:T(8,128)S(1)}, u32[]{:S(2)}, u32[]{:S(2)}) collective-permute-start(f32[8,144,128]{2,1,0:T(8,128)} %galerkin.10), channel_id=1, source_target_pairs={{0,16},{4,20},{8,24},{12,28},{16,0},{20,4},{24,8},{28,12},{1,17},{... | collective-permute-start | bytes 1769480 | tf_op jit(solution)/shard_map/ppermute | solution.py:385
  66.5 0.0 collective-permute-start
  66.5 1.8 collective-permute-start.6
  68.4 0.0 collective-permute-start.5
  68.4 29.2 %collective-permute-done.refs_0_ = f32[2,144,128]{2,1,0:T(8,128)S(1)} collective-permute-done((f32[2,144,128]{2,1,0:T(8,128)}, f32[2,144,128]{2,1,0:T(8,128)S(1)}, u32[]{:S(2)}, u32[]{:S(2)}) %collective-permute-start) | collective-permute-done | bytes 147488 | tf_op jit(solution)/shard_map/ppermute | solution.py:385
  97.6 0.0 copy-start.9
  97.6 0.7 copy-done.9
  98.3 2.8 %collective-permute-start.4 = (f32[10,144,128]{2,1,0:T(8,128)}, f32[10,144,128]{2,1,0:T(8,128)}, u32[]{:S(2)}, u32[]{:S(2)}) collective-permute-start(f32[10,144,128]{2,1,0:T(8,128)} %galerkin.13), channel_id=1, source_target_pairs={{0,28},{4,24},{8,20},{12,16},{16,12},{20,8},{24,4},{28,0},{1,29},{... | collective-permute-start | bytes 2211848 | tf_op jit(solution)/shard_map/ppermute | solution.py:385
  101.0 0.0 collective-permute-done.1.refs_1_
  101.0 0.0 copy-start.7
  101.0 0.8 copy-done.7
  101.9 2.2 collective-permute-start.3
  104.1 0.0 collective-permute-done.7.refs_7_
  104.1 0.0 copy-start.5
  104.1 0.9 copy-done.5
  105.0 0.0 collective-permute-start.2
  105.0 5.1 %all-to-all-start = ((f32[8,8,135]{2,1,0:T(8,128)}), f32[8,8,135]{2,1,0:T(8,128)S(1)}, u32[]{:S(2)}, u32[]{:S(2)}) async-start(f32[8,8,135]{2,1,0:T(8,128)} %get-tuple-element.46), calls=%async_computation | async-start | bytes 131072 | tf_op jit(solution)/shard_map/all_to_all | solution.py:391
  110.1 87.1 %all-to-all-done = f32[8,8,135]{2,1,0:T(8,128)S(1)} async-done(((f32[8,8,135]{2,1,0:T(8,128)}), f32[8,8,135]{2,1,0:T(8,128)S(1)}, u32[]{:S(2)}, u32[]{:S(2)}) %all-to-all-start) | async-done | bytes 34592 | tf_op jit(solution)/shard_map/all_to_all | solution.py:391
  197.2 0.7 broadcast_in_dim.8
  197.9 4.0 %all-to-all-start.1 = ((f32[4,64,135]{2,1,0:T(8,128)}), f32[4,64,135]{2,1,0:T(8,128)}, u32[]{:S(2)}, u32[]{:S(2)}) async-start(f32[4,64,135]{2,1,0:T(8,128)} %broadcast_in_dim.8), calls=%async_computation.1 | async-start | bytes 524288 | tf_op jit(solution)/shard_map/all_to_all | solution.py:362
  202.0 6.3 %galerkin.17.refs_8_ = f32[10,144,128]{2,1,0:T(8,128)} custom-call(s32[80]{0:T(128)} %get-tuple-element.45.fetch, s32[8]{0:T(128)} %get-tuple-element.28.count, f32[40,320,320]{2,1,0:T(8,128)} %a_ref.1, f32[40,320,320]{2,1,0:T(8,128)} %a_ref.1, bf16[320,256]{1,0:T(8,128)(2,1)} %get-tuple-element.29.refs_2_, bf16[320,256]{1,0:T(8,128)(2,1)} %get-tuple-element.30.refs_3_, ...), custom_call_target="tpu_custom_call" | custom-call | flops 1572864000 | bytes 4792320 | tf_op jit(solution)/shard_map/galerkin/pallas_call | solution.py:254
  208.2 0.0 all-to-all-done.1
  208.2 0.0 copy-start.2
  208.3 0.9 copy-done.2
  209.2 0.0 copy-start.4
  209.2 1.0 copy-done.4
  210.2 0.0 copy-start.13
  210.2 0.7 copy-done.13
  210.8 0.0 copy-start.14
  210.8 0.7 copy-done.14
  211.5 0.0 copy-start
  211.5 0.0 copy-start.8
  211.5 0.0 copy-start.10
  211.5 0.0 copy-start.11
  211.6 0.0 copy-start.12
  211.6 9.5 %products.1 = f32[256,256]{1,0:T(8,128)S(1)} custom-call(s32[2,40]{1,0:T(2,128)S(1)} %bitcast.17, s32[256]{0:T(256)S(1)} %copy-done.14, f32[40,320,320]{2,1,0:T(8,128)} %a_ref.1, f32[256,135]{1,0:T(8,128)} %bitcast.6.x_ref, f32[320,256]{1,0:T(8,128)S(1)} %copy-done.4, f32[135,320]{1,0:T(8,128)S(1)} %bitcast.13), custom_call_target="tpu_custom_call" | custom-call | flops 16384000 | bytes 16384000 | tf_op jit(solution)/shard_map/products/pallas_call | solution.py:189
  221.0 11.3 %all_to_all.20 = f32[4,64,256]{2,1,0:T(8,128)} all-to-all(f32[4,64,256]{2,1,0:T(8,128)S(1)} %bitcast.15), channel_id=1, replica_groups=mesh['wide'=8,'narrow'=4] {'narrow'}, dimensions={0} | all-to-all | bytes 524288 | tf_op jit(solution)/shard_map/all_to_all | solution.py:400
  232.3 1.6 reduce_sum.9
  233.9 10.8 %all_to_all.21.sums = f32[8,8,256]{2,1,0:T(8,128)S(1)} all-to-all(f32[8,8,256]{2,1,0:T(8,128)} %bitcast.19), channel_id=1, replica_groups=mesh['wide'=8,'narrow'=4] {'wide'}, dimensions={0} | all-to-all | bytes 131072 | tf_op jit(solution)/shard_map/all_to_all | solution.py:402
  244.7 0.0 collective-permute-done.6.refs_6_
  244.7 0.0 collective-permute-done.5.refs_5_
  244.7 0.0 collective-permute-done.4.refs_4_
  244.7 0.0 collective-permute-done.3.refs_3_
  244.7 0.0 collective-permute-done.2.refs_2_
  244.7 0.0 copy-done
  244.7 0.0 copy-done.1
  244.7 0.0 copy-done.3
  244.8 0.0 copy-done.6
  244.8 0.0 copy-done.8
  244.8 0.0 copy-done.10
  244.8 0.0 copy-done.11
  244.8 0.0 copy-done.12
  244.8 8.3 %unpack.1 = (f32[135,135,80]{2,1,0:T(8,128)}, f32[8,320]{1,0:T(8,128)}) custom-call(s32[1]{0:T(128)} %bitcast.me, f32[8,8,256]{2,1,0:T(8,128)S(1)} %all_to_all.21.sums, f32[8,256]{1,0:T(8,128)S(1)} %copy-done.11, f32[8,135]{1,0:T(8,128)S(1)} %copy-done.12, f32[135,320]{1,0:T(8,128)S(1)} %bitcast.14, f32[135,8,135]{2,1,0:T(8,128)S(1)} %bitcast.11, ...), custom_call_target="tpu_custom_call" | custom-call | bytes 11796480 | tf_op jit(solution)/shard_map/unpack/pallas_call | solution.py:333
  (3 shorter events, 0.0 us)
Async XLA Ops:
  59.0 45.1 %collective-permute-start.7 = (f32[10,144,128]{2,1,0:T(8,128)}, f32[10,144,128]{2,1,0:T(8,128)S(1)}, u32[]{:S(2)}, u32[]{:S(2)}) collective-permute-start(f32[10,144,128]{2,1,0:T(8,128)} %galerkin.16), channel_id=1, source_target_pairs={{0,4},{4,0},{8,12},{12,8},{16,20},{20,16},{24,28},{28,24},{1,5},{5... | collective-permute-start | bytes 2211848 | tf_op jit(solution)/shard_map/ppermute | solution.py:385
  59.9 41.2 %collective-permute-start.1 = (f32[8,144,128]{2,1,0:T(8,128)}, f32[8,144,128]{2,1,0:T(8,128)S(1)}, u32[]{:S(2)}, u32[]{:S(2)}) collective-permute-start(f32[8,144,128]{2,1,0:T(8,128)} %galerkin.10), channel_id=1, source_target_pairs={{0,16},{4,20},{8,24},{12,28},{16,0},{20,4},{24,8},{28,12},{1,17},{... | collective-permute-start | bytes 1769480 | tf_op jit(solution)/shard_map/ppermute | solution.py:385
  66.5 31.1 %collective-permute-start = (f32[2,144,128]{2,1,0:T(8,128)}, f32[2,144,128]{2,1,0:T(8,128)S(1)}, u32[]{:S(2)}, u32[]{:S(2)}) collective-permute-start(f32[2,144,128]{2,1,0:T(8,128)} %galerkin.9), channel_id=1, source_target_pairs={{0,16},{4,20},{8,24},{12,28},{16,0},{20,4},{24,8},{28,12},{1,17},{... | collective-permute-start | bytes 442376 | tf_op jit(solution)/shard_map/ppermute | solution.py:385
  66.5 178.2 %collective-permute-start.6 = (f32[10,144,128]{2,1,0:T(8,128)}, f32[10,144,128]{2,1,0:T(8,128)}, u32[]{:S(2)}, u32[]{:S(2)}) collective-permute-start(f32[10,144,128]{2,1,0:T(8,128)} %galerkin.15), channel_id=1, source_target_pairs={{0,12},{4,8},{8,4},{12,0},{16,28},{20,24},{24,20},{28,16},{1,13},{... | collective-permute-start | bytes 2211848 | tf_op jit(solution)/shard_map/ppermute | solution.py:385
  68.4 176.3 %collective-permute-start.5 = (f32[10,144,128]{2,1,0:T(8,128)}, f32[10,144,128]{2,1,0:T(8,128)}, u32[]{:S(2)}, u32[]{:S(2)}) collective-permute-start(f32[10,144,128]{2,1,0:T(8,128)} %galerkin.14), channel_id=1, source_target_pairs={{0,8},{4,12},{8,0},{12,4},{16,24},{20,28},{24,16},{28,20},{1,9},{5... | collective-permute-start | bytes 2211848 | tf_op jit(solution)/shard_map/ppermute | solution.py:385
  97.6 0.7 copy-start.9
  98.3 146.4 %collective-permute-start.4 = (f32[10,144,128]{2,1,0:T(8,128)}, f32[10,144,128]{2,1,0:T(8,128)}, u32[]{:S(2)}, u32[]{:S(2)}) collective-permute-start(f32[10,144,128]{2,1,0:T(8,128)} %galerkin.13), channel_id=1, source_target_pairs={{0,28},{4,24},{8,20},{12,16},{16,12},{20,8},{24,4},{28,0},{1,29},{... | collective-permute-start | bytes 2211848 | tf_op jit(solution)/shard_map/ppermute | solution.py:385
  101.0 0.8 copy-start.7
  101.9 142.8 %collective-permute-start.3 = (f32[10,144,128]{2,1,0:T(8,128)}, f32[10,144,128]{2,1,0:T(8,128)}, u32[]{:S(2)}, u32[]{:S(2)}) collective-permute-start(f32[10,144,128]{2,1,0:T(8,128)} %galerkin.12), channel_id=1, source_target_pairs={{0,24},{4,28},{8,16},{12,20},{16,8},{20,12},{24,0},{28,4},{1,25},{... | collective-permute-start | bytes 2211848 | tf_op jit(solution)/shard_map/ppermute | solution.py:385
  104.1 0.9 copy-start.5
  105.0 139.7 %collective-permute-start.2 = (f32[10,144,128]{2,1,0:T(8,128)}, f32[10,144,128]{2,1,0:T(8,128)}, u32[]{:S(2)}, u32[]{:S(2)}) collective-permute-start(f32[10,144,128]{2,1,0:T(8,128)} %galerkin.11), channel_id=1, source_target_pairs={{0,20},{4,16},{8,28},{12,24},{16,4},{20,0},{24,12},{28,8},{1,21},{... | collective-permute-start | bytes 2211848 | tf_op jit(solution)/shard_map/ppermute | solution.py:385
  105.0 92.2 %all-to-all-start = ((f32[8,8,135]{2,1,0:T(8,128)}), f32[8,8,135]{2,1,0:T(8,128)S(1)}, u32[]{:S(2)}, u32[]{:S(2)}) async-start(f32[8,8,135]{2,1,0:T(8,128)} %get-tuple-element.46), calls=%async_computation | async-start | bytes 131072 | tf_op jit(solution)/shard_map/all_to_all | solution.py:391
  197.9 10.3 %all-to-all-start.1 = ((f32[4,64,135]{2,1,0:T(8,128)}), f32[4,64,135]{2,1,0:T(8,128)}, u32[]{:S(2)}, u32[]{:S(2)}) async-start(f32[4,64,135]{2,1,0:T(8,128)} %broadcast_in_dim.8), calls=%async_computation.1 | async-start | bytes 524288 | tf_op jit(solution)/shard_map/all_to_all | solution.py:362
  208.2 0.9 copy-start.2
  209.2 1.0 copy-start.4
  210.2 0.7 copy-start.13
  210.8 0.7 copy-start.14
  211.5 33.2 %copy-start = (f32[8,135,135]{2,0,1:T(8,128)S(1)}, f32[8,135,135]{2,0,1:T(8,128)}, u32[]{:S(2)}) copy-start(f32[8,135,135]{2,0,1:T(8,128)} %param.11) | copy-start | bytes 1749604
  211.5 33.2 %copy-start.1 = (f32[10,144,128]{2,1,0:T(8,128)S(1)}, f32[10,144,128]{2,1,0:T(8,128)}, u32[]{:S(2)}) copy-start(f32[10,144,128]{2,1,0:T(8,128)} %galerkin.17.refs_8_) | copy-start | bytes 2211844
  211.5 33.2 %copy-start.3 = (f32[320,135]{0,1:T(8,128)S(1)}, f32[320,135]{0,1:T(8,128)}, u32[]{:S(2)}) copy-start(f32[320,135]{0,1:T(8,128)} %param.9) | copy-start | bytes 518404
  211.5 33.2 %copy-start.6 = (f32[10,144,128]{2,1,0:T(8,128)S(1)}, f32[10,144,128]{2,1,0:T(8,128)}, u32[]{:S(2)}) copy-start(f32[10,144,128]{2,1,0:T(8,128)} %copy-done.5) | copy-start | bytes 2211844
  211.5 33.2 %copy-start.8 = (f32[8,144,128]{2,1,0:T(8,128)S(1)}, f32[8,144,128]{2,1,0:T(8,128)}, u32[]{:S(2)}) copy-start(f32[8,144,128]{2,1,0:T(8,128)} %copy-done.7) | copy-start | bytes 1769476
  211.5 33.2 %copy-start.10 = (f32[2,144,128]{2,1,0:T(8,128)S(1)}, f32[2,144,128]{2,1,0:T(8,128)}, u32[]{:S(2)}) copy-start(f32[2,144,128]{2,1,0:T(8,128)} %copy-done.9) | copy-start | bytes 442372
  211.5 33.2 %copy-start.11 = (f32[8,256]{1,0:T(8,128)S(1)}, f32[8,256]{1,0:T(8,128)}, u32[]{:S(2)}) copy-start(f32[8,256]{1,0:T(8,128)} %get-tuple-element.49.rhs) | copy-start | bytes 24580
  211.6 33.2 %copy-start.12 = (f32[8,135]{1,0:T(8,128)S(1)}, f32[8,135]{1,0:T(8,128)}, u32[]{:S(2)}) copy-start(f32[8,135]{1,0:T(8,128)} %get-tuple-element.37.sweep) | copy-start | bytes 12964
